TPU v7x, 32 devices: a whole 2x2x4 slice. The times are simulated.
32 devices in a mesh: kcol: 8 (over y, x, core), ion: 4 (over z).
Axes of the slice: x: 2, y: 2, z: 4, core: 2. Of those that a mesh axis runs over, the one named last changes fastest.
Arguments:
- ions: float32 [4, 81920], P(None, ('kcol', 'ion')), may hold values from -1.5 to 1.5, as said below
- col_ids: int32 [1024], P('kcol'), may hold values from 0 to 4095, as said below
Outputs:
- ion_forces: float32 [4, 81920], P(None, ('kcol', 'ion'))
- energy: float32 [], replicated
Inputs may be any that keep to these rules, and one draw needn't show every extreme that they name: `col_ids`: distinct column numbers. `ions`: rows 0 to 2 lie in [0, 1); row 3 has magnitudes 0.5 to 1.5.
All inputs are finite; a program needn't handle non-finite values.
Results may differ from a plain program's by a relative error of at most 0.0003.
Values sent between devices are 32-bit elements; how exact they have to be, the bound alone decides.
No kernel may reach another device: no remote copies, remote signals or barrier semaphores. Data moves between devices by JAX's collectives and lax.ppermute only.
A program may use at most 64 MiB of HBM per device.

v0:
```python
import math

import jax
import jax.numpy as jnp
from jax import lax
from jax.sharding import PartitionSpec as P

KX = 32


def wave_numbers(col_ids):
    wave_x = jnp.arange(KX, dtype=jnp.int32)
    wave_y = col_ids // 64 - 32
    wave_z = col_ids % 64 - 32
    return (wave_x, wave_y, wave_z)


def kspace_weight(wave_x, wave_y, wave_z):
    radial = wave_y * wave_y + wave_z * wave_z
    along = wave_x * wave_x
    squared = along[:, None] + radial[None, :]
    inside = (squared <= 1024) & (squared > 0)
    squared_f = squared.astype(jnp.float32)
    halving = jnp.where(wave_x == 0, jnp.float32(0.5), jnp.float32(1.0))[:, None]
    return jnp.where(
        inside,
        halving * jnp.exp(-squared_f / 1600.0) / jnp.maximum(squared_f, 1.0),
        jnp.float32(0.0),
    )


def phase_tables(block, wave_x, wave_y, wave_z):
    two_pi = 2.0 * math.pi
    angle_x = two_pi * wave_x.astype(jnp.float32)[:, None] * block[0][None, :]
    angle_yz = two_pi * (
        wave_y.astype(jnp.float32)[:, None] * block[1][None, :]
        + wave_z.astype(jnp.float32)[:, None] * block[2][None, :]
    )
    return (jnp.cos(angle_x), jnp.sin(angle_x), jnp.cos(angle_yz), jnp.sin(angle_yz))


def factor_piece(block, waves):
    cos_x, sin_x, cos_yz, sin_yz = phase_tables(block, *waves)
    charge = block[3][None, :]
    left = jnp.concatenate([charge * cos_x, charge * sin_x], 0)
    right = jnp.concatenate([cos_yz, sin_yz], 0)
    product = lax.dot_general(
        left,
        right,
        (((1,), (1,)), ((), ())),
        precision=lax.Precision.HIGHEST,
        preferred_element_type=jnp.float32,
    )
    nwave = cos_x.shape[0]
    ncol = cos_yz.shape[0]
    real_part = product[:nwave, :ncol] - product[nwave:, ncol:]
    imag_part = product[:nwave, ncol:] + product[nwave:, :ncol]
    return jnp.stack([real_part, imag_part])


def combine_matrix(weight, factor, wave_x):
    g_real = weight * factor[0]
    g_imag = -weight * factor[1]
    scaled = wave_x.astype(jnp.float32)[:, None]
    x_real = scaled * g_real
    x_imag = scaled * g_imag
    return jnp.concatenate(
        [
            jnp.concatenate([g_real.T, -g_imag.T], 1),
            jnp.concatenate([g_imag.T, g_real.T], 1),
            jnp.concatenate([x_real.T, -x_imag.T], 1),
            jnp.concatenate([x_imag.T, x_real.T], 1),
        ],
        0,
    )


def force_piece(block, combined, waves, force_scale, potential_scale):
    cos_x, sin_x, cos_yz, sin_yz = phase_tables(block, *waves)
    basis = jnp.concatenate([cos_x, sin_x], 0)
    spread = jnp.dot(
        combined, basis, precision=lax.Precision.HIGHEST, preferred_element_type=jnp.float32
    )
    ncol = cos_yz.shape[0]
    h_real0 = spread[:ncol]
    h_imag0 = spread[ncol : 2 * ncol]
    h_real1 = spread[2 * ncol : 3 * ncol]
    h_imag1 = spread[3 * ncol :]
    imag_zero = h_real0 * sin_yz + h_imag0 * cos_yz
    real_zero = h_real0 * cos_yz - h_imag0 * sin_yz
    imag_one = h_real1 * sin_yz + h_imag1 * cos_yz
    charge = block[3]
    wave_y = waves[1].astype(jnp.float32)[:, None]
    wave_z = waves[2].astype(jnp.float32)[:, None]
    force_x = force_scale * charge * jnp.sum(imag_one, 0)
    force_y = force_scale * charge * jnp.sum(wave_y * imag_zero, 0)
    force_z = force_scale * charge * jnp.sum(wave_z * imag_zero, 0)
    potential = potential_scale * jnp.sum(real_zero, 0)
    return jnp.stack([force_x, force_y, force_z, potential])


def per_device(ions, col_ids):
    groups = lax.axis_size("kcol")
    piece = ions.shape[1]
    total = piece * groups * lax.axis_size("ion")
    waves = wave_numbers(col_ids)
    weight = kspace_weight(*waves)
    ncol = col_ids.shape[0]
    gathered = lax.all_gather(ions, "kcol", axis=1, tiled=True)

    def add_factor(piece_index, partial_value):
        block = lax.dynamic_slice_in_dim(gathered, piece_index * piece, piece, 1)
        return partial_value + factor_piece(block, waves)

    partial_value = lax.fori_loop(0, groups, add_factor, jnp.zeros((2, KX, ncol), jnp.float32))
    factor = lax.psum(partial_value, "ion")
    energy_group = jnp.float32(0.01 / total) * jnp.sum(
        weight * (factor[0] * factor[0] + factor[1] * factor[1])
    )
    combined = combine_matrix(weight, factor, waves[0])
    force_scale = jnp.float32(0.04 * math.pi / math.sqrt(total))
    potential_scale = jnp.float32(0.4 / math.sqrt(total))

    def place_forces(piece_index, result):
        block = lax.dynamic_slice_in_dim(gathered, piece_index * piece, piece, 1)
        return lax.dynamic_update_slice_in_dim(
            result,
            force_piece(block, combined, waves, force_scale, potential_scale),
            piece_index * piece,
            1,
        )

    row_forces = lax.fori_loop(0, groups, place_forces, jnp.zeros((4, groups * piece), jnp.float32))
    summed, energy = lax.psum((row_forces, energy_group), "kcol")
    owned = lax.dynamic_slice_in_dim(summed, lax.axis_index("kcol") * piece, piece, 1)
    return (owned, energy)


def solution(mesh):
    return jax.shard_map(
        per_device,
        mesh=mesh,
        in_specs=(P(None, ("kcol", "ion")), P("kcol")),
        out_specs=(P(None, ("kcol", "ion")), P()),
        check_vma=False,
    )
```

profile of v0, /device:TPU:0, one launch (start us, length us, event | category | flops | bytes accessed | tf_op | source)
XLA Modules:
  0.0 265.6 jit_solution(9668760638139759695)
XLA Ops:
  7.9 11.2 %all_gather.3 = f32[4,20480]{1,0:T(4,128)S(1)} all-gather(f32[4,2560]{1,0:T(4,128)} %param.6), channel_id=1, replica_groups=mesh['kcol'=8,'ion'=4] {'kcol'}, dimensions={1}, use_global_device_ids=true | all-gather | bytes 368640 | tf_op jit(solution)/shard_map/all_gather | solution.py:109
  19.1 70.5 %while.33 = (s32[]{:T(128)}, f32[2,32,128]{2,1,0:T(8,128)S(1)}, f32[4,20480]{1,0:T(4,128)S(1)}, f32[128,1]{0,1:T(1,128)S(1)}, f32[128,1]{0,1:T(1,128)S(1)}, /*in...) while((s32[]{:T(128)}, f32[2,32,128]{2,1,0:T(8,128)S(1)}, ...), condition=%wide.region_1.2_spmd.clone, body=%wide.region_0.1_spmd.clone.sunk | while | flops 505724992 | bytes 6940129 | solution.py:115
  19.2 4.8 %fusion.62 = (f32[128,2560]{1,0:T(8,128)S(1)}, f32[128,2560]{1,0:T(8,128)S(1)}) fusion(f32[2560]{0:T(1024)S(1)} %get-tuple-element.535, f32[128]{0:T(128)S(1)} %bitcast.69, f32[2560]{0:T(1024)S(1)} %get-tuple-element.536, f32[128]{0:T(128)S(1)} %bitcast.71), kind=kLoop, calls=%fused_computation.37.clone.1 | loop fusion | flops 1310720 | bytes 2642944 | tf_op jit(solution)/shard_map/while/body/eval_jaxpr/cos | solution.py:39
  24.1 1.2 fusion.64
  25.3 2.5 fusion.65
  28.1 4.8 %fusion.62 = (f32[128,2560]{1,0:T(8,128)S(1)}, f32[128,2560]{1,0:T(8,128)S(1)}) fusion(f32[2560]{0:T(1024)S(1)} %get-tuple-element.535, f32[128]{0:T(128)S(1)} %bitcast.69, f32[2560]{0:T(1024)S(1)} %get-tuple-element.536, f32[128]{0:T(128)S(1)} %bitcast.71), kind=kLoop, calls=%fused_computation.37.clone.1 | loop fusion | flops 1310720 | bytes 2642944 | tf_op jit(solution)/shard_map/while/body/eval_jaxpr/cos | solution.py:39
  32.9 1.2 fusion.64
  34.1 2.5 fusion.65
  36.9 4.8 %fusion.62 = (f32[128,2560]{1,0:T(8,128)S(1)}, f32[128,2560]{1,0:T(8,128)S(1)}) fusion(f32[2560]{0:T(1024)S(1)} %get-tuple-element.535, f32[128]{0:T(128)S(1)} %bitcast.69, f32[2560]{0:T(1024)S(1)} %get-tuple-element.536, f32[128]{0:T(128)S(1)} %bitcast.71), kind=kLoop, calls=%fused_computation.37.clone.1 | loop fusion | flops 1310720 | bytes 2642944 | tf_op jit(solution)/shard_map/while/body/eval_jaxpr/cos | solution.py:39
  41.7 1.2 fusion.64
  43.0 2.5 fusion.65
  45.7 4.8 %fusion.62 = (f32[128,2560]{1,0:T(8,128)S(1)}, f32[128,2560]{1,0:T(8,128)S(1)}) fusion(f32[2560]{0:T(1024)S(1)} %get-tuple-element.535, f32[128]{0:T(128)S(1)} %bitcast.69, f32[2560]{0:T(1024)S(1)} %get-tuple-element.536, f32[128]{0:T(128)S(1)} %bitcast.71), kind=kLoop, calls=%fused_computation.37.clone.1 | loop fusion | flops 1310720 | bytes 2642944 | tf_op jit(solution)/shard_map/while/body/eval_jaxpr/cos | solution.py:39
  50.5 1.2 fusion.64
  51.8 2.5 fusion.65
  54.5 4.8 %fusion.62 = (f32[128,2560]{1,0:T(8,128)S(1)}, f32[128,2560]{1,0:T(8,128)S(1)}) fusion(f32[2560]{0:T(1024)S(1)} %get-tuple-element.535, f32[128]{0:T(128)S(1)} %bitcast.69, f32[2560]{0:T(1024)S(1)} %get-tuple-element.536, f32[128]{0:T(128)S(1)} %bitcast.71), kind=kLoop, calls=%fused_computation.37.clone.1 | loop fusion | flops 1310720 | bytes 2642944 | tf_op jit(solution)/shard_map/while/body/eval_jaxpr/cos | solution.py:39
  59.4 1.2 fusion.64
  60.6 2.5 fusion.65
  63.3 4.8 %fusion.62 = (f32[128,2560]{1,0:T(8,128)S(1)}, f32[128,2560]{1,0:T(8,128)S(1)}) fusion(f32[2560]{0:T(1024)S(1)} %get-tuple-element.535, f32[128]{0:T(128)S(1)} %bitcast.69, f32[2560]{0:T(1024)S(1)} %get-tuple-element.536, f32[128]{0:T(128)S(1)} %bitcast.71), kind=kLoop, calls=%fused_computation.37.clone.1 | loop fusion | flops 1310720 | bytes 2642944 | tf_op jit(solution)/shard_map/while/body/eval_jaxpr/cos | solution.py:39
  68.2 1.2 fusion.64
  69.4 2.5 fusion.65
  72.2 4.8 %fusion.62 = (f32[128,2560]{1,0:T(8,128)S(1)}, f32[128,2560]{1,0:T(8,128)S(1)}) fusion(f32[2560]{0:T(1024)S(1)} %get-tuple-element.535, f32[128]{0:T(128)S(1)} %bitcast.69, f32[2560]{0:T(1024)S(1)} %get-tuple-element.536, f32[128]{0:T(128)S(1)} %bitcast.71), kind=kLoop, calls=%fused_computation.37.clone.1 | loop fusion | flops 1310720 | bytes 2642944 | tf_op jit(solution)/shard_map/while/body/eval_jaxpr/cos | solution.py:39
  77.0 1.2 fusion.64
  78.2 2.5 fusion.65
  81.0 4.8 %fusion.62 = (f32[128,2560]{1,0:T(8,128)S(1)}, f32[128,2560]{1,0:T(8,128)S(1)}) fusion(f32[2560]{0:T(1024)S(1)} %get-tuple-element.535, f32[128]{0:T(128)S(1)} %bitcast.69, f32[2560]{0:T(1024)S(1)} %get-tuple-element.536, f32[128]{0:T(128)S(1)} %bitcast.71), kind=kLoop, calls=%fused_computation.37.clone.1 | loop fusion | flops 1310720 | bytes 2642944 | tf_op jit(solution)/shard_map/while/body/eval_jaxpr/cos | solution.py:39
  85.8 1.2 fusion.64
  87.1 2.5 fusion.65
  89.6 19.3 %psum.21 = f32[2,32,128]{2,1,0:T(8,128)S(1)} all-reduce(f32[2,32,128]{2,1,0:T(8,128)S(1)} %get-tuple-element.329), channel_id=1, replica_groups=mesh['kcol'=8,'ion'=4] {'ion'}, use_global_device_ids=true, to_apply=%region_2.3 | all-reduce | flops 8192 | bytes 65536 | tf_op jit(solution)/shard_map/psum | solution.py:116
  109.9 95.1 %while.32 = (s32[]{:T(128)}, f32[4,20480]{1,0:T(4,128)S(1)}, f32[4,20480]{1,0:T(4,128)S(1)}, f32[512,64]{1,0:T(8,128)S(1)}, f32[128,1]{0,1:T(1,128)S(1)}, /*inde...) while((s32[]{:T(128)}, f32[4,20480]{1,0:T(4,128)S(1)}, ...), condition=%wide.region_8.9_spmd.clone, body=%wide.region_3.8_spmd.clone.sunk | while | flops 1013137984 | bytes 12256743 | solution.py:133
  110.0 1.2 multiply_cosine_fusion.3
  111.2 4.3 %convolution_bitcast_fusion.2 = f32[512,2560]{1,0:T(8,128)S(1)} fusion(f32[512,64]{1,0:T(8,128)S(1)} %get-tuple-element.610, f32[32,2560]{1,0:T(8,128)S(1)} %get-tuple-element.519, f32[32,2560]{1,0:T(8,128)S(1)} %get-tuple-element.520), kind=kOutput, calls=%fused_computation.2.clone.1 | convolution fusion | flops 1006796800 | bytes 6029312 | tf_op jit(solution)/shard_map/while/body/eval_jaxpr/dot_general | solution.py:81
  115.6 6.0 %multiply_reduce_fusion.4 = (f32[2560]{0:T(1024)S(1)}, f32[2560]{0:T(1024)S(1)}, f32[2560]{0:T(1024)S(1)}, f32[2560]{0:T(1024)S(1)}) fusion(f32[128]{0:T(128)S(1)} %bitcast.72, f32[128]{0:T(128)S(1)} %bitcast.70, f32[512,2560]{1,0:T(8,128)S(1)} %convolution_bitcast_fusion.2, f32[2560]{0:T(1024)S(1)} %get-tuple-element.521, f32[2560]{0:T(1024)S(1)} %get-tuple-element.522), kind=kLoop, calls=%fused_computation.9.clone.1 | loop fusion | flops 6215680 | bytes 5305344 | tf_op jit(solution)/shard_map/while/body/eval_jaxpr/reduce_sum | solution.py:96
  123.1 4.3 %convolution_bitcast_fusion.2 = f32[512,2560]{1,0:T(8,128)S(1)} fusion(f32[512,64]{1,0:T(8,128)S(1)} %get-tuple-element.610, f32[32,2560]{1,0:T(8,128)S(1)} %get-tuple-element.519, f32[32,2560]{1,0:T(8,128)S(1)} %get-tuple-element.520), kind=kOutput, calls=%fused_computation.2.clone.1 | convolution fusion | flops 1006796800 | bytes 6029312 | tf_op jit(solution)/shard_map/while/body/eval_jaxpr/dot_general | solution.py:81
  127.5 6.0 %multiply_reduce_fusion.4 = (f32[2560]{0:T(1024)S(1)}, f32[2560]{0:T(1024)S(1)}, f32[2560]{0:T(1024)S(1)}, f32[2560]{0:T(1024)S(1)}) fusion(f32[128]{0:T(128)S(1)} %bitcast.72, f32[128]{0:T(128)S(1)} %bitcast.70, f32[512,2560]{1,0:T(8,128)S(1)} %convolution_bitcast_fusion.2, f32[2560]{0:T(1024)S(1)} %get-tuple-element.521, f32[2560]{0:T(1024)S(1)} %get-tuple-element.522), kind=kLoop, calls=%fused_computation.9.clone.1 | loop fusion | flops 6215680 | bytes 5305344 | tf_op jit(solution)/shard_map/while/body/eval_jaxpr/reduce_sum | solution.py:96
  135.0 4.3 %convolution_bitcast_fusion.2 = f32[512,2560]{1,0:T(8,128)S(1)} fusion(f32[512,64]{1,0:T(8,128)S(1)} %get-tuple-element.610, f32[32,2560]{1,0:T(8,128)S(1)} %get-tuple-element.519, f32[32,2560]{1,0:T(8,128)S(1)} %get-tuple-element.520), kind=kOutput, calls=%fused_computation.2.clone.1 | convolution fusion | flops 1006796800 | bytes 6029312 | tf_op jit(solution)/shard_map/while/body/eval_jaxpr/dot_general | solution.py:81
  139.4 6.0 %multiply_reduce_fusion.4 = (f32[2560]{0:T(1024)S(1)}, f32[2560]{0:T(1024)S(1)}, f32[2560]{0:T(1024)S(1)}, f32[2560]{0:T(1024)S(1)}) fusion(f32[128]{0:T(128)S(1)} %bitcast.72, f32[128]{0:T(128)S(1)} %bitcast.70, f32[512,2560]{1,0:T(8,128)S(1)} %convolution_bitcast_fusion.2, f32[2560]{0:T(1024)S(1)} %get-tuple-element.521, f32[2560]{0:T(1024)S(1)} %get-tuple-element.522), kind=kLoop, calls=%fused_computation.9.clone.1 | loop fusion | flops 6215680 | bytes 5305344 | tf_op jit(solution)/shard_map/while/body/eval_jaxpr/reduce_sum | solution.py:96
  146.9 4.3 %convolution_bitcast_fusion.2 = f32[512,2560]{1,0:T(8,128)S(1)} fusion(f32[512,64]{1,0:T(8,128)S(1)} %get-tuple-element.610, f32[32,2560]{1,0:T(8,128)S(1)} %get-tuple-element.519, f32[32,2560]{1,0:T(8,128)S(1)} %get-tuple-element.520), kind=kOutput, calls=%fused_computation.2.clone.1 | convolution fusion | flops 1006796800 | bytes 6029312 | tf_op jit(solution)/shard_map/while/body/eval_jaxpr/dot_general | solution.py:81
  151.2 6.0 %multiply_reduce_fusion.4 = (f32[2560]{0:T(1024)S(1)}, f32[2560]{0:T(1024)S(1)}, f32[2560]{0:T(1024)S(1)}, f32[2560]{0:T(1024)S(1)}) fusion(f32[128]{0:T(128)S(1)} %bitcast.72, f32[128]{0:T(128)S(1)} %bitcast.70, f32[512,2560]{1,0:T(8,128)S(1)} %convolution_bitcast_fusion.2, f32[2560]{0:T(1024)S(1)} %get-tuple-element.521, f32[2560]{0:T(1024)S(1)} %get-tuple-element.522), kind=kLoop, calls=%fused_computation.9.clone.1 | loop fusion | flops 6215680 | bytes 5305344 | tf_op jit(solution)/shard_map/while/body/eval_jaxpr/reduce_sum | solution.py:96
  158.8 4.3 %convolution_bitcast_fusion.2 = f32[512,2560]{1,0:T(8,128)S(1)} fusion(f32[512,64]{1,0:T(8,128)S(1)} %get-tuple-element.610, f32[32,2560]{1,0:T(8,128)S(1)} %get-tuple-element.519, f32[32,2560]{1,0:T(8,128)S(1)} %get-tuple-element.520), kind=kOutput, calls=%fused_computation.2.clone.1 | convolution fusion | flops 1006796800 | bytes 6029312 | tf_op jit(solution)/shard_map/while/body/eval_jaxpr/dot_general | solution.py:81
  163.1 6.0 %multiply_reduce_fusion.4 = (f32[2560]{0:T(1024)S(1)}, f32[2560]{0:T(1024)S(1)}, f32[2560]{0:T(1024)S(1)}, f32[2560]{0:T(1024)S(1)}) fusion(f32[128]{0:T(128)S(1)} %bitcast.72, f32[128]{0:T(128)S(1)} %bitcast.70, f32[512,2560]{1,0:T(8,128)S(1)} %convolution_bitcast_fusion.2, f32[2560]{0:T(1024)S(1)} %get-tuple-element.521, f32[2560]{0:T(1024)S(1)} %get-tuple-element.522), kind=kLoop, calls=%fused_computation.9.clone.1 | loop fusion | flops 6215680 | bytes 5305344 | tf_op jit(solution)/shard_map/while/body/eval_jaxpr/reduce_sum | solution.py:96
  170.7 4.3 %convolution_bitcast_fusion.2 = f32[512,2560]{1,0:T(8,128)S(1)} fusion(f32[512,64]{1,0:T(8,128)S(1)} %get-tuple-element.610, f32[32,2560]{1,0:T(8,128)S(1)} %get-tuple-element.519, f32[32,2560]{1,0:T(8,128)S(1)} %get-tuple-element.520), kind=kOutput, calls=%fused_computation.2.clone.1 | convolution fusion | flops 1006796800 | bytes 6029312 | tf_op jit(solution)/shard_map/while/body/eval_jaxpr/dot_general | solution.py:81
  175.0 6.0 %multiply_reduce_fusion.4 = (f32[2560]{0:T(1024)S(1)}, f32[2560]{0:T(1024)S(1)}, f32[2560]{0:T(1024)S(1)}, f32[2560]{0:T(1024)S(1)}) fusion(f32[128]{0:T(128)S(1)} %bitcast.72, f32[128]{0:T(128)S(1)} %bitcast.70, f32[512,2560]{1,0:T(8,128)S(1)} %convolution_bitcast_fusion.2, f32[2560]{0:T(1024)S(1)} %get-tuple-element.521, f32[2560]{0:T(1024)S(1)} %get-tuple-element.522), kind=kLoop, calls=%fused_computation.9.clone.1 | loop fusion | flops 6215680 | bytes 5305344 | tf_op jit(solution)/shard_map/while/body/eval_jaxpr/reduce_sum | solution.py:96
  182.6 4.3 %convolution_bitcast_fusion.2 = f32[512,2560]{1,0:T(8,128)S(1)} fusion(f32[512,64]{1,0:T(8,128)S(1)} %get-tuple-element.610, f32[32,2560]{1,0:T(8,128)S(1)} %get-tuple-element.519, f32[32,2560]{1,0:T(8,128)S(1)} %get-tuple-element.520), kind=kOutput, calls=%fused_computation.2.clone.1 | convolution fusion | flops 1006796800 | bytes 6029312 | tf_op jit(solution)/shard_map/while/body/eval_jaxpr/dot_general | solution.py:81
  186.9 6.0 %multiply_reduce_fusion.4 = (f32[2560]{0:T(1024)S(1)}, f32[2560]{0:T(1024)S(1)}, f32[2560]{0:T(1024)S(1)}, f32[2560]{0:T(1024)S(1)}) fusion(f32[128]{0:T(128)S(1)} %bitcast.72, f32[128]{0:T(128)S(1)} %bitcast.70, f32[512,2560]{1,0:T(8,128)S(1)} %convolution_bitcast_fusion.2, f32[2560]{0:T(1024)S(1)} %get-tuple-element.521, f32[2560]{0:T(1024)S(1)} %get-tuple-element.522), kind=kLoop, calls=%fused_computation.9.clone.1 | loop fusion | flops 6215680 | bytes 5305344 | tf_op jit(solution)/shard_map/while/body/eval_jaxpr/reduce_sum | solution.py:96
  194.5 4.3 %convolution_bitcast_fusion.2 = f32[512,2560]{1,0:T(8,128)S(1)} fusion(f32[512,64]{1,0:T(8,128)S(1)} %get-tuple-element.610, f32[32,2560]{1,0:T(8,128)S(1)} %get-tuple-element.519, f32[32,2560]{1,0:T(8,128)S(1)} %get-tuple-element.520), kind=kOutput, calls=%fused_computation.2.clone.1 | convolution fusion | flops 1006796800 | bytes 6029312 | tf_op jit(solution)/shard_map/while/body/eval_jaxpr/dot_general | solution.py:81
  198.8 6.0 %multiply_reduce_fusion.4 = (f32[2560]{0:T(1024)S(1)}, f32[2560]{0:T(1024)S(1)}, f32[2560]{0:T(1024)S(1)}, f32[2560]{0:T(1024)S(1)}) fusion(f32[128]{0:T(128)S(1)} %bitcast.72, f32[128]{0:T(128)S(1)} %bitcast.70, f32[512,2560]{1,0:T(8,128)S(1)} %convolution_bitcast_fusion.2, f32[2560]{0:T(1024)S(1)} %get-tuple-element.521, f32[2560]{0:T(1024)S(1)} %get-tuple-element.522), kind=kLoop, calls=%fused_computation.9.clone.1 | loop fusion | flops 6215680 | bytes 5305344 | tf_op jit(solution)/shard_map/while/body/eval_jaxpr/reduce_sum | solution.py:96
  206.4 12.4 %psum.23 = f32[]{:T(128)} all-reduce(f32[]{:T(128)S(6)} %mul_shard_map.3), channel_id=1, replica_groups=mesh['kcol'=8,'ion'=4] {'kcol'}, use_global_device_ids=true, to_apply=%region_11.12 | all-reduce | flops 1 | bytes 8 | tf_op jit(solution)/shard_map/psum | solution.py:134
  218.8 38.5 %all-reduce.2.cloned.1.call-done = f32[4,20480]{1,0:T(4,128)} async-done(((f32[4,20480]{1,0:T(4,128)}), f32[4,20480]{1,0:T(4,128)}) %all-reduce.2.cloned.1.call-update) | async-done | bytes 327696 | tf_op jit(solution)/shard_map/psum | solution.py:134
  257.3 1.4 constant_dynamic-slice_fusion
  (101 shorter events, 14.9 us)
Async XLA Ops:
  7.2 250.2 %all-reduce.2.cloned.1.call-start = ((), (), s32[]{:S(2)}) async-start(), calls=%async_computation | async-start | bytes 655360 | tf_op jit(solution)/shard_map/psum | solution.py:134
  205.0 0.7 copy-start
Sparse Core Ops, SparseCore 0:
  205.9 51.3 all-reduce.1
where the time goes:
time: 266 us
  other arithmetic  109 us (41%)
  matrix products  54.6 us (21%)
  blocking collectives  42.8 us (16%)
  waiting for transfers between devices  38.5 us (14%)
  between operations  14.8 us (6%)
  local copies, waits for them, and re-layouts  4.71 us (2%)
    reduce_sum x8, other arithmetic, force_piece(): force_y = force_scale * charge * jnp.sum(wave_y * imag_zero, 0)  47.9 us
    cos x8, other arithmetic, phase_tables(): jnp.cos(angle_yz)  38.6 us
    psum x1, waiting for transfers between devices, per_device(): summed, energy = lax.psum((row_forces, energy_group), 'kcol')  38.5 us
    dot_general x8, matrix products, force_piece(): jnp.dot(combined, basis, precision=lax.Precision.HIGHEST, preferred_eleme...  34.5 us
    dot_general x8, matrix products, factor_piece(): lax.dot_general(left, right, (((1,), (1,)), ((), ())), precision=lax.Prec...  20.1 us
    psum x1, blocking collectives, per_device(): factor = lax.psum(partial_value, 'ion')  19.3 us
    psum x1, blocking collectives, per_device(): summed, energy = lax.psum((row_forces, energy_group), 'kcol')  12.4 us
    all_gather x1, blocking collectives, per_device(): gathered = lax.all_gather(ions, 'kcol', axis=1, tiled=True)  11.2 us
  transfers between devices with their start and end apart: 1, of which 1 were waited for; matrix products, arithmetic and copies ran while one was open for 0% of the time, Pallas kernels for 0%

commit v1 on v0

v1 whole, which is shorter than its diff:
```python
import functools
import math

import jax
import jax.numpy as jnp
from jax import lax
from jax.experimental import pallas as pl
from jax.experimental.pallas import tpu as pltpu
from jax.sharding import PartitionSpec as P

KX = 32
SPAN = 64
LANES = 128
TILE = 256
COS_COEFFS = (
    0.9999992107823219,
    -19.738980355764017,
    64.92865742103359,
    -85.27162153430098,
    58.790492120130835,
    -21.07110562763074,
)


def cos_turns(turns):
    rest = turns - jnp.round(turns)
    square = rest * rest
    value = jnp.float32(COS_COEFFS[-1])
    for coeff in COS_COEFFS[-2::-1]:
        value = value * square + jnp.float32(coeff)
    return value


def split(value):
    high = value.astype(jnp.bfloat16)
    low = (value - high.astype(jnp.float32)).astype(jnp.bfloat16)
    return high, low


def lane_iota(rows):
    return lax.broadcasted_iota(jnp.int32, (rows, LANES), 1)


def column_of(block, row):
    return jnp.broadcast_to(block.T[:, row : row + 1], (LANES, LANES))


def fill_yz_tables(ions8_ref, table_ref):
    lane = lane_iota(LANES)
    wave = (lane % SPAN - SPAN // 2).astype(jnp.float32)
    shift = jnp.where(lane < SPAN, jnp.float32(0.0), jnp.float32(-0.25))

    def body(b, carry):
        base = pl.multiple_of(b * LANES, LANES)
        block = ions8_ref[:, pl.ds(base, LANES)]
        table_ref[pl.ds(base, LANES), :LANES] = cos_turns(column_of(block, 1) * wave + shift)
        table_ref[pl.ds(base, LANES), LANES:] = cos_turns(column_of(block, 2) * wave + shift)
        return carry

    lax.fori_loop(0, table_ref.shape[0] // LANES, body, 0)


def columns_block(table_ref, pick_ref, start, rows):
    y_part = table_ref[start : start + rows, :LANES]
    z_part = table_ref[start : start + rows, LANES:]

    def take(part, row):
        pick = jnp.broadcast_to(pick_ref[0, row : row + 1, :], (rows, LANES))
        return jnp.take_along_axis(part, pick, axis=1, mode="promise_in_bounds")

    cos_y, sin_y = take(y_part, 0), take(y_part, 1)
    cos_z, sin_z = take(z_part, 2), take(z_part, 3)
    return cos_y * cos_z - sin_y * sin_z, sin_y * cos_z + cos_y * sin_z


def fill_columns(table_ref, pick_ref, start, high_ref, low_ref, rows=64):
    for r in range(start, start + TILE, rows):
        cos_part, sin_part = columns_block(table_ref, pick_ref, r, rows)
        high_ref[r : r + rows, :LANES], low_ref[r : r + rows, :LANES] = split(cos_part)
        high_ref[r : r + rows, LANES:], low_ref[r : r + rows, LANES:] = split(sin_part)


def dot(a, b, dims=((1,), (0,))):
    return lax.dot_general(a, b, (dims, ((), ())), preferred_element_type=jnp.float32)


def factor_kernel(ions8_ref, pick_ref, out_ref, table_ref, left_ref, high_ref, low_ref):
    count = ions8_ref.shape[1]

    @pl.when(pl.program_id(0) == 0)
    def _():
        fill_yz_tables(ions8_ref, table_ref)
        wave = lax.broadcasted_iota(jnp.int32, (2 * KX, LANES), 0)
        shift = jnp.where(wave < KX, jnp.float32(0.0), jnp.float32(-0.25))
        wave = (wave % KX).astype(jnp.float32)

        def body(b, carry):
            at = pl.ds(pl.multiple_of(b * LANES, LANES), LANES)
            value = ions8_ref[3:4, at] * cos_turns(wave * ions8_ref[0:1, at] + shift)
            left_ref[: 2 * KX, at], left_ref[2 * KX :, at] = split(value)
            return carry

        lax.fori_loop(0, count // LANES, body, 0)

    total_high = jnp.zeros((4 * KX, 2 * LANES), jnp.float32)
    total_low = jnp.zeros((2 * KX, 2 * LANES), jnp.float32)
    for start in range(0, count, TILE):
        fill_columns(table_ref, pick_ref, start, high_ref, low_ref)
        left = left_ref[:, start : start + TILE]
        total_high += dot(left, high_ref[start : start + TILE, :])
        total_low += dot(left[: 2 * KX], low_ref[start : start + TILE, :])
    product = total_high[: 2 * KX] + total_high[2 * KX :] + total_low
    out_ref[0, :KX, :] = product[:KX, :LANES] - product[KX:, LANES:]
    out_ref[0, KX:, :] = product[:KX, LANES:] + product[KX:, :LANES]


def force_kernel(
    ions8_ref, pick_ref, wave_ref, factor_ref, out_ref, energy_ref, table_ref, high_ref, low_ref, sum_ref,
    *, force_scale, potential_scale,
):
    count = ions8_ref.shape[1]
    group = pl.program_id(0)

    @pl.when(group == 0)
    def _():
        fill_yz_tables(ions8_ref, table_ref)
        sum_ref[...] = jnp.zeros_like(sum_ref)

    wave_x = lax.broadcasted_iota(jnp.int32, (KX, LANES), 0)
    wave_y = jnp.broadcast_to(wave_ref[0, 0:1, :], (KX, LANES))
    wave_z = jnp.broadcast_to(wave_ref[0, 1:2, :], (KX, LANES))
    squared = wave_x * wave_x + (wave_y * wave_y + wave_z * wave_z)
    inside = (squared <= 1024) & (squared > 0)
    squared_f = squared.astype(jnp.float32)
    halving = jnp.where(wave_x == 0, jnp.float32(0.5), jnp.float32(1.0))
    weight = jnp.where(
        inside,
        halving * jnp.exp(-squared_f / 1600.0) / jnp.maximum(squared_f, 1.0),
        jnp.float32(0.0),
    )
    real = factor_ref[0, :KX, :]
    imag = factor_ref[0, KX:, :]
    energy_ref[0] = jnp.sum((weight * (real * real + imag * imag)).reshape(KX // 8, 8, LANES), 0)
    g_real = weight * real
    g_imag = -weight * imag
    base = jnp.concatenate(
        [jnp.concatenate([g_real, -g_imag], 1), jnp.concatenate([g_imag, g_real], 1)], 0
    )
    scale_x = (lax.broadcasted_iota(jnp.int32, (2 * KX, 1), 0) % KX).astype(jnp.float32)
    scale_y = jnp.concatenate([wave_ref[0, 0:1, :]] * 2, 1).astype(jnp.float32)
    scale_z = jnp.concatenate([wave_ref[0, 1:2, :]] * 2, 1).astype(jnp.float32)
    mix = jnp.concatenate([base, base * scale_y, base * scale_z, base * scale_x], 0)
    mix_high, mix_low = split(mix)
    nt = ((1,), (1,))
    for start in range(0, count, TILE):
        fill_columns(table_ref, pick_ref, start, high_ref, low_ref)
        high = high_ref[start : start + TILE, :]
        low = low_ref[start : start + TILE, :]
        sum_ref[start : start + TILE, :] += dot(high, mix_high, nt) + dot(high, mix_low, nt) + dot(low, mix_high, nt)

    @pl.when(group == pl.num_programs(0) - 1)
    def _():
        lane = lane_iota(LANES)
        wave = (lane % KX).astype(jnp.float32)
        quarter = lane // KX
        shift = jnp.where(quarter == 1, 0.25, jnp.where(quarter == 2, -0.25, 0.0)).astype(jnp.float32)
        row = lax.broadcasted_iota(jnp.int32, (8, 2 * LANES), 0)
        col = lax.broadcasted_iota(jnp.int32, (8, 2 * LANES), 1) // (2 * KX)
        pick = (row < 4) & (col == jnp.where(row == 0, 3, jnp.where(row == 3, 0, row)))
        pick = jnp.where(pick, 1.0, 0.0).astype(jnp.bfloat16)

        def body(b, carry):
            at = pl.ds(pl.multiple_of(b * LANES, LANES), LANES)
            phase = cos_turns(column_of(ions8_ref[:, at], 0) * wave + shift)
            other = jnp.where(lane < 2 * KX, pltpu.roll(phase, 2 * KX, 1), phase)
            value = sum_ref[at, :] * jnp.concatenate([phase, other], 1)
            value_high, value_low = split(value)
            sums = dot(pick, value_high, nt) + dot(pick, value_low, nt)
            charge = ions8_ref[3:4, at]
            out_ref[0:3, at] = sums[0:3] * (charge * jnp.float32(force_scale))
            out_ref[3:4, at] = sums[3:4] * jnp.float32(potential_scale)
            return carry

        lax.fori_loop(0, count // LANES, body, 0)


def tree_sum(parts):
    while len(parts) > 1:
        parts = [parts[i] + parts[i + 1] for i in range(0, len(parts), 2)]
    return parts[0]


def flip(value, axis, step):
    size = lax.axis_size(axis)
    return lax.ppermute(value, axis, [(i, i ^ step) for i in range(size)])


def swap_groups(value, step):
    return jnp.concatenate([value[i ^ step][None] for i in range(value.shape[0])], 0)


def per_device(ions, col_ids):
    groups = lax.axis_size("kcol")
    rows = lax.axis_size("ion")
    count = ions.shape[1]
    total = count * groups * rows
    cols = col_ids[None]
    step = 1
    while step < groups:
        cols = jnp.concatenate([cols, flip(cols, "kcol", step)], 0)
        step *= 2
    wave_y = cols // SPAN - SPAN // 2
    wave_z = cols % SPAN - SPAN // 2
    pick = jnp.stack([wave_y + SPAN // 2, wave_y + 3 * SPAN // 2, wave_z + SPAN // 2, wave_z + 3 * SPAN // 2], 1)
    waves = jnp.stack([wave_y, wave_z], 1)
    ions8 = jnp.concatenate([ions, jnp.zeros_like(ions)], 0)

    ions_spec = pl.BlockSpec((8, count), lambda g: (0, 0))
    pick_spec = pl.BlockSpec((1, 4, LANES), lambda g: (g, 0, 0))
    wave_spec = pl.BlockSpec((1, 2, LANES), lambda g: (g, 0, 0))
    factor_spec = pl.BlockSpec((1, 2 * KX, LANES), lambda g: (g, 0, 0))
    halves = [pltpu.VMEM((count, 2 * LANES), jnp.bfloat16)] * 2
    partial_factor = pl.pallas_call(
        factor_kernel,
        grid=(groups,),
        in_specs=[ions_spec, pick_spec],
        out_specs=factor_spec,
        out_shape=jax.ShapeDtypeStruct((groups, 2 * KX, LANES), jnp.float32),
        scratch_shapes=[
            pltpu.VMEM((count, 2 * LANES), jnp.float32),
            pltpu.VMEM((4 * KX, count), jnp.bfloat16),
            *halves,
        ],
        name="factor",
    )(ions8, pick)

    pairs = partial_factor.reshape(groups // 2, 2, 2 * KX, LANES)
    kept = pairs[:, 0] + flip(pairs[:, 1], "kcol", 1)
    step = 2
    while step < groups:
        kept = kept + swap_groups(flip(kept, "kcol", step), step // 2)
        step *= 2
    step = 1
    while step < rows:
        kept = kept + flip(kept, "ion", step)
        step *= 2
    factor = jnp.stack([kept, flip(kept, "kcol", 1)], 1).reshape(groups, 2 * KX, LANES)

    forces, energy_parts = pl.pallas_call(
        functools.partial(
            force_kernel,
            force_scale=0.04 * math.pi / math.sqrt(total),
            potential_scale=0.4 / math.sqrt(total),
        ),
        grid=(groups,),
        in_specs=[ions_spec, pick_spec, wave_spec, factor_spec],
        out_specs=[pl.BlockSpec((4, count), lambda g: (0, 0)), pl.BlockSpec((1, 8, LANES), lambda g: (g, 0, 0))],
        out_shape=[
            jax.ShapeDtypeStruct((4, count), jnp.float32),
            jax.ShapeDtypeStruct((groups, 8, LANES), jnp.float32),
        ],
        scratch_shapes=[
            pltpu.VMEM((count, 2 * LANES), jnp.float32),
            *halves,
            pltpu.VMEM((count, 2 * LANES), jnp.float32),
        ],
        name="force",
    )(ions8, pick, waves, factor)
    energy = jnp.float32(0.01 / total) * jnp.sum(tree_sum([energy_parts[i] for i in range(groups)]))
    return (forces, energy)


def solution(mesh):
    return jax.shard_map(
        per_device,
        mesh=mesh,
        in_specs=(P(None, ("kcol", "ion")), P("kcol")),
        out_specs=(P(None, ("kcol", "ion")), P()),
        check_vma=False,
    )
```

time: 266 us -> 103 us (0.39)
  other arithmetic: 109 us -> 3.42 us
  Pallas kernels: 0 us -> 60.3 us
  matrix products: 54.6 us -> 0 us
  blocking collectives: 42.8 us -> 0 us
  waiting for transfers between devices: 38.5 us -> 19.1 us
  starting transfers between devices: 0.04 us -> 14.7 us
  between operations: 14.8 us -> 2.5 us
    pallas_call x0 -> x2, Pallas kernels: none -> 60.3 us  [the longest x1 34.7 us: per_device(): pl.pallas_call(functools.partial(force_kernel, force_scale=0.04 * math.pi...]
    dot_general x16 -> x0, matrix products: 54.6 us -> none  [the longest x8 34.5 us: force_piece(): jnp.dot(combined, basis, precision=lax.Precision.HIGHEST, preferred_eleme...]
    cos x16 -> x0, other arithmetic: 48.3 us -> none  [the longest x8 38.6 us: phase_tables(): jnp.cos(angle_yz)]
    reduce_sum x9 -> x1, other arithmetic: 48.6 us -> 1.34 us  [per_device(): jnp.sum(tree_sum([energy_parts[i] for i in range(groups)]))]
    psum x1 -> x0, waiting for transfers between devices: 38.5 us -> none  [per_device(): summed, energy = lax.psum((row_forces, energy_group), 'kcol')]
    psum x2 -> x0, blocking collectives: 31.7 us -> none  [the longest x1 19.3 us: per_device(): factor = lax.psum(partial_value, 'ion')]
    ppermute x0 -> x9, waiting for transfers between devices: none -> 19.1 us  [flip(): return lax.ppermute(value, axis, [(i, i ^ step) for i in range(size)])]
    ppermute x0 -> x9, starting transfers between devices: none -> 14.7 us  [flip(): return lax.ppermute(value, axis, [(i, i ^ step) for i in range(size)])]
  transfers between devices with their start and end apart: 1 -> 9, of which waited for: 1 -> 9; matrix products, arithmetic and copies ran while one was open for 0% -> 2% of each run, Pallas kernels for 0% -> 0%
where the time goes in v1:
time: 103 us
  Pallas kernels  60.3 us (59%)
  waiting for transfers between devices  19.1 us (19%)
  starting transfers between devices  14.7 us (14%)
  other arithmetic  3.42 us (3%)
  local copies, waits for them, and re-layouts  3.07 us (3%)
  between operations  2.5 us (2%)
    pallas_call x1, Pallas kernels, per_device(): pl.pallas_call(functools.partial(force_kernel, force_scale=0.04 * math.pi...  34.7 us
    pallas_call x1, Pallas kernels, per_device(): pl.pallas_call(factor_kernel, grid=(groups,), in_specs=[ions_spec, pick_s...  25.7 us
    ppermute x9, waiting for transfers between devices, flip(): return lax.ppermute(value, axis, [(i, i ^ step) for i in range(size)])  19.1 us
    ppermute x9, starting transfers between devices, flip(): return lax.ppermute(value, axis, [(i, i ^ step) for i in range(size)])  14.7 us
  transfers between devices with their start and end apart: 9, of which 9 were waited for; matrix products, arithmetic and copies ran while one was open for 2% of the time, Pallas kernels for 0%

profile of v1, /device:TPU:0, one launch (start us, length us, event | category | flops | bytes accessed | tf_op | source)
XLA Modules:
  0.0 103.1 jit_solution(14904655833857050710)
XLA Ops:
  0.6 0.0 copy-start.1
  0.6 0.6 copy-done.1
  1.3 0.5 collective-permute-start
  1.8 0.8 collective-permute-done
  2.6 2.8 %collective-permute-start.1 = (s32[2,128]{1,0:T(2,128)S(1)}, s32[2,128]{1,0:T(2,128)S(1)}, u32[]{:S(2)}, u32[]{:S(2)}) collective-permute-start(s32[2,128]{1,0:T(2,128)S(1)} %pad_add_fusion.4), channel_id=1, source_target_pairs={{0,8},{4,12},{8,0},{12,4},{16,24},{20,28},{24,16},{28,20},{1,9},{5... | collective-permute-start | bytes 3080 | tf_op jit(solution)/shard_map/ppermute | solution.py:195
  5.4 1.6 %collective-permute-done.1 = s32[2,128]{1,0:T(2,128)S(1)} collective-permute-done((s32[2,128]{1,0:T(2,128)S(1)}, s32[2,128]{1,0:T(2,128)S(1)}, u32[]{:S(2)}, u32[]{:S(2)}) %collective-permute-start.1) | collective-permute-done | bytes 1056 | tf_op jit(solution)/shard_map/ppermute | solution.py:195
  7.0 2.1 %collective-permute-start.2 = (s32[4,128]{1,0:T(4,128)S(1)}, s32[4,128]{1,0:T(4,128)S(1)}, u32[]{:S(2)}, u32[]{:S(2)}) collective-permute-start(s32[4,128]{1,0:T(4,128)S(1)} %pad_add_fusion.3), channel_id=1, source_target_pairs={{0,16},{4,20},{8,24},{12,28},{16,0},{20,4},{24,8},{28,12},{1,17},{... | collective-permute-start | bytes 6152 | tf_op jit(solution)/shard_map/ppermute | solution.py:195
  9.1 1.4 %concatenate.113.ions8_ref = f32[8,2560]{1,0:T(8,128)} pad(f32[4,2560]{1,0:T(4,128)} %param.2, f32[]{:T(128)} %constant.33.clone.1), padding=0_4x0_0 | pad | bytes 122884 | tf_op jit(solution)/shard_map/concatenate | solution.py:216
  10.5 0.2 collective-permute-done.2
  10.7 0.6 pad_add_fusion.pick_ref
  11.3 25.7 %factor.1 = f32[8,64,128]{2,1,0:T(8,128)} custom-call(f32[8,2560]{1,0:T(8,128)} %concatenate.113.ions8_ref, s32[8,4,128]{2,1,0:T(4,128)} %pad_add_fusion.pick_ref), custom_call_target="tpu_custom_call" | custom-call | tf_op jit(solution)/shard_map/factor/pallas_call | solution.py:223
  37.0 0.0 copy-start
  37.0 1.0 slice_bitcast_fusion
  38.0 0.1 collective-permute-start.3
  38.1 1.3 %collective-permute-done.3 = f32[4,64,128]{2,1,0:T(8,128)S(1)} collective-permute-done((f32[4,64,128]{2,1,0:T(8,128)S(1)}, f32[4,64,128]{2,1,0:T(8,128)S(1)}, u32[]{:S(2)}, u32[]{:S(2)}) %collective-permute-start.3) | collective-permute-done | bytes 131104 | tf_op jit(solution)/shard_map/ppermute | solution.py:195
  39.4 0.0 copy-done
  39.4 2.1 %collective-permute-start.4 = (f32[4,64,128]{2,1,0:T(8,128)S(1)}, f32[4,64,128]{2,1,0:T(8,128)S(1)}, u32[]{:S(2)}, u32[]{:S(2)}) collective-permute-start(f32[4,64,128]{2,1,0:T(8,128)S(1)} %fusion), channel_id=1, source_target_pairs={{0,8},{4,12},{8,0},{12,4},{16,24},{20,28},{24,16},{28,20},{1,9},{5... | collective-permute-start | bytes 393224 | tf_op jit(solution)/shard_map/ppermute | solution.py:195
  41.5 3.8 %collective-permute-done.4 = f32[4,64,128]{2,1,0:T(8,128)S(1)} collective-permute-done((f32[4,64,128]{2,1,0:T(8,128)S(1)}, f32[4,64,128]{2,1,0:T(8,128)S(1)}, u32[]{:S(2)}, u32[]{:S(2)}) %collective-permute-start.4) | collective-permute-done | bytes 131104 | tf_op jit(solution)/shard_map/ppermute | solution.py:195
  45.4 1.8 %collective-permute-start.5 = (f32[4,64,128]{2,1,0:T(8,128)S(1)}, f32[4,64,128]{2,1,0:T(8,128)S(1)}, u32[]{:S(2)}, u32[]{:S(2)}) collective-permute-start(f32[4,64,128]{2,1,0:T(8,128)S(1)} %maximum_add_fusion), channel_id=1, source_target_pairs={{0,16},{4,20},{8,24},{12,28},{16,0},{20,4},{24,8},{28,12},{1,17},{... | collective-permute-start | bytes 393224 | tf_op jit(solution)/shard_map/ppermute | solution.py:195
  47.2 3.2 %collective-permute-done.5 = f32[4,64,128]{2,1,0:T(8,128)S(1)} collective-permute-done((f32[4,64,128]{2,1,0:T(8,128)S(1)}, f32[4,64,128]{2,1,0:T(8,128)S(1)}, u32[]{:S(2)}, u32[]{:S(2)}) %collective-permute-start.5) | collective-permute-done | bytes 131104 | tf_op jit(solution)/shard_map/ppermute | solution.py:195
  50.4 1.9 %collective-permute-start.6 = (f32[4,64,128]{2,1,0:T(8,128)S(1)}, f32[4,64,128]{2,1,0:T(8,128)S(1)}, u32[]{:S(2)}, u32[]{:S(2)}) collective-permute-start(f32[4,64,128]{2,1,0:T(8,128)S(1)} %maximum_add_fusion.1), channel_id=1, source_target_pairs={{0,1},{1,0},{2,3},{3,2},{4,5},{5,4},{6,7},{7,6},{8,9},{9,8},{10,11... | collective-permute-start | bytes 393224 | tf_op jit(solution)/shard_map/ppermute | solution.py:195
  52.3 3.1 %collective-permute-done.6 = f32[4,64,128]{2,1,0:T(8,128)S(1)} collective-permute-done((f32[4,64,128]{2,1,0:T(8,128)S(1)}, f32[4,64,128]{2,1,0:T(8,128)S(1)}, u32[]{:S(2)}, u32[]{:S(2)}) %collective-permute-start.6) | collective-permute-done | bytes 131104 | tf_op jit(solution)/shard_map/ppermute | solution.py:195
  55.5 3.3 %collective-permute-start.7 = (f32[4,64,128]{2,1,0:T(8,128)S(1)}, f32[4,64,128]{2,1,0:T(8,128)S(1)}, u32[]{:S(2)}, u32[]{:S(2)}) collective-permute-start(f32[4,64,128]{2,1,0:T(8,128)S(1)} %add.147), channel_id=1, source_target_pairs={{0,2},{1,3},{2,0},{3,1},{4,6},{5,7},{6,4},{7,5},{8,10},{9,11},{10,... | collective-permute-start | bytes 393224 | tf_op jit(solution)/shard_map/ppermute | solution.py:195
  58.8 4.4 %collective-permute-done.7 = f32[4,64,128]{2,1,0:T(8,128)S(1)} collective-permute-done((f32[4,64,128]{2,1,0:T(8,128)S(1)}, f32[4,64,128]{2,1,0:T(8,128)S(1)}, u32[]{:S(2)}, u32[]{:S(2)}) %collective-permute-start.7) | collective-permute-done | bytes 131104 | tf_op jit(solution)/shard_map/ppermute | solution.py:195
  63.2 0.1 collective-permute-start.8
  63.3 0.6 pad_add_fusion.1.wave_ref
  63.9 0.7 collective-permute-done.8
  64.6 0.7 pad_maximum_fusion
  65.3 34.7 %force.1 = (f32[4,2560]{1,0:T(4,128)}, f32[8,8,128]{2,1,0:T(8,128)}) custom-call(f32[8,2560]{1,0:T(8,128)} %concatenate.113.ions8_ref, s32[8,4,128]{2,1,0:T(4,128)} %pad_add_fusion.pick_ref, s32[8,2,128]{2,1,0:T(2,128)} %pad_add_fusion.1.wave_ref, f32[8,64,128]{2,1,0:T(8,128)} %bitcast.25), custom_call_target="tpu_custom_call" | custom-call | tf_op jit(solution)/shard_map/force/pallas_call | solution.py:249
  100.0 1.3 %add_reduce_fusion = f32[]{:T(128)} fusion(f32[8,8,128]{2,1,0:T(8,128)} %get-tuple-element.5), kind=kLoop, calls=%fused_computation.14 | loop fusion | flops 8191 | bytes 32772 | tf_op jit(solution)/shard_map/reduce_sum | solution.py:269
  (12 shorter events, 0.2 us)
Async XLA Ops:
  0.6 0.7 copy-start.1
  1.3 1.3 %collective-permute-start = (s32[1,128]{1,0:T(1,128)S(1)}, s32[1,128]{1,0:T(1,128)S(1)}, u32[]{:S(2)}, u32[]{:S(2)}) collective-permute-start(s32[1,128]{1,0:T(1,128)S(1)} %bitcast.28), channel_id=1, source_target_pairs={{0,4},{4,0},{8,12},{12,8},{16,20},{20,16},{24,28},{28,24},{1,5},{5... | collective-permute-start | bytes 1544 | tf_op jit(solution)/shard_map/ppermute | solution.py:195
  2.6 4.4 %collective-permute-start.1 = (s32[2,128]{1,0:T(2,128)S(1)}, s32[2,128]{1,0:T(2,128)S(1)}, u32[]{:S(2)}, u32[]{:S(2)}) collective-permute-start(s32[2,128]{1,0:T(2,128)S(1)} %pad_add_fusion.4), channel_id=1, source_target_pairs={{0,8},{4,12},{8,0},{12,4},{16,24},{20,28},{24,16},{28,20},{1,9},{5... | collective-permute-start | bytes 3080 | tf_op jit(solution)/shard_map/ppermute | solution.py:195
  7.0 3.7 %collective-permute-start.2 = (s32[4,128]{1,0:T(4,128)S(1)}, s32[4,128]{1,0:T(4,128)S(1)}, u32[]{:S(2)}, u32[]{:S(2)}) collective-permute-start(s32[4,128]{1,0:T(4,128)S(1)} %pad_add_fusion.3), channel_id=1, source_target_pairs={{0,16},{4,20},{8,24},{12,28},{16,0},{20,4},{24,8},{28,12},{1,17},{... | collective-permute-start | bytes 6152 | tf_op jit(solution)/shard_map/ppermute | solution.py:195
  37.0 2.4 %copy-start = (f32[8,64,128]{2,1,0:T(8,128)S(1)}, f32[8,64,128]{2,1,0:T(8,128)}, u32[]{:S(2)}) copy-start(f32[8,64,128]{2,1,0:T(8,128)} %factor.1) | copy-start | bytes 786436
  38.0 1.4 %collective-permute-start.3 = (f32[4,64,128]{2,1,0:T(8,128)S(1)}, f32[4,64,128]{2,1,0:T(8,128)S(1)}, u32[]{:S(2)}, u32[]{:S(2)}) collective-permute-start(f32[4,64,128]{2,1,0:T(8,128)S(1)} %slice_bitcast_fusion), channel_id=1, source_target_pairs={{0,4},{4,0},{8,12},{12,8},{16,20},{20,16},{24,28},{28,24},{1,5},{5... | collective-permute-start | bytes 393224 | tf_op jit(solution)/shard_map/ppermute | solution.py:195
  39.4 5.9 %collective-permute-start.4 = (f32[4,64,128]{2,1,0:T(8,128)S(1)}, f32[4,64,128]{2,1,0:T(8,128)S(1)}, u32[]{:S(2)}, u32[]{:S(2)}) collective-permute-start(f32[4,64,128]{2,1,0:T(8,128)S(1)} %fusion), channel_id=1, source_target_pairs={{0,8},{4,12},{8,0},{12,4},{16,24},{20,28},{24,16},{28,20},{1,9},{5... | collective-permute-start | bytes 393224 | tf_op jit(solution)/shard_map/ppermute | solution.py:195
  45.4 5.0 %collective-permute-start.5 = (f32[4,64,128]{2,1,0:T(8,128)S(1)}, f32[4,64,128]{2,1,0:T(8,128)S(1)}, u32[]{:S(2)}, u32[]{:S(2)}) collective-permute-start(f32[4,64,128]{2,1,0:T(8,128)S(1)} %maximum_add_fusion), channel_id=1, source_target_pairs={{0,16},{4,20},{8,24},{12,28},{16,0},{20,4},{24,8},{28,12},{1,17},{... | collective-permute-start | bytes 393224 | tf_op jit(solution)/shard_map/ppermute | solution.py:195
  50.4 5.0 %collective-permute-start.6 = (f32[4,64,128]{2,1,0:T(8,128)S(1)}, f32[4,64,128]{2,1,0:T(8,128)S(1)}, u32[]{:S(2)}, u32[]{:S(2)}) collective-permute-start(f32[4,64,128]{2,1,0:T(8,128)S(1)} %maximum_add_fusion.1), channel_id=1, source_target_pairs={{0,1},{1,0},{2,3},{3,2},{4,5},{5,4},{6,7},{7,6},{8,9},{9,8},{10,11... | collective-permute-start | bytes 393224 | tf_op jit(solution)/shard_map/ppermute | solution.py:195
  55.5 7.7 %collective-permute-start.7 = (f32[4,64,128]{2,1,0:T(8,128)S(1)}, f32[4,64,128]{2,1,0:T(8,128)S(1)}, u32[]{:S(2)}, u32[]{:S(2)}) collective-permute-start(f32[4,64,128]{2,1,0:T(8,128)S(1)} %add.147), channel_id=1, source_target_pairs={{0,2},{1,3},{2,0},{3,1},{4,6},{5,7},{6,4},{7,5},{8,10},{9,11},{10,... | collective-permute-start | bytes 393224 | tf_op jit(solution)/shard_map/ppermute | solution.py:195
  63.2 1.4 %collective-permute-start.8 = (f32[4,64,128]{2,1,0:T(8,128)S(1)}, f32[4,64,128]{2,1,0:T(8,128)S(1)}, u32[]{:S(2)}, u32[]{:S(2)}) collective-permute-start(f32[4,64,128]{2,1,0:T(8,128)S(1)} %add.148), channel_id=1, source_target_pairs={{0,4},{4,0},{8,12},{12,8},{16,20},{20,16},{24,28},{28,24},{1,5},{5... | collective-permute-start | bytes 393224 | tf_op jit(solution)/shard_map/ppermute | solution.py:195

commit v2 on v1

v2 whole, which is shorter than its diff:
```python
import functools
import math

import jax
import jax.numpy as jnp
from jax import lax
from jax.experimental import pallas as pl
from jax.experimental.pallas import tpu as pltpu
from jax.sharding import PartitionSpec as P

KX = 32
SPAN = 64
HALF = SPAN // 2
LANES = 128
TILE = 256
NT = ((1,), (1,))
NN = ((1,), (0,))
SIN_COEFFS = (3.1415902702069918, -5.167406733272337, 2.5440105185033337, -0.5594624554679438)
COS_COEFFS = (0.9999999532476085, -4.934792830619664, 4.058411352862771, -1.3318765680813944, 0.21968961109803095)


def horner(coeffs, square):
    value = jnp.float32(coeffs[-1])
    for coeff in coeffs[-2::-1]:
        value = value * square + jnp.float32(coeff)
    return value


def cos_sin_turns(turns):
    rest = turns - jnp.round(turns)
    square = rest * rest
    sin_half = rest * horner(SIN_COEFFS, square)
    cos_half = horner(COS_COEFFS, square)
    twice = sin_half + sin_half
    return 1.0 - twice * sin_half, twice * cos_half


def split(value):
    high = value.astype(jnp.bfloat16)
    low = (value - high.astype(jnp.float32)).astype(jnp.bfloat16)
    return high, low


def dot(a, b, dims):
    return lax.dot_general(a, b, (dims, ((), ())), preferred_element_type=jnp.float32)


def row_starts(rows):
    return sorted({*range(0, rows - 7, 8), rows - 8})


def table_kernel(ions_ref, cos_y, sin_y, cos_z, sin_z, basis_ref, left_ref, coord_ref):
    count = ions_ref.shape[1]
    rows = count // LANES
    for s in range(rows):
        at = slice(s * LANES, (s + 1) * LANES)
        coord_ref[0, s : s + 1, :] = ions_ref[1:2, at]
        coord_ref[1, s : s + 1, :] = ions_ref[2:3, at]

    def fill(m, carry):
        wave = m.astype(jnp.float32)
        for axis, (cos_ref, sin_ref) in enumerate(((cos_y, sin_y), (cos_z, sin_z))):
            cos_part, sin_part = cos_sin_turns(coord_ref[axis] * wave)
            up = pl.ds((HALF + m) * rows, rows)
            down = pl.ds((HALF - m) * rows, rows)
            cos_ref[up, :] = cos_part
            sin_ref[up, :] = sin_part
            cos_ref[down, :] = cos_part
            sin_ref[down, :] = -sin_part
        return carry

    lax.fori_loop(0, HALF + 1, fill, 0)
    wave_x = lax.broadcasted_iota(jnp.int32, (KX, LANES), 0).astype(jnp.float32)

    def body(b, carry):
        at = pl.ds(pl.multiple_of(b * LANES, LANES), LANES)
        cos_part, sin_part = cos_sin_turns(wave_x * ions_ref[0:1, at])
        basis_ref[:KX, at] = cos_part
        basis_ref[KX:, at] = sin_part
        charge = ions_ref[3:4, at]
        left_ref[:KX, at], left_ref[2 * KX : 3 * KX, at] = split(charge * cos_part)
        left_ref[KX : 2 * KX, at], left_ref[3 * KX :, at] = split(charge * sin_part)
        return carry

    lax.fori_loop(0, rows, body, 0)


def factor_kernel(pick_ref, cos_y, sin_y, cos_z, sin_z, left_ref, out_ref, high_ref, low_ref, cos_ref, sin_ref):
    rows = left_ref.shape[1] // LANES

    def column(c, carry):
        at_y = pick_ref[0, 0, c]
        at_z = pick_ref[0, 1, c]
        for start in row_starts(rows):
            y_at = pl.ds(at_y + start, 8)
            z_at = pl.ds(at_z + start, 8)
            cy, sy, cz, sz = cos_y[y_at, :], sin_y[y_at, :], cos_z[z_at, :], sin_z[z_at, :]
            at = pl.ds(c * rows + start, 8)
            cos_ref[at, :] = cy * cz - sy * sz
            sin_ref[at, :] = sy * cz + cy * sz
        return carry

    lax.fori_loop(0, LANES, column, 0, unroll=8)
    total_high = jnp.zeros((4 * KX, 2 * LANES), jnp.float32)
    total_low = jnp.zeros((2 * KX, 2 * LANES), jnp.float32)
    for tile in range(rows // 2):
        for s in (2 * tile, 2 * tile + 1):
            at = pl.ds(s, LANES, stride=rows)
            high_ref[0, s, :LANES, :], low_ref[0, s, :LANES, :] = split(cos_ref[at, :])
            high_ref[0, s, LANES:, :], low_ref[0, s, LANES:, :] = split(sin_ref[at, :])
        high = jnp.concatenate([high_ref[0, 2 * tile], high_ref[0, 2 * tile + 1]], 1)
        low = jnp.concatenate([low_ref[0, 2 * tile], low_ref[0, 2 * tile + 1]], 1)
        left = left_ref[:, tile * TILE : (tile + 1) * TILE]
        total_high += dot(left, high, NT)
        total_low += dot(left[: 2 * KX], low, NT)
    product = total_high[: 2 * KX] + total_high[2 * KX :] + total_low
    out_ref[0, :KX, :] = product[:KX, :LANES] - product[KX:, LANES:]
    out_ref[0, KX:, :] = product[:KX, LANES:] + product[KX:, :LANES]


def fill_mix(waves_ref, factor_ref, energy_ref, mix_ref, group):
    wave_x = lax.broadcasted_iota(jnp.int32, (KX, LANES), 0)
    wave_y = waves_ref[group, 0:1, :]
    wave_z = waves_ref[group, 1:2, :]
    squared = wave_x * wave_x + jnp.broadcast_to(wave_y * wave_y + wave_z * wave_z, (KX, LANES))
    inside = (squared <= 1024) & (squared > 0)
    squared_f = squared.astype(jnp.float32)
    halving = jnp.where(wave_x == 0, jnp.float32(0.5), jnp.float32(1.0))
    weight = jnp.where(
        inside,
        halving * jnp.exp(-squared_f / 1600.0) / jnp.maximum(squared_f, 1.0),
        jnp.float32(0.0),
    )
    real = factor_ref[group, :KX, :]
    imag = factor_ref[group, KX:, :]
    energy = weight * (real * real + imag * imag)
    energy_ref[group] = sum(energy[i : i + 8] for i in range(0, KX, 8))
    g_real = weight * real
    g_imag = -weight * imag
    wave_y = wave_y.astype(jnp.float32)
    wave_z = wave_z.astype(jnp.float32)
    lanes_cos = slice(group * TILE, group * TILE + LANES)
    lanes_sin = slice(group * TILE + LANES, (group + 1) * TILE)
    for part, scale in enumerate((None, wave_y, wave_z)):
        re, im = (g_real, g_imag) if scale is None else (g_real * scale, g_imag * scale)
        for offset, cos_value, sin_value in ((0, re, -im), (KX, im, re)):
            at = slice(part * 2 * KX + offset, part * 2 * KX + offset + KX)
            low_at = slice(6 * KX + at.start, 6 * KX + at.stop)
            mix_ref[at, lanes_cos], mix_ref[low_at, lanes_cos] = split(cos_value)
            mix_ref[at, lanes_sin], mix_ref[low_at, lanes_sin] = split(sin_value)


def force_kernel(
    waves_ref, factor_ref, high_ref, low_ref, basis_ref, ions_ref, out_ref, energy_ref, mix_ref,
    *, force_scale, potential_scale,
):
    groups = factor_ref.shape[0]

    @pl.when(pl.program_id(0) == 0)
    def _():
        for group in range(groups):
            fill_mix(waves_ref, factor_ref, energy_ref, mix_ref, group)

    def matrix(ref):
        return jnp.concatenate([ref[:, i].reshape(groups * TILE, LANES) for i in range(2)], 1)

    by_high = dot(mix_ref[...], matrix(high_ref), NN)
    by_low = dot(mix_ref[: 6 * KX, :], matrix(low_ref), NN)
    total = by_high[: 6 * KX] + by_high[6 * KX :] + by_low
    re0, im0, rey, imy, rez, imz = (total[i * KX : (i + 1) * KX] for i in range(6))
    cos_part = basis_ref[:KX, :]
    sin_part = basis_ref[KX:, :]
    wave_x = lax.broadcasted_iota(jnp.int32, (KX, TILE), 0).astype(jnp.float32)

    def reduce(value):
        return jnp.sum(value, 0, keepdims=True)

    charge = ions_ref[3:4, :] * jnp.float32(force_scale)
    out_ref[0:1, :] = charge * reduce(wave_x * (re0 * sin_part + im0 * cos_part))
    out_ref[1:2, :] = charge * reduce(rey * sin_part + imy * cos_part)
    out_ref[2:3, :] = charge * reduce(rez * sin_part + imz * cos_part)
    out_ref[3:4, :] = jnp.float32(potential_scale) * reduce(re0 * cos_part - im0 * sin_part)


def tree_sum(parts):
    while len(parts) > 1:
        parts = [parts[i] + parts[i + 1] for i in range(0, len(parts), 2)]
    return parts[0]


def flip(value, axis, step):
    size = lax.axis_size(axis)
    return lax.ppermute(value, axis, [(i, i ^ step) for i in range(size)])


def swap_groups(value, step):
    return jnp.concatenate([value[i ^ step][None] for i in range(value.shape[0])], 0)


def whole(shape):
    return pl.BlockSpec(shape, lambda g: (0,) * len(shape))


def per_device(ions, col_ids):
    groups = lax.axis_size("kcol")
    ranks = lax.axis_size("ion")
    count = ions.shape[1]
    rows = count // LANES
    total = count * groups * ranks
    table_shape = ((SPAN + 1) * rows, LANES)
    tables = pl.pallas_call(
        table_kernel,
        out_shape=[jax.ShapeDtypeStruct(table_shape, jnp.float32)] * 4
        + [
            jax.ShapeDtypeStruct((2 * KX, count), jnp.float32),
            jax.ShapeDtypeStruct((4 * KX, count), jnp.bfloat16),
        ],
        scratch_shapes=[pltpu.VMEM((2, rows, LANES), jnp.float32)],
        name="tables",
    )(ions)
    *yz_tables, basis, left = tables

    cols = col_ids[None]
    step = 1
    while step < groups:
        cols = jnp.concatenate([cols, flip(cols, "kcol", step)], 0)
        step *= 2
    index = jnp.stack([cols // SPAN, cols % SPAN], 1)
    waves = index - HALF

    pick_spec = pl.BlockSpec((1, 2, LANES), lambda g: (g, 0, 0), memory_space=pltpu.SMEM)
    halves_shape = jax.ShapeDtypeStruct((groups, rows, TILE, LANES), jnp.bfloat16)
    halves_spec = pl.BlockSpec((1, rows, TILE, LANES), lambda g: (g, 0, 0, 0))
    partial_factor, high, low = pl.pallas_call(
        factor_kernel,
        grid=(groups,),
        in_specs=[pick_spec, *[whole(table_shape)] * 4, whole((4 * KX, count))],
        out_specs=[pl.BlockSpec((1, 2 * KX, LANES), lambda g: (g, 0, 0)), halves_spec, halves_spec],
        out_shape=[jax.ShapeDtypeStruct((groups, 2 * KX, LANES), jnp.float32), halves_shape, halves_shape],
        scratch_shapes=[pltpu.VMEM((LANES * rows, LANES), jnp.float32)] * 2,
        name="factor",
    )(index * rows, *yz_tables, left)

    pairs = partial_factor.reshape(groups // 2, 2, 2 * KX, LANES)
    kept = pairs[:, 0] + flip(pairs[:, 1], "kcol", 1)
    step = 2
    while step < groups:
        kept = kept + swap_groups(flip(kept, "kcol", step), step // 2)
        step *= 2
    step = 1
    while step < ranks:
        kept = kept + flip(kept, "ion", step)
        step *= 2
    factor = jnp.stack([kept, flip(kept, "kcol", 1)], 1).reshape(groups, 2 * KX, LANES)

    tile_spec = pl.BlockSpec((groups, 2, TILE, LANES), lambda t: (0, t, 0, 0))
    forces, energy_parts = pl.pallas_call(
        functools.partial(
            force_kernel,
            force_scale=0.04 * math.pi / math.sqrt(total),
            potential_scale=0.4 / math.sqrt(total),
        ),
        grid=(count // TILE,),
        in_specs=[
            whole(waves.shape),
            whole(factor.shape),
            tile_spec,
            tile_spec,
            pl.BlockSpec((2 * KX, TILE), lambda t: (0, t)),
            pl.BlockSpec((4, TILE), lambda t: (0, t)),
        ],
        out_specs=[pl.BlockSpec((4, TILE), lambda t: (0, t)), whole((groups, 8, LANES))],
        out_shape=[
            jax.ShapeDtypeStruct((4, count), jnp.float32),
            jax.ShapeDtypeStruct((groups, 8, LANES), jnp.float32),
        ],
        scratch_shapes=[pltpu.VMEM((12 * KX, groups * TILE), jnp.bfloat16)],
        name="force",
    )(waves, factor, high, low, basis, ions)
    energy = jnp.float32(0.01 / total) * jnp.sum(tree_sum([energy_parts[i] for i in range(groups)]))
    return (forces, energy)


def solution(mesh):
    return jax.shard_map(
        per_device,
        mesh=mesh,
        in_specs=(P(None, ("kcol", "ion")), P("kcol")),
        out_specs=(P(None, ("kcol", "ion")), P()),
        check_vma=False,
    )
```

time: 103 us -> 78.4 us (0.76)
  Pallas kernels: 60.3 us -> 34.9 us
  waiting for transfers between devices: 19.1 us -> 21.7 us
  starting transfers between devices: 14.7 us -> 12.2 us
  other arithmetic: 3.42 us -> 5.66 us
  local copies, waits for them, and re-layouts: 3.07 us -> 0.93 us
    pallas_call x1, Pallas kernels: 34.7 us -> 14.2 us  [per_device(): pl.pallas_call(functools.partial(force_kernel, force_scale=0.04 * math.pi...]
    pallas_call x1 -> x2, Pallas kernels: 25.7 us -> 20.7 us  [the longest x1 16.6 us: per_device(): pl.pallas_call(factor_kernel, grid=(groups,), in_specs=[pick_spec, *[whol...]
    ppermute x9, waiting for transfers between devices: 19.1 us -> 21.7 us  [flip(): return lax.ppermute(value, axis, [(i, i ^ step) for i in range(size)])]
    ppermute x9, starting transfers between devices: 14.7 us -> 12.2 us  [flip(): return lax.ppermute(value, axis, [(i, i ^ step) for i in range(size)])]
    concatenate x1 -> x0, local copies, waits for them, and re-layouts: 1.41 us -> none  [per_device(): ions8 = jnp.concatenate([ions, jnp.zeros_like(ions)], 0)]
    concatenate x2, other arithmetic: 0.02 us -> 1.33 us  [per_device(): cols = jnp.concatenate([cols, flip(cols, 'kcol', step)], 0)]
    another operation x2 -> x0, other arithmetic: 1.22 us -> none  [the longest x1 0.62 us: per_device(): jnp.stack([wave_y + SPAN // 2, wave_y + 3 * SPAN // 2, wave_z + SPAN // 2...]
  transfers between devices with their start and end apart: 9 -> 9, of which waited for: 9 -> 8; matrix products, arithmetic and copies ran while one was open for 2% -> 0% of each run, Pallas kernels for 0% -> 5%
where the time goes in v2:
time: 78.4 us; the launch traced here: 77.9 us
  Pallas kernels  34.9 us (45%)
  waiting for transfers between devices  21.7 us (28%)
  starting transfers between devices  12.2 us (16%)
  other arithmetic  5.66 us (7%)
  between operations  2.48 us (3%)
  local copies, waits for them, and re-layouts  0.93 us (1%)
    ppermute x9, waiting for transfers between devices, flip(): return lax.ppermute(value, axis, [(i, i ^ step) for i in range(size)])  21.7 us
    pallas_call x1, Pallas kernels, per_device(): pl.pallas_call(factor_kernel, grid=(groups,), in_specs=[pick_spec, *[whol...  16.6 us
    pallas_call x1, Pallas kernels, per_device(): pl.pallas_call(functools.partial(force_kernel, force_scale=0.04 * math.pi...  14.2 us
    ppermute x9, starting transfers between devices, flip(): return lax.ppermute(value, axis, [(i, i ^ step) for i in range(size)])  12.2 us
    pallas_call x1, Pallas kernels, per_device(): pl.pallas_call(table_kernel, out_shape=[jax.ShapeDtypeStruct(table_shape,...  4.14 us
  transfers between devices with their start and end apart: 9, of which 8 were waited for; matrix products, arithmetic and copies ran while one was open for 0% of the time, Pallas kernels for 5%

profile of v2, /device:TPU:0, one launch (start us, length us, event | category | flops | bytes accessed | tf_op | source)
XLA Modules:
  0.0 77.9 jit_solution(17901864414794713329)
XLA Ops:
  0.6 0.6 collective-permute-start
  1.2 1.0 %collective-permute-done = s32[1,128]{1,0:T(1,128)S(1)} collective-permute-done((s32[1,128]{1,0:T(1,128)}, s32[1,128]{1,0:T(1,128)S(1)}, u32[]{:S(2)}, u32[]{:S(2)}) %collective-permute-start) | collective-permute-done | bytes 544 | tf_op jit(solution)/shard_map/ppermute | solution.py:193
  2.1 0.7 pad_add_fusion.3
  2.8 2.8 %collective-permute-start.1 = (s32[2,128]{1,0:T(2,128)S(1)}, s32[2,128]{1,0:T(2,128)S(1)}, u32[]{:S(2)}, u32[]{:S(2)}) collective-permute-start(s32[2,128]{1,0:T(2,128)S(1)} %pad_add_fusion.3), channel_id=1, source_target_pairs={{0,8},{4,12},{8,0},{12,4},{16,24},{20,28},{24,16},{28,20},{1,9},{5... | collective-permute-start | bytes 3080 | tf_op jit(solution)/shard_map/ppermute | solution.py:193
  5.6 1.6 %collective-permute-done.1 = s32[2,128]{1,0:T(2,128)S(1)} collective-permute-done((s32[2,128]{1,0:T(2,128)S(1)}, s32[2,128]{1,0:T(2,128)S(1)}, u32[]{:S(2)}, u32[]{:S(2)}) %collective-permute-start.1) | collective-permute-done | bytes 1056 | tf_op jit(solution)/shard_map/ppermute | solution.py:193
  7.2 0.7 pad_add_fusion.2
  7.8 2.1 %collective-permute-start.2 = (s32[4,128]{1,0:T(4,128)S(1)}, s32[4,128]{1,0:T(4,128)S(1)}, u32[]{:S(2)}, u32[]{:S(2)}) collective-permute-start(s32[4,128]{1,0:T(4,128)S(1)} %pad_add_fusion.2), channel_id=1, source_target_pairs={{0,16},{4,20},{8,24},{12,28},{16,0},{20,4},{24,8},{28,12},{1,17},{... | collective-permute-start | bytes 6152 | tf_op jit(solution)/shard_map/ppermute | solution.py:193
  9.9 4.1 %tables.1 = (f32[1300,128]{1,0:T(8,128)}, f32[1300,128]{1,0:T(8,128)}, f32[1300,128]{1,0:T(8,128)}, f32[1300,128]{1,0:T(8,128)}, f32[64,2560]{1,0:T(8,128)}, /*index=5*/bf16[128,2560]{1,0:T(8,128)(2,1)}) custom-call(f32[4,2560]{1,0:T(4,128)} %ions_ref.3), custom_call_target="tpu_custom_call" | custom-call | tf_op jit(solution)/shard_map/tables/pallas_call | solution.py:211
  14.0 0.0 collective-permute-done.2
  14.0 0.7 and_select_fusion.1
  14.7 0.6 broadcast_multiply_fusion
  15.3 16.6 %factor.1 = (f32[8,64,128]{2,1,0:T(8,128)}, bf16[8,20,256,128]{3,2,1,0:T(8,128)(2,1)}, bf16[8,20,256,128]{3,2,1,0:T(8,128)(2,1)}) custom-call(s32[8,2,128]{2,1,0:T(2,128)} %get-tuple-element.32.pick_ref, f32[1300,128]{1,0:T(8,128)} %get-tuple-element.13.cos_y, f32[1300,128]{1,0:T(8,128)} %get-tuple-element.14.sin_y, f32[1300,128]{1,0:T(8,128)} %get-tuple-element.15.cos_z, ...), custom_call_target="tpu_custom_call" | custom-call | tf_op jit(solution)/shard_map/factor/pallas_call | solution.py:234
  31.9 0.9 %slice_bitcast_fusion = f32[4,64,128]{2,1,0:T(8,128)S(1)} fusion(f32[4,2,64,128]{3,2,1,0:T(8,128)} %bitcast.25), kind=kLoop, calls=%fused_computation.1 | loop fusion | bytes 262144 | tf_op jit(solution)/shard_map/squeeze | solution.py:245
  32.8 0.1 collective-permute-start.3
  32.9 1.3 %collective-permute-done.3 = f32[4,64,128]{2,1,0:T(8,128)S(1)} collective-permute-done((f32[4,64,128]{2,1,0:T(8,128)S(1)}, f32[4,64,128]{2,1,0:T(8,128)S(1)}, u32[]{:S(2)}, u32[]{:S(2)}) %collective-permute-start.3) | collective-permute-done | bytes 131104 | tf_op jit(solution)/shard_map/ppermute | solution.py:193
  34.3 0.9 %fusion = f32[4,64,128]{2,1,0:T(8,128)S(1)} fusion(f32[4,64,128]{2,1,0:T(8,128)S(1)} %collective-permute-done.3, f32[4,2,64,128]{3,2,1,0:T(8,128)} %bitcast.26), kind=kLoop, calls=%fused_computation.3 | loop fusion | flops 32768 | bytes 393216 | tf_op jit(solution)/shard_map/add | solution.py:245
  35.2 1.6 %collective-permute-start.4 = (f32[4,64,128]{2,1,0:T(8,128)S(1)}, f32[4,64,128]{2,1,0:T(8,128)S(1)}, u32[]{:S(2)}, u32[]{:S(2)}) collective-permute-start(f32[4,64,128]{2,1,0:T(8,128)S(1)} %fusion), channel_id=1, source_target_pairs={{0,8},{4,12},{8,0},{12,4},{16,24},{20,28},{24,16},{28,20},{1,9},{5... | collective-permute-start | bytes 393224 | tf_op jit(solution)/shard_map/ppermute | solution.py:193
  36.7 4.1 %collective-permute-done.4 = f32[4,64,128]{2,1,0:T(8,128)S(1)} collective-permute-done((f32[4,64,128]{2,1,0:T(8,128)S(1)}, f32[4,64,128]{2,1,0:T(8,128)S(1)}, u32[]{:S(2)}, u32[]{:S(2)}) %collective-permute-start.4) | collective-permute-done | bytes 131104 | tf_op jit(solution)/shard_map/ppermute | solution.py:193
  40.8 0.3 collective-permute-start.5
  41.2 4.7 %collective-permute-done.5 = f32[4,64,128]{2,1,0:T(8,128)S(1)} collective-permute-done((f32[4,64,128]{2,1,0:T(8,128)S(1)}, f32[4,64,128]{2,1,0:T(8,128)S(1)}, u32[]{:S(2)}, u32[]{:S(2)}) %collective-permute-start.5) | collective-permute-done | bytes 131104 | tf_op jit(solution)/shard_map/ppermute | solution.py:193
  45.9 1.6 %collective-permute-start.6 = (f32[4,64,128]{2,1,0:T(8,128)S(1)}, f32[4,64,128]{2,1,0:T(8,128)S(1)}, u32[]{:S(2)}, u32[]{:S(2)}) collective-permute-start(f32[4,64,128]{2,1,0:T(8,128)S(1)} %maximum_add_fusion.1), channel_id=1, source_target_pairs={{0,1},{1,0},{2,3},{3,2},{4,5},{5,4},{6,7},{7,6},{8,9},{9,8},{10,11... | collective-permute-start | bytes 393224 | tf_op jit(solution)/shard_map/ppermute | solution.py:193
  47.6 3.4 %collective-permute-done.6 = f32[4,64,128]{2,1,0:T(8,128)S(1)} collective-permute-done((f32[4,64,128]{2,1,0:T(8,128)S(1)}, f32[4,64,128]{2,1,0:T(8,128)S(1)}, u32[]{:S(2)}, u32[]{:S(2)}) %collective-permute-start.6) | collective-permute-done | bytes 131104 | tf_op jit(solution)/shard_map/ppermute | solution.py:193
  51.0 3.1 %collective-permute-start.7 = (f32[4,64,128]{2,1,0:T(8,128)S(1)}, f32[4,64,128]{2,1,0:T(8,128)S(1)}, u32[]{:S(2)}, u32[]{:S(2)}) collective-permute-start(f32[4,64,128]{2,1,0:T(8,128)S(1)} %add.69), channel_id=1, source_target_pairs={{0,2},{1,3},{2,0},{3,1},{4,6},{5,7},{6,4},{7,5},{8,10},{9,11},{10,... | collective-permute-start | bytes 393224 | tf_op jit(solution)/shard_map/ppermute | solution.py:193
  54.1 4.4 %collective-permute-done.7 = f32[4,64,128]{2,1,0:T(8,128)S(1)} collective-permute-done((f32[4,64,128]{2,1,0:T(8,128)S(1)}, f32[4,64,128]{2,1,0:T(8,128)S(1)}, u32[]{:S(2)}, u32[]{:S(2)}) %collective-permute-start.7) | collective-permute-done | bytes 131104 | tf_op jit(solution)/shard_map/ppermute | solution.py:193
  58.4 0.1 collective-permute-start.8
  58.5 1.3 %collective-permute-done.8 = f32[4,64,128]{2,1,0:T(8,128)S(1)} collective-permute-done((f32[4,64,128]{2,1,0:T(8,128)S(1)}, f32[4,64,128]{2,1,0:T(8,128)S(1)}, u32[]{:S(2)}, u32[]{:S(2)}) %collective-permute-start.8) | collective-permute-done | bytes 131104 | tf_op jit(solution)/shard_map/ppermute | solution.py:193
  59.9 0.7 pad_maximum_fusion
  60.6 14.2 %force.1 = (f32[4,2560]{1,0:T(4,128)}, f32[8,8,128]{2,1,0:T(8,128)}) custom-call(s32[8,2,128]{2,1,0:T(2,128)} %get-tuple-element.33.waves_ref, f32[8,64,128]{2,1,0:T(8,128)} %bitcast.23, bf16[8,20,256,128]{3,2,1,0:T(8,128)(2,1)} %get-tuple-element.19.high_ref, bf16[8,20,256,128]{3,2,1,0:T(8,128)(2,1)} %get-tuple-element.20.low_ref, ...), custom_call_target="tpu_custom_call" | custom-call | tf_op jit(solution)/shard_map/force/pallas_call | solution.py:257
  74.8 1.3 %add_reduce_fusion = f32[]{:T(128)} fusion(f32[8,8,128]{2,1,0:T(8,128)} %get-tuple-element.23), kind=kLoop, calls=%fused_computation.13 | loop fusion | flops 8191 | bytes 32772 | tf_op jit(solution)/shard_map/reduce_sum | solution.py:280
  (7 shorter events, 0.1 us)
Async XLA Ops:
  0.6 1.5 %collective-permute-start = (s32[1,128]{1,0:T(1,128)}, s32[1,128]{1,0:T(1,128)S(1)}, u32[]{:S(2)}, u32[]{:S(2)}) collective-permute-start(s32[1,128]{1,0:T(1,128)} %bitcast.28), channel_id=1, source_target_pairs={{0,4},{4,0},{8,12},{12,8},{16,20},{20,16},{24,28},{28,24},{1,5},{5... | collective-permute-start | bytes 1544 | tf_op jit(solution)/shard_map/ppermute | solution.py:193
  2.8 4.4 %collective-permute-start.1 = (s32[2,128]{1,0:T(2,128)S(1)}, s32[2,128]{1,0:T(2,128)S(1)}, u32[]{:S(2)}, u32[]{:S(2)}) collective-permute-start(s32[2,128]{1,0:T(2,128)S(1)} %pad_add_fusion.3), channel_id=1, source_target_pairs={{0,8},{4,12},{8,0},{12,4},{16,24},{20,28},{24,16},{28,20},{1,9},{5... | collective-permute-start | bytes 3080 | tf_op jit(solution)/shard_map/ppermute | solution.py:193
  7.8 6.2 %collective-permute-start.2 = (s32[4,128]{1,0:T(4,128)S(1)}, s32[4,128]{1,0:T(4,128)S(1)}, u32[]{:S(2)}, u32[]{:S(2)}) collective-permute-start(s32[4,128]{1,0:T(4,128)S(1)} %pad_add_fusion.2), channel_id=1, source_target_pairs={{0,16},{4,20},{8,24},{12,28},{16,0},{20,4},{24,8},{28,12},{1,17},{... | collective-permute-start | bytes 6152 | tf_op jit(solution)/shard_map/ppermute | solution.py:193
  32.8 1.4 %collective-permute-start.3 = (f32[4,64,128]{2,1,0:T(8,128)S(1)}, f32[4,64,128]{2,1,0:T(8,128)S(1)}, u32[]{:S(2)}, u32[]{:S(2)}) collective-permute-start(f32[4,64,128]{2,1,0:T(8,128)S(1)} %slice_bitcast_fusion), channel_id=1, source_target_pairs={{0,4},{4,0},{8,12},{12,8},{16,20},{20,16},{24,28},{28,24},{1,5},{5... | collective-permute-start | bytes 393224 | tf_op jit(solution)/shard_map/ppermute | solution.py:193
  35.2 5.6 %collective-permute-start.4 = (f32[4,64,128]{2,1,0:T(8,128)S(1)}, f32[4,64,128]{2,1,0:T(8,128)S(1)}, u32[]{:S(2)}, u32[]{:S(2)}) collective-permute-start(f32[4,64,128]{2,1,0:T(8,128)S(1)} %fusion), channel_id=1, source_target_pairs={{0,8},{4,12},{8,0},{12,4},{16,24},{20,28},{24,16},{28,20},{1,9},{5... | collective-permute-start | bytes 393224 | tf_op jit(solution)/shard_map/ppermute | solution.py:193
  40.8 5.0 %collective-permute-start.5 = (f32[4,64,128]{2,1,0:T(8,128)S(1)}, f32[4,64,128]{2,1,0:T(8,128)S(1)}, u32[]{:S(2)}, u32[]{:S(2)}) collective-permute-start(f32[4,64,128]{2,1,0:T(8,128)S(1)} %maximum_add_fusion), channel_id=1, source_target_pairs={{0,16},{4,20},{8,24},{12,28},{16,0},{20,4},{24,8},{28,12},{1,17},{... | collective-permute-start | bytes 393224 | tf_op jit(solution)/shard_map/ppermute | solution.py:193
  45.9 5.0 %collective-permute-start.6 = (f32[4,64,128]{2,1,0:T(8,128)S(1)}, f32[4,64,128]{2,1,0:T(8,128)S(1)}, u32[]{:S(2)}, u32[]{:S(2)}) collective-permute-start(f32[4,64,128]{2,1,0:T(8,128)S(1)} %maximum_add_fusion.1), channel_id=1, source_target_pairs={{0,1},{1,0},{2,3},{3,2},{4,5},{5,4},{6,7},{7,6},{8,9},{9,8},{10,11... | collective-permute-start | bytes 393224 | tf_op jit(solution)/shard_map/ppermute | solution.py:193
  51.0 7.4 %collective-permute-start.7 = (f32[4,64,128]{2,1,0:T(8,128)S(1)}, f32[4,64,128]{2,1,0:T(8,128)S(1)}, u32[]{:S(2)}, u32[]{:S(2)}) collective-permute-start(f32[4,64,128]{2,1,0:T(8,128)S(1)} %add.69), channel_id=1, source_target_pairs={{0,2},{1,3},{2,0},{3,1},{4,6},{5,7},{6,4},{7,5},{8,10},{9,11},{10,... | collective-permute-start | bytes 393224 | tf_op jit(solution)/shard_map/ppermute | solution.py:193
  58.4 1.4 %collective-permute-start.8 = (f32[4,64,128]{2,1,0:T(8,128)S(1)}, f32[4,64,128]{2,1,0:T(8,128)S(1)}, u32[]{:S(2)}, u32[]{:S(2)}) collective-permute-start(f32[4,64,128]{2,1,0:T(8,128)S(1)} %add.70), channel_id=1, source_target_pairs={{0,4},{4,0},{8,12},{12,8},{16,20},{20,16},{24,28},{28,24},{1,5},{5... | collective-permute-start | bytes 393224 | tf_op jit(solution)/shard_map/ppermute | solution.py:193

commit v3 on v2

--- a/solution.py
+++ b/solution.py
@@ -13,6 +13,7 @@
 HALF = SPAN // 2
 LANES = 128
 TILE = 256
+MIB = 1 << 20
 NT = ((1,), (1,))
 NN = ((1,), (0,))
 SIN_COEFFS = (3.1415902702069918, -5.167406733272337, 2.5440105185033337, -0.5594624554679438)
@@ -216,6 +217,7 @@
             jax.ShapeDtypeStruct((4 * KX, count), jnp.bfloat16),
         ],
         scratch_shapes=[pltpu.VMEM((2, rows, LANES), jnp.float32)],
+        compiler_params=pltpu.CompilerParams(vmem_limit_bytes=8 * MIB),
         name="tables",
     )(ions)
     *yz_tables, basis, left = tables
@@ -238,6 +240,7 @@
         out_specs=[pl.BlockSpec((1, 2 * KX, LANES), lambda g: (g, 0, 0)), halves_spec, halves_spec],
         out_shape=[jax.ShapeDtypeStruct((groups, 2 * KX, LANES), jnp.float32), halves_shape, halves_shape],
         scratch_shapes=[pltpu.VMEM((LANES * rows, LANES), jnp.float32)] * 2,
+        compiler_params=pltpu.CompilerParams(vmem_limit_bytes=20 * MIB),
         name="factor",
     )(index * rows, *yz_tables, left)
 
@@ -275,6 +278,7 @@
             jax.ShapeDtypeStruct((groups, 8, LANES), jnp.float32),
         ],
         scratch_shapes=[pltpu.VMEM((12 * KX, groups * TILE), jnp.bfloat16)],
+        compiler_params=pltpu.CompilerParams(vmem_limit_bytes=16 * MIB),
         name="force",
     )(waves, factor, high, low, basis, ions)
     energy = jnp.float32(0.01 / total) * jnp.sum(tree_sum([energy_parts[i] for i in range(groups)]))

time: 78.4 us -> 66.8 us (0.85)
  Pallas kernels: 34.9 us -> 25.8 us
  other arithmetic: 5.66 us -> 2.74 us
  waiting for transfers between devices: 21.7 us -> 20.6 us
  starting transfers between devices: 12.2 us -> 13.2 us
    pallas_call x1, Pallas kernels: 14.2 us -> 10.5 us  [per_device(): pl.pallas_call(functools.partial(force_kernel, force_scale=0.04 * math.pi...]
    pallas_call x1, Pallas kernels: 16.6 us -> 13.9 us  [per_device(): pl.pallas_call(factor_kernel, grid=(groups,), in_specs=[pick_spec, *[whol...]
    pallas_call x1, Pallas kernels: 4.14 us -> 1.47 us  [per_device(): pl.pallas_call(table_kernel, out_shape=[jax.ShapeDtypeStruct(table_shape,...]
    unnamed x0 -> x4, local copies, waits for them, and re-layouts: none -> 1.55 us
    ppermute x9, starting transfers between devices: 12.2 us -> 13.2 us  [flip(): return lax.ppermute(value, axis, [(i, i ^ step) for i in range(size)])]
    ppermute x9, waiting for transfers between devices: 21.7 us -> 20.6 us  [flip(): return lax.ppermute(value, axis, [(i, i ^ step) for i in range(size)])]
    add x1, other arithmetic: 0.93 us -> 0.02 us  [per_device(): kept = pairs[:, 0] + flip(pairs[:, 1], 'kcol', 1)]
    squeeze x1, local copies, waits for them, and re-layouts: 0.91 us -> 0.01 us  [per_device(): kept = pairs[:, 0] + flip(pairs[:, 1], 'kcol', 1)]
  transfers between devices with their start and end apart: 9 -> 9, of which waited for: 8 -> 8; matrix products, arithmetic and copies ran while one was open for 0% -> 0% of each run, Pallas kernels for 5% -> 2%
where the time goes in v3:
time: 66.8 us; the launch traced here: 66.6 us
  Pallas kernels  25.8 us (39%)
  waiting for transfers between devices  20.6 us (31%)
  starting transfers between devices  13.2 us (20%)
  other arithmetic  2.74 us (4%)
  between operations  2.53 us (4%)
  local copies, waits for them, and re-layouts  1.58 us (2%)
    ppermute x9, waiting for transfers between devices, flip(): return lax.ppermute(value, axis, [(i, i ^ step) for i in range(size)])  20.6 us
    pallas_call x1, Pallas kernels, per_device(): pl.pallas_call(factor_kernel, grid=(groups,), in_specs=[pick_spec, *[whol...  13.9 us
    ppermute x9, starting transfers between devices, flip(): return lax.ppermute(value, axis, [(i, i ^ step) for i in range(size)])  13.2 us
    pallas_call x1, Pallas kernels, per_device(): pl.pallas_call(functools.partial(force_kernel, force_scale=0.04 * math.pi...  10.5 us
    unnamed x4, local copies, waits for them, and re-layouts  1.55 us
    pallas_call x1, Pallas kernels, per_device(): pl.pallas_call(table_kernel, out_shape=[jax.ShapeDtypeStruct(table_shape,...  1.47 us
  transfers between devices with their start and end apart: 9, of which 8 were waited for; matrix products, arithmetic and copies ran while one was open for 0% of the time, Pallas kernels for 2%

profile of v3, /device:TPU:0, one launch (start us, length us, event | category | flops | bytes accessed | tf_op | source)
XLA Modules:
  0.0 66.6 jit_solution(11669330800273097898)
XLA Ops:
  0.6 0.6 collective-permute-start
  1.2 1.0 %collective-permute-done = s32[1,128]{1,0:T(1,128)S(1)} collective-permute-done((s32[1,128]{1,0:T(1,128)}, s32[1,128]{1,0:T(1,128)S(1)}, u32[]{:S(2)}, u32[]{:S(2)}) %collective-permute-start) | collective-permute-done | bytes 544 | tf_op jit(solution)/shard_map/ppermute | solution.py:194
  2.1 0.7 pad_add_fusion.3
  2.8 2.8 %collective-permute-start.1 = (s32[2,128]{1,0:T(2,128)S(1)}, s32[2,128]{1,0:T(2,128)S(1)}, u32[]{:S(2)}, u32[]{:S(2)}) collective-permute-start(s32[2,128]{1,0:T(2,128)S(1)} %pad_add_fusion.3), channel_id=1, source_target_pairs={{0,8},{4,12},{8,0},{12,4},{16,24},{20,28},{24,16},{28,20},{1,9},{5... | collective-permute-start | bytes 3080 | tf_op jit(solution)/shard_map/ppermute | solution.py:194
  5.6 1.6 %collective-permute-done.1 = s32[2,128]{1,0:T(2,128)S(1)} collective-permute-done((s32[2,128]{1,0:T(2,128)S(1)}, s32[2,128]{1,0:T(2,128)S(1)}, u32[]{:S(2)}, u32[]{:S(2)}) %collective-permute-start.1) | collective-permute-done | bytes 1056 | tf_op jit(solution)/shard_map/ppermute | solution.py:194
  7.2 0.7 pad_add_fusion.2
  7.8 2.1 %collective-permute-start.2 = (s32[4,128]{1,0:T(4,128)S(1)}, s32[4,128]{1,0:T(4,128)S(1)}, u32[]{:S(2)}, u32[]{:S(2)}) collective-permute-start(s32[4,128]{1,0:T(4,128)S(1)} %pad_add_fusion.2), channel_id=1, source_target_pairs={{0,16},{4,20},{8,24},{12,28},{16,0},{20,4},{24,8},{28,12},{1,17},{... | collective-permute-start | bytes 6152 | tf_op jit(solution)/shard_map/ppermute | solution.py:194
  9.9 0.0 copy-start
  9.9 0.8 %copy-done = f32[4,2560]{1,0:T(4,128)S(1)} copy-done((f32[4,2560]{1,0:T(4,128)S(1)}, f32[4,2560]{1,0:T(4,128)}, u32[]{:S(2)}) %copy-start) | copy-done | bytes 40984
  10.7 1.5 %tables.1 = (f32[1300,128]{1,0:T(8,128)S(1)}, f32[1300,128]{1,0:T(8,128)S(1)}, f32[1300,128]{1,0:T(8,128)S(1)}, f32[1300,128]{1,0:T(8,128)S(1)}, f32[64,2560]{1,0:T(8,128)S(1)}, /*index=5*/bf16[128,2560]{1,0:T(8,128)(2,1)S(1)}) custom-call(f32[4,2560]{1,0:T(4,128)S(1)} %copy-done), custom_call_target="tpu_custom_call" | custom-call | tf_op jit(solution)/shard_map/tables/pallas_call | solution.py:212
  12.1 0.0 collective-permute-done.2
  12.2 0.7 %and_select_fusion.1 = (s32[8,1,128]{2,1,0:T(1,128)S(1)}, s32[8,1,128]{2,1,0:T(1,128)S(1)}) fusion(s32[4,1,128]{2,1,0:T(1,128)S(1)} %bitcast.34, s32[2,1,128]{2,1,0:T(1,128)S(1)} %bitcast.33, s32[1,1,128]{2,1,0:T(1,128)S(1)} %bitcast.32, s32[1,1,128]{2,1,0:T(1,128)} %bitcast.31), kind=kLoop, calls=%fused_computation.7 | loop fusion | flops 18432 | bytes 12288 | tf_op jit(solution)/shard_map/jit(floor_divide)/jit(_where)/select_n | solution.py:230
  12.9 13.9 %factor.1 = (f32[8,64,128]{2,1,0:T(8,128)S(1)}, bf16[8,20,256,128]{3,2,1,0:T(8,128)(2,1)S(1)}, bf16[8,20,256,128]{3,2,1,0:T(8,128)(2,1)S(1)}) custom-call(s32[8,2,128]{2,1,0:T(2,128)S(1)} %get-tuple-element.32.pick_ref, f32[1300,128]{1,0:T(8,128)S(1)} %get-tuple-element.13.cos_y, f32[1300,128]{1,0:T(8,128)S(1)} %get-tuple-element.14.sin_y, ...), custom_call_target="tpu_custom_call" | custom-call | tf_op jit(solution)/shard_map/factor/pallas_call | solution.py:236
  26.8 0.1 collective-permute-start.3
  26.9 1.3 %collective-permute-done.3 = f32[4,64,128]{2,1,0:T(8,128)S(1)} collective-permute-done((f32[4,64,128]{2,1,0:T(8,128)S(1)}, f32[4,64,128]{2,1,0:T(8,128)S(1)}, u32[]{:S(2)}, u32[]{:S(2)}) %collective-permute-start.3) | collective-permute-done | bytes 131104 | tf_op jit(solution)/shard_map/ppermute | solution.py:194
  28.2 1.6 %collective-permute-start.4 = (f32[4,64,128]{2,1,0:T(8,128)S(1)}, f32[4,64,128]{2,1,0:T(8,128)S(1)}, u32[]{:S(2)}, u32[]{:S(2)}) collective-permute-start(f32[4,64,128]{2,1,0:T(8,128)S(1)} %fusion), channel_id=1, source_target_pairs={{0,8},{4,12},{8,0},{12,4},{16,24},{20,28},{24,16},{28,20},{1,9},{5... | collective-permute-start | bytes 393224 | tf_op jit(solution)/shard_map/ppermute | solution.py:194
  29.8 4.1 %collective-permute-done.4 = f32[4,64,128]{2,1,0:T(8,128)S(1)} collective-permute-done((f32[4,64,128]{2,1,0:T(8,128)S(1)}, f32[4,64,128]{2,1,0:T(8,128)S(1)}, u32[]{:S(2)}, u32[]{:S(2)}) %collective-permute-start.4) | collective-permute-done | bytes 131104 | tf_op jit(solution)/shard_map/ppermute | solution.py:194
  33.9 1.4 %collective-permute-start.5 = (f32[4,64,128]{2,1,0:T(8,128)S(1)}, f32[4,64,128]{2,1,0:T(8,128)S(1)}, u32[]{:S(2)}, u32[]{:S(2)}) collective-permute-start(f32[4,64,128]{2,1,0:T(8,128)S(1)} %maximum_add_fusion), channel_id=1, source_target_pairs={{0,16},{4,20},{8,24},{12,28},{16,0},{20,4},{24,8},{28,12},{1,17},{... | collective-permute-start | bytes 393224 | tf_op jit(solution)/shard_map/ppermute | solution.py:194
  35.3 3.6 %collective-permute-done.5 = f32[4,64,128]{2,1,0:T(8,128)S(1)} collective-permute-done((f32[4,64,128]{2,1,0:T(8,128)S(1)}, f32[4,64,128]{2,1,0:T(8,128)S(1)}, u32[]{:S(2)}, u32[]{:S(2)}) %collective-permute-start.5) | collective-permute-done | bytes 131104 | tf_op jit(solution)/shard_map/ppermute | solution.py:194
  39.0 1.6 %collective-permute-start.6 = (f32[4,64,128]{2,1,0:T(8,128)S(1)}, f32[4,64,128]{2,1,0:T(8,128)S(1)}, u32[]{:S(2)}, u32[]{:S(2)}) collective-permute-start(f32[4,64,128]{2,1,0:T(8,128)S(1)} %maximum_add_fusion.1), channel_id=1, source_target_pairs={{0,1},{1,0},{2,3},{3,2},{4,5},{5,4},{6,7},{7,6},{8,9},{9,8},{10,11... | collective-permute-start | bytes 393224 | tf_op jit(solution)/shard_map/ppermute | solution.py:194
  40.6 3.4 %collective-permute-done.6 = f32[4,64,128]{2,1,0:T(8,128)S(1)} collective-permute-done((f32[4,64,128]{2,1,0:T(8,128)S(1)}, f32[4,64,128]{2,1,0:T(8,128)S(1)}, u32[]{:S(2)}, u32[]{:S(2)}) %collective-permute-start.6) | collective-permute-done | bytes 131104 | tf_op jit(solution)/shard_map/ppermute | solution.py:194
  44.0 3.1 %collective-permute-start.7 = (f32[4,64,128]{2,1,0:T(8,128)S(1)}, f32[4,64,128]{2,1,0:T(8,128)S(1)}, u32[]{:S(2)}, u32[]{:S(2)}) collective-permute-start(f32[4,64,128]{2,1,0:T(8,128)S(1)} %add.69), channel_id=1, source_target_pairs={{0,2},{1,3},{2,0},{3,1},{4,6},{5,7},{6,4},{7,5},{8,10},{9,11},{10,... | collective-permute-start | bytes 393224 | tf_op jit(solution)/shard_map/ppermute | solution.py:194
  47.1 4.4 %collective-permute-done.7 = f32[4,64,128]{2,1,0:T(8,128)S(1)} collective-permute-done((f32[4,64,128]{2,1,0:T(8,128)S(1)}, f32[4,64,128]{2,1,0:T(8,128)S(1)}, u32[]{:S(2)}, u32[]{:S(2)}) %collective-permute-start.7) | collective-permute-done | bytes 131104 | tf_op jit(solution)/shard_map/ppermute | solution.py:194
  51.5 0.1 collective-permute-start.8
  51.6 1.3 %collective-permute-done.8 = f32[4,64,128]{2,1,0:T(8,128)S(1)} collective-permute-done((f32[4,64,128]{2,1,0:T(8,128)S(1)}, f32[4,64,128]{2,1,0:T(8,128)S(1)}, u32[]{:S(2)}, u32[]{:S(2)}) %collective-permute-start.8) | collective-permute-done | bytes 131104 | tf_op jit(solution)/shard_map/ppermute | solution.py:194
  52.9 0.0 copy-start.1
  52.9 0.8 %copy-done.1 = f32[4,2560]{1,0:T(4,128)S(1)} copy-done((f32[4,2560]{1,0:T(4,128)S(1)}, f32[4,2560]{1,0:T(4,128)}, u32[]{:S(2)}) %copy-start.1) | copy-done | bytes 40984
  53.7 10.5 %force.1 = (f32[4,2560]{1,0:T(4,128)}, f32[8,8,128]{2,1,0:T(8,128)S(1)}) custom-call(s32[8,2,128]{2,1,0:T(2,128)S(1)} %get-tuple-element.33.waves_ref, f32[8,64,128]{2,1,0:T(8,128)S(1)} %bitcast.23, bf16[8,20,256,128]{3,2,1,0:T(8,128)(2,1)S(1)} %get-tuple-element.19.high_ref, bf16[8,20,256,128]{3,2,1,0:T(8,128)(2,1)S(1)} %get-tuple-element.20.low_ref, ...), custom_call_target="tpu_custom_call" | custom-call | tf_op jit(solution)/shard_map/force/pallas_call | solution.py:260
  64.2 0.6 add_reduce_fusion
  (11 shorter events, 0.2 us)
Async XLA Ops:
  0.6 1.5 %collective-permute-start = (s32[1,128]{1,0:T(1,128)}, s32[1,128]{1,0:T(1,128)S(1)}, u32[]{:S(2)}, u32[]{:S(2)}) collective-permute-start(s32[1,128]{1,0:T(1,128)} %bitcast.28), channel_id=1, source_target_pairs={{0,4},{4,0},{8,12},{12,8},{16,20},{20,16},{24,28},{28,24},{1,5},{5... | collective-permute-start | bytes 1544 | tf_op jit(solution)/shard_map/ppermute | solution.py:194
  2.8 4.4 %collective-permute-start.1 = (s32[2,128]{1,0:T(2,128)S(1)}, s32[2,128]{1,0:T(2,128)S(1)}, u32[]{:S(2)}, u32[]{:S(2)}) collective-permute-start(s32[2,128]{1,0:T(2,128)S(1)} %pad_add_fusion.3), channel_id=1, source_target_pairs={{0,8},{4,12},{8,0},{12,4},{16,24},{20,28},{24,16},{28,20},{1,9},{5... | collective-permute-start | bytes 3080 | tf_op jit(solution)/shard_map/ppermute | solution.py:194
  7.8 4.3 %collective-permute-start.2 = (s32[4,128]{1,0:T(4,128)S(1)}, s32[4,128]{1,0:T(4,128)S(1)}, u32[]{:S(2)}, u32[]{:S(2)}) collective-permute-start(s32[4,128]{1,0:T(4,128)S(1)} %pad_add_fusion.2), channel_id=1, source_target_pairs={{0,16},{4,20},{8,24},{12,28},{16,0},{20,4},{24,8},{28,12},{1,17},{... | collective-permute-start | bytes 6152 | tf_op jit(solution)/shard_map/ppermute | solution.py:194
  9.9 0.8 %copy-start = (f32[4,2560]{1,0:T(4,128)S(1)}, f32[4,2560]{1,0:T(4,128)}, u32[]{:S(2)}) copy-start(f32[4,2560]{1,0:T(4,128)} %ions_ref.3) | copy-start | bytes 122884
  26.8 1.4 %collective-permute-start.3 = (f32[4,64,128]{2,1,0:T(8,128)S(1)}, f32[4,64,128]{2,1,0:T(8,128)S(1)}, u32[]{:S(2)}, u32[]{:S(2)}) collective-permute-start(f32[4,64,128]{2,1,0:T(8,128)S(1)} %slice_bitcast_fusion), channel_id=1, source_target_pairs={{0,4},{4,0},{8,12},{12,8},{16,20},{20,16},{24,28},{28,24},{1,5},{5... | collective-permute-start | bytes 393224 | tf_op jit(solution)/shard_map/ppermute | solution.py:194
  28.2 5.6 %collective-permute-start.4 = (f32[4,64,128]{2,1,0:T(8,128)S(1)}, f32[4,64,128]{2,1,0:T(8,128)S(1)}, u32[]{:S(2)}, u32[]{:S(2)}) collective-permute-start(f32[4,64,128]{2,1,0:T(8,128)S(1)} %fusion), channel_id=1, source_target_pairs={{0,8},{4,12},{8,0},{12,4},{16,24},{20,28},{24,16},{28,20},{1,9},{5... | collective-permute-start | bytes 393224 | tf_op jit(solution)/shard_map/ppermute | solution.py:194
  33.9 5.0 %collective-permute-start.5 = (f32[4,64,128]{2,1,0:T(8,128)S(1)}, f32[4,64,128]{2,1,0:T(8,128)S(1)}, u32[]{:S(2)}, u32[]{:S(2)}) collective-permute-start(f32[4,64,128]{2,1,0:T(8,128)S(1)} %maximum_add_fusion), channel_id=1, source_target_pairs={{0,16},{4,20},{8,24},{12,28},{16,0},{20,4},{24,8},{28,12},{1,17},{... | collective-permute-start | bytes 393224 | tf_op jit(solution)/shard_map/ppermute | solution.py:194
  39.0 5.0 %collective-permute-start.6 = (f32[4,64,128]{2,1,0:T(8,128)S(1)}, f32[4,64,128]{2,1,0:T(8,128)S(1)}, u32[]{:S(2)}, u32[]{:S(2)}) collective-permute-start(f32[4,64,128]{2,1,0:T(8,128)S(1)} %maximum_add_fusion.1), channel_id=1, source_target_pairs={{0,1},{1,0},{2,3},{3,2},{4,5},{5,4},{6,7},{7,6},{8,9},{9,8},{10,11... | collective-permute-start | bytes 393224 | tf_op jit(solution)/shard_map/ppermute | solution.py:194
  44.0 7.4 %collective-permute-start.7 = (f32[4,64,128]{2,1,0:T(8,128)S(1)}, f32[4,64,128]{2,1,0:T(8,128)S(1)}, u32[]{:S(2)}, u32[]{:S(2)}) collective-permute-start(f32[4,64,128]{2,1,0:T(8,128)S(1)} %add.69), channel_id=1, source_target_pairs={{0,2},{1,3},{2,0},{3,1},{4,6},{5,7},{6,4},{7,5},{8,10},{9,11},{10,... | collective-permute-start | bytes 393224 | tf_op jit(solution)/shard_map/ppermute | solution.py:194
  51.5 1.4 %collective-permute-start.8 = (f32[4,64,128]{2,1,0:T(8,128)S(1)}, f32[4,64,128]{2,1,0:T(8,128)S(1)}, u32[]{:S(2)}, u32[]{:S(2)}) collective-permute-start(f32[4,64,128]{2,1,0:T(8,128)S(1)} %add.70), channel_id=1, source_target_pairs={{0,4},{4,0},{8,12},{12,8},{16,20},{20,16},{24,28},{28,24},{1,5},{5... | collective-permute-start | bytes 393224 | tf_op jit(solution)/shard_map/ppermute | solution.py:194
  52.9 0.8 %copy-start.1 = (f32[4,2560]{1,0:T(4,128)S(1)}, f32[4,2560]{1,0:T(4,128)}, u32[]{:S(2)}) copy-start(f32[4,2560]{1,0:T(4,128)} %ions_ref.3) | copy-start | bytes 122884

commit v4 on v0

v4 whole, which is shorter than its diff:
```python
import functools
import math

import jax
import jax.numpy as jnp
from jax import lax
from jax.experimental import pallas as pl
from jax.experimental.pallas import tpu as pltpu
from jax.sharding import PartitionSpec as P

KX = 32
SPAN = 64
HALF = SPAN // 2
LANES = 128
TILE = 256
MIB = 1 << 20
NT = ((1,), (1,))
NN = ((1,), (0,))
SIN_COEFFS = (
    3.1415926401307073,
    -5.167710083507923,
    2.5500775232148563,
    -0.5982912856211671,
    0.07765766030589402,
)
COS_COEFFS = (
    0.9999999532476085,
    -4.934792830619664,
    4.058411352862771,
    -1.3318765680813944,
    0.21968961109803095,
)


def horner(coeffs, square):
    value = jnp.float32(coeffs[-1])
    for coeff in coeffs[-2::-1]:
        value = value * square + jnp.float32(coeff)
    return value


def cos_sin_turns(turns):
    rest = turns - jnp.round(turns)
    square = rest * rest
    sin_half = rest * horner(SIN_COEFFS, square)
    cos_half = horner(COS_COEFFS, square)
    twice = sin_half + sin_half
    return 1.0 - twice * sin_half, twice * cos_half


def times(a, b):
    return a[0] * b[0] - a[1] * b[1], a[1] * b[0] + a[0] * b[1]


def split(value):
    high = value.astype(jnp.bfloat16)
    low = (value - high.astype(jnp.float32)).astype(jnp.bfloat16)
    return high, low


def dot(a, b, dims):
    return lax.dot_general(a, b, (dims, ((), ())), preferred_element_type=jnp.float32)


def row_starts(rows):
    return sorted({*range(0, rows - 7, 8), rows - 8})


def fill_yz_tables(ions_ref, coord_ref, tables):
    rows = ions_ref.shape[1] // LANES
    for s in range(rows):
        at = slice(s * LANES, (s + 1) * LANES)
        coord_ref[0, s : s + 1, :] = ions_ref[1:2, at]
        coord_ref[1, s : s + 1, :] = ions_ref[2:3, at]
    for axis in range(2):
        for start in row_starts(rows):
            base = cos_sin_turns(coord_ref[axis, start : start + 8, :])
            value = (jnp.ones_like(base[0]), jnp.zeros_like(base[0]))
            for m in range(HALF + 1):
                up = 2 * (HALF + m) * rows + start
                down = 2 * (HALF - m) * rows + start
                if m < HALF:
                    tables[axis][up : up + 8, :] = value[0]
                    tables[axis][up + rows : up + rows + 8, :] = value[1]
                if m:
                    tables[axis][down : down + 8, :] = value[0]
                    tables[axis][down + rows : down + rows + 8, :] = -value[1]
                value = base if m == 0 else times(value, base)


def fill_x_tables(ions_ref, basis_ref, left_ref):
    rows = ions_ref.shape[1] // LANES
    wave = lax.broadcasted_iota(jnp.int32, (8, LANES), 0).astype(jnp.float32)
    for s in range(rows):
        at = slice(s * LANES, (s + 1) * LANES)
        coord = ions_ref[0:1, at]
        value = cos_sin_turns(wave * coord)
        stride = cos_sin_turns(jnp.broadcast_to(8.0 * coord, (8, LANES)))
        parts = [value]
        for _ in range(KX // 8 - 1):
            parts.append(times(parts[-1], stride))
        charge = ions_ref[3:4, at]
        for half in range(2):
            whole = jnp.concatenate([part[half] for part in parts], 0)
            basis_ref[half * KX : (half + 1) * KX, at] = whole
            high, low = split(charge * whole)
            left_ref[half * KX : (half + 1) * KX, at] = high
            left_ref[(2 + half) * KX : (3 + half) * KX, at] = low


def fill_columns(ids_ref, tables, phase_ref, columns):
    y_table, z_table = tables
    rows = phase_ref.shape[1] // LANES
    for c in columns:
        col = ids_ref[c]
        y_at = (col >> 6) * (2 * rows)
        z_at = (col & (SPAN - 1)) * (2 * rows)
        for start in row_starts(rows):
            y_part = [y_table[pl.ds(y_at + half * rows + start, 8), :] for half in range(2)]
            z_part = [z_table[pl.ds(z_at + half * rows + start, 8), :] for half in range(2)]
            at = pl.ds(c * rows + start, 8)
            phase_ref[0, at, :], phase_ref[1, at, :] = times(y_part, z_part)


def add_factors(left_ref, phase_ref, high_ref, low_ref, group, before_ref, out_ref, next_columns):
    rows = phase_ref.shape[1] // LANES
    tiles = rows // 2
    share = -(-LANES // tiles)
    by_high = jnp.zeros((4 * KX, TILE), jnp.float32)
    by_low = jnp.zeros((2 * KX, TILE), jnp.float32)
    for tile in range(tiles):
        pair = (2 * tile, 2 * tile + 1)
        for s in pair:
            for half in range(2):
                to = slice(half * LANES, (half + 1) * LANES)
                high, low = split(phase_ref[half, pl.ds(s, LANES, stride=rows), :])
                high_ref[group, s, to, :] = high
                low_ref[group, s, to, :] = low
        next_columns(range(tile * share, min((tile + 1) * share, LANES)))
        high = jnp.concatenate([high_ref[group, s] for s in pair], 1)
        low = jnp.concatenate([low_ref[group, s] for s in pair], 1)
        left = left_ref[:, tile * TILE : (tile + 1) * TILE]
        by_high += dot(left, high, NT)
        by_low += dot(left[: 2 * KX], low, NT)
    product = by_high[: 2 * KX] + by_high[2 * KX :] + by_low
    out_ref[group, :KX, :] = before_ref[group, :KX, :] + (product[:KX, :LANES] - product[KX:, LANES:])
    out_ref[group, KX:, :] = before_ref[group, KX:, :] + (product[:KX, LANES:] + product[KX:, :LANES])


def factor_kernel(
    ions_ref, ids0_ref, ids1_ref, before_ref, out_ref, high_ref, low_ref, basis_ref,
    coord_ref, left_ref, y_table, z_table, phase0_ref, phase1_ref,
):
    tables = (y_table, z_table)
    fill_yz_tables(ions_ref, coord_ref, tables)
    fill_x_tables(ions_ref, basis_ref, left_ref)

    def first_columns(step, carry):
        fill_columns(ids0_ref, tables, phase0_ref, [step * 16 + i for i in range(16)])
        return carry

    lax.fori_loop(0, LANES // 16, first_columns, 0)
    add_factors(
        left_ref, phase0_ref, high_ref, low_ref, 0, before_ref, out_ref,
        lambda columns: fill_columns(ids1_ref, tables, phase1_ref, columns),
    )
    add_factors(left_ref, phase1_ref, high_ref, low_ref, 1, before_ref, out_ref, lambda columns: None)


def mix_kernel(ids0_ref, ids1_ref, own_ref, other_ref, mix_ref, energy_ref):
    wave_x = lax.broadcasted_iota(jnp.int32, (KX, LANES), 0)
    halving = jnp.where(wave_x == 0, jnp.float32(0.5), jnp.float32(1.0))
    energies = []
    for group, (ids_ref, factor_ref) in enumerate(((ids0_ref, own_ref), (ids1_ref, other_ref))):
        wave_y = (ids_ref[...] >> 6) - HALF
        wave_z = (ids_ref[...] & (SPAN - 1)) - HALF
        squared = wave_x * wave_x + jnp.broadcast_to(wave_y * wave_y + wave_z * wave_z, (KX, LANES))
        inside = (squared <= 1024) & (squared > 0)
        squared_f = squared.astype(jnp.float32)
        weight = jnp.where(
            inside,
            halving * jnp.exp(-squared_f / 1600.0) / jnp.maximum(squared_f, 1.0),
            jnp.float32(0.0),
        )
        real = factor_ref[:KX, :]
        imag = factor_ref[KX:, :]
        energy = weight * (real * real + imag * imag)
        energies.append(sum(energy[i : i + 4] for i in range(0, KX, 4)))
        g_real = weight * real
        g_imag = -weight * imag
        lanes_cos = slice(group * TILE, group * TILE + LANES)
        lanes_sin = slice(group * TILE + LANES, (group + 1) * TILE)
        for part, wave in enumerate((None, wave_y, wave_z)):
            re, im = g_real, g_imag
            if wave is not None:
                re, im = re * wave.astype(jnp.float32), im * wave.astype(jnp.float32)
            for offset, cos_value, sin_value in ((0, re, -im), (KX, im, re)):
                at = slice(part * 2 * KX + offset, part * 2 * KX + offset + KX)
                low_at = slice(6 * KX + at.start, 6 * KX + at.stop)
                mix_ref[at, lanes_cos], mix_ref[low_at, lanes_cos] = split(cos_value)
                mix_ref[at, lanes_sin], mix_ref[low_at, lanes_sin] = split(sin_value)
    energy_ref[...] = energies[0] + energies[1]


def force_kernel(mix_ref, energy_ref, *refs, force_scale, potential_scale):
    *block_refs, out_ref = refs
    wave_x = lax.broadcasted_iota(jnp.int32, (KX, TILE), 0).astype(jnp.float32)

    def reduce(value):
        return jnp.sum(value, 0, keepdims=True)

    def matrix(ref, tile):
        return jnp.concatenate([ref[:, 2 * tile + i].reshape(2 * TILE, LANES) for i in range(2)], 1)

    for block in range(len(block_refs) // 4):
        high_ref, low_ref, basis_ref, ions_ref = block_refs[4 * block : 4 * block + 4]
        count = ions_ref.shape[1]
        for tile in range(count // TILE):
            at = slice(tile * TILE, (tile + 1) * TILE)
            to = slice(block * count + at.start, block * count + at.stop)
            by_high = dot(mix_ref[...], matrix(high_ref, tile), NN)
            by_low = dot(mix_ref[: 6 * KX, :], matrix(low_ref, tile), NN)
            total = by_high[: 6 * KX] + by_high[6 * KX :] + by_low
            re0, im0, rey, imy, rez, imz = (total[i * KX : (i + 1) * KX] for i in range(6))
            cos_part = basis_ref[:KX, at]
            sin_part = basis_ref[KX:, at]
            charge = ions_ref[3:4, at] * jnp.float32(force_scale)
            out_ref[0:1, to] = charge * reduce(wave_x * (re0 * sin_part + im0 * cos_part))
            out_ref[1:2, to] = charge * reduce(rey * sin_part + imy * cos_part)
            out_ref[2:3, to] = charge * reduce(rez * sin_part + imz * cos_part)
            out_ref[3:4, to] = jnp.float32(potential_scale) * reduce(re0 * cos_part - im0 * sin_part)
    out_ref[:, out_ref.shape[1] - LANES :] = energy_ref[...]


def flip(value, axis, step):
    size = lax.axis_size(axis)
    return lax.ppermute(value, axis, [(i, i ^ step) for i in range(size)])


def per_device(ions, col_ids):
    groups = lax.axis_size("kcol")
    ranks = lax.axis_size("ion")
    blocks = groups // 2
    count = ions.shape[1]
    rows = count // LANES
    total = count * groups * ranks

    ids = (col_ids, flip(col_ids, "kcol", 1))
    ion_blocks = [ions] + [flip(ions, "kcol", 2 * i) for i in range(1, blocks)]

    smem = pl.BlockSpec(memory_space=pltpu.SMEM)
    vmem = pl.BlockSpec(memory_space=pltpu.VMEM)
    params = pltpu.CompilerParams(vmem_limit_bytes=24 * MIB)
    halves_shape = jax.ShapeDtypeStruct((2, rows, TILE, LANES), jnp.bfloat16)
    factor_call = pl.pallas_call(
        factor_kernel,
        in_specs=[vmem, smem, smem, vmem],
        out_specs=[vmem] * 4,
        out_shape=[
            jax.ShapeDtypeStruct((2, 2 * KX, LANES), jnp.float32),
            halves_shape,
            halves_shape,
            jax.ShapeDtypeStruct((2 * KX, count), jnp.float32),
        ],
        scratch_shapes=[
            pltpu.VMEM((2, rows, LANES), jnp.float32),
            pltpu.VMEM((4 * KX, count), jnp.bfloat16),
            *[pltpu.VMEM((2 * (SPAN + 1) * rows, LANES), jnp.float32)] * 2,
            *[pltpu.VMEM((2, LANES * rows, LANES), jnp.float32)] * 2,
        ],
        compiler_params=params,
        name="factor",
    )
    partial_factor = jnp.zeros((2, 2 * KX, LANES), jnp.float32)
    saved = []
    for block in ion_blocks:
        partial_factor, high, low, basis = factor_call(block, *ids, partial_factor)
        saved.append((high, low, basis, block))

    own = partial_factor[0] + flip(partial_factor[1], "kcol", 1)
    step = 1
    while step < ranks:
        own = own + flip(own, "ion", step)
        step *= 2
    mix, energy = pl.pallas_call(
        mix_kernel,
        in_specs=[vmem] * 4,
        out_specs=[vmem] * 2,
        out_shape=[
            jax.ShapeDtypeStruct((12 * KX, 2 * TILE), jnp.bfloat16),
            jax.ShapeDtypeStruct((4, LANES), jnp.float32),
        ],
        compiler_params=params,
        name="mix",
    )(*[part.reshape(1, LANES) for part in ids], own, flip(own, "kcol", 1))

    def forces_of(parts, energy):
        return pl.pallas_call(
            functools.partial(
                force_kernel,
                force_scale=0.04 * math.pi / math.sqrt(total),
                potential_scale=0.4 / math.sqrt(total),
            ),
            in_specs=[vmem] * (2 + 4 * len(parts)),
            out_specs=vmem,
            out_shape=jax.ShapeDtypeStruct((4, len(parts) * count + LANES), jnp.float32),
            compiler_params=params,
            name="force",
        )(mix, energy, *[array for part in parts for array in part])

    received = []

    def with_received(first, last):
        value = forces_of(saved[first:last], energy)
        for array in received:
            tail = array[:, array.shape[1] - LANES :]
            value = value + jnp.concatenate([array[:, first * count : last * count], tail], 1)
        return value

    size = blocks // 2
    while size:
        received.append(flip(with_received(size, 2 * size), "kcol", 2 * size))
        size //= 2
    result = with_received(0, 1)
    return result[:, :count], jnp.float32(0.01 / total) * jnp.sum(result[:, count:])


def solution(mesh):
    return jax.shard_map(
        per_device,
        mesh=mesh,
        in_specs=(P(None, ("kcol", "ion")), P("kcol")),
        out_specs=(P(None, ("kcol", "ion")), P()),
        check_vma=False,
    )
```

time: 266 us -> 53 us (0.20)
  other arithmetic: 109 us -> 0.65 us
  matrix products: 54.6 us -> 0 us
  blocking collectives: 42.8 us -> 0 us
  waiting for transfers between devices: 38.5 us -> 8.98 us
  Pallas kernels: 0 us -> 24.4 us
  starting transfers between devices: 0.04 us -> 13.5 us
  between operations: 14.8 us -> 2.54 us
    dot_general x16 -> x0, matrix products: 54.6 us -> none  [the longest x8 34.5 us: force_piece(): jnp.dot(combined, basis, precision=lax.Precision.HIGHEST, preferred_eleme...]
    cos x16 -> x0, other arithmetic: 48.3 us -> none  [the longest x8 38.6 us: phase_tables(): jnp.cos(angle_yz)]
    reduce_sum x9 -> x1, other arithmetic: 48.6 us -> 0.6 us  [per_device(): jnp.sum(result[:, count:])]
    psum x1 -> x0, waiting for transfers between devices: 38.5 us -> none  [per_device(): summed, energy = lax.psum((row_forces, energy_group), 'kcol')]
    psum x2 -> x0, blocking collectives: 31.7 us -> none  [the longest x1 19.3 us: per_device(): factor = lax.psum(partial_value, 'ion')]
    pallas_call x0 -> x8, Pallas kernels: none -> 24.4 us  [the longest x4 17.5 us: per_device(): partial_factor, high, low, basis = factor_call(block, *ids, partial_factor)]
    ppermute x0 -> x10, starting transfers between devices: none -> 13.5 us  [flip(): return lax.ppermute(value, axis, [(i, i ^ step) for i in range(size)])]
    all_gather x1 -> x0, blocking collectives: 11.2 us -> none  [per_device(): gathered = lax.all_gather(ions, 'kcol', axis=1, tiled=True)]
  transfers between devices with their start and end apart: 1 -> 10, of which waited for: 1 -> 7; matrix products, arithmetic and copies ran while one was open for 0% -> 0% of each run, Pallas kernels for 0% -> 31%
where the time goes in v4:
time: 53 us; the launch traced here: 52.8 us
  Pallas kernels  24.4 us (46%)
  starting transfers between devices  13.5 us (25%)
  waiting for transfers between devices  8.98 us (17%)
  local copies, waits for them, and re-layouts  2.72 us (5%)
  between operations  2.54 us (5%)
  other arithmetic  0.65 us (1%)
    pallas_call x4, Pallas kernels, per_device(): partial_factor, high, low, basis = factor_call(block, *ids, partial_factor)  17.5 us
    ppermute x10, starting transfers between devices, flip(): return lax.ppermute(value, axis, [(i, i ^ step) for i in range(size)])  13.5 us
    ppermute x10, waiting for transfers between devices, flip(): return lax.ppermute(value, axis, [(i, i ^ step) for i in range(size)])  8.98 us
    pallas_call x3, Pallas kernels, forces_of(): pl.pallas_call(functools.partial(force_kernel, force_scale=0.04 * math.pi...  6.75 us
    unnamed x8, local copies, waits for them, and re-layouts  2.08 us
  transfers between devices with their start and end apart: 10, of which 7 were waited for; matrix products, arithmetic and copies ran while one was open for 0% of the time, Pallas kernels for 31%

profile of v4, /device:TPU:0, one launch (start us, length us, event | category | flops | bytes accessed | tf_op | source)
XLA Modules:
  0.0 52.8 jit_solution(13737703875135913596)
XLA Ops:
  0.6 3.0 %collective-permute-start.3 = (f32[4,2560]{1,0:T(4,128)}, f32[4,2560]{1,0:T(4,128)S(1)}, u32[]{:S(2)}, u32[]{:S(2)}) collective-permute-start(f32[4,2560]{1,0:T(4,128)} %refs_3_.1), channel_id=1, source_target_pairs={{0,8},{4,12},{8,0},{12,4},{16,24},{20,28},{24,16},{28,20},{1,9},{5... | collective-permute-start | bytes 122888 | tf_op jit(solution)/shard_map/ppermute | solution.py:237
  3.7 1.5 %collective-permute-start.2 = (f32[4,2560]{1,0:T(4,128)}, f32[4,2560]{1,0:T(4,128)S(1)}, u32[]{:S(2)}, u32[]{:S(2)}) collective-permute-start(f32[4,2560]{1,0:T(4,128)} %refs_3_.1), channel_id=1, source_target_pairs={{0,16},{4,20},{8,24},{12,28},{16,0},{20,4},{24,8},{28,12},{1,17},{... | collective-permute-start | bytes 122888 | tf_op jit(solution)/shard_map/ppermute | solution.py:237
  5.2 0.0 collective-permute-start.1
  5.2 0.0 collective-permute-start
  5.2 1.3 %collective-permute-done.ids1_ref = s32[128]{0:T(128)S(1)} collective-permute-done((s32[128]{0:T(128)}, s32[128]{0:T(128)S(1)}, u32[]{:S(2)}, u32[]{:S(2)}) %collective-permute-start) | collective-permute-done | bytes 544 | tf_op jit(solution)/shard_map/ppermute | solution.py:237
  6.5 0.0 copy-start
  6.5 0.8 %copy-done = f32[4,2560]{1,0:T(4,128)S(1)} copy-done((f32[4,2560]{1,0:T(4,128)S(1)}, f32[4,2560]{1,0:T(4,128)}, u32[]{:S(2)}) %copy-start) | copy-done | bytes 40984
  7.3 0.0 copy-start.2
  7.3 0.7 %copy-done.2 = s32[128]{0:T(128)S(1)} copy-done((s32[128]{0:T(128)S(1)}, s32[128]{0:T(128)}, u32[]{:S(2)}) %copy-start.2) | copy-done | bytes 536
  7.9 4.3 %factor.4 = (f32[2,64,128]{2,1,0:T(8,128)S(1)}, bf16[2,20,256,128]{3,2,1,0:T(8,128)(2,1)S(1)}, bf16[2,20,256,128]{3,2,1,0:T(8,128)(2,1)S(1)}, f32[64,2560]{1,0:T(8,128)S(1)}) custom-call(f32[4,2560]{1,0:T(4,128)S(1)} %copy-done, s32[128]{0:T(128)S(1)} %copy-done.2, s32[128]{0:T(128)S(1)} %collective-permute-done.ids1_ref, ...), custom_call_target="tpu_custom_call" | custom-call | tf_op jit(solution)/shard_map/factor/pallas_call | solution.py:277
  12.3 0.0 collective-permute-done.3.ions_ref.refs_3_
  12.3 0.0 copy-start.3
  12.3 0.6 %copy-done.3 = s32[128]{0:T(128)S(1)} copy-done((s32[128]{0:T(128)S(1)}, s32[128]{0:T(128)}, u32[]{:S(2)}) %copy-start.3) | copy-done | bytes 536
  12.9 4.3 %factor.5 = (f32[2,64,128]{2,1,0:T(8,128)S(1)}, bf16[2,20,256,128]{3,2,1,0:T(8,128)(2,1)S(1)}, bf16[2,20,256,128]{3,2,1,0:T(8,128)(2,1)S(1)}, f32[64,2560]{1,0:T(8,128)S(1)}) custom-call(f32[4,2560]{1,0:T(4,128)S(1)} %collective-permute-done.3.ions_ref.refs_3_, s32[128]{0:T(128)S(1)} %copy-done.3, s32[128]{0:T(128)S(1)} %collective-permute-done.ids1_ref, ...), custom_call_target="tpu_custom_call" | custom-call | tf_op jit(solution)/shard_map/factor/pallas_call | solution.py:277
  17.3 0.0 collective-permute-done.2.ions_ref.refs_3_
  17.3 4.3 %factor.6 = (f32[2,64,128]{2,1,0:T(8,128)S(1)}, bf16[2,20,256,128]{3,2,1,0:T(8,128)(2,1)S(1)}, bf16[2,20,256,128]{3,2,1,0:T(8,128)(2,1)S(1)}, f32[64,2560]{1,0:T(8,128)S(1)}) custom-call(f32[4,2560]{1,0:T(4,128)S(1)} %collective-permute-done.2.ions_ref.refs_3_, s32[128]{0:T(128)S(1)} %copy-done.3, s32[128]{0:T(128)S(1)} %collective-permute-done.ids1_ref, ...), custom_call_target="tpu_custom_call" | custom-call | tf_op jit(solution)/shard_map/factor/pallas_call | solution.py:277
  21.6 0.0 collective-permute-done.1.ions_ref.refs_7_
  21.6 4.6 %factor.7 = (f32[2,64,128]{2,1,0:T(8,128)S(1)}, bf16[2,20,256,128]{3,2,1,0:T(8,128)(2,1)S(1)}, bf16[2,20,256,128]{3,2,1,0:T(8,128)(2,1)S(1)}, f32[64,2560]{1,0:T(8,128)S(1)}) custom-call(f32[4,2560]{1,0:T(4,128)S(1)} %collective-permute-done.1.ions_ref.refs_7_, s32[128]{0:T(128)S(1)} %copy-done.3, s32[128]{0:T(128)S(1)} %collective-permute-done.ids1_ref, ...), custom_call_target="tpu_custom_call" | custom-call | tf_op jit(solution)/shard_map/factor/pallas_call | solution.py:277
  26.2 0.2 collective-permute-start.4
  26.4 1.0 %collective-permute-done.4 = f32[64,128]{1,0:T(8,128)S(1)} collective-permute-done((f32[64,128]{1,0:T(8,128)S(1)}, f32[64,128]{1,0:T(8,128)S(1)}, u32[]{:S(2)}, u32[]{:S(2)}) %collective-permute-start.4) | collective-permute-done | bytes 32800 | tf_op jit(solution)/shard_map/ppermute | solution.py:237
  27.5 2.0 %collective-permute-start.5 = (f32[64,128]{1,0:T(8,128)S(1)}, f32[64,128]{1,0:T(8,128)S(1)}, u32[]{:S(2)}, u32[]{:S(2)}) collective-permute-start(f32[64,128]{1,0:T(8,128)S(1)} %bitcast_add_fusion), channel_id=1, source_target_pairs={{0,1},{1,0},{2,3},{3,2},{4,5},{5,4},{6,7},{7,6},{8,9},{9,8},{10,11... | collective-permute-start | bytes 98312 | tf_op jit(solution)/shard_map/ppermute | solution.py:237
  29.5 1.9 %collective-permute-done.5 = f32[64,128]{1,0:T(8,128)S(1)} collective-permute-done((f32[64,128]{1,0:T(8,128)S(1)}, f32[64,128]{1,0:T(8,128)S(1)}, u32[]{:S(2)}, u32[]{:S(2)}) %collective-permute-start.5) | collective-permute-done | bytes 32800 | tf_op jit(solution)/shard_map/ppermute | solution.py:237
  31.4 3.0 %collective-permute-start.6 = (f32[64,128]{1,0:T(8,128)S(1)}, f32[64,128]{1,0:T(8,128)S(1)}, u32[]{:S(2)}, u32[]{:S(2)}) collective-permute-start(f32[64,128]{1,0:T(8,128)S(1)} %add.19), channel_id=1, source_target_pairs={{0,2},{1,3},{2,0},{3,1},{4,6},{5,7},{6,4},{7,5},{8,10},{9,11},{10,... | collective-permute-start | bytes 98312 | tf_op jit(solution)/shard_map/ppermute | solution.py:237
  34.4 1.9 %collective-permute-done.6 = f32[64,128]{1,0:T(8,128)S(1)} collective-permute-done((f32[64,128]{1,0:T(8,128)S(1)}, f32[64,128]{1,0:T(8,128)S(1)}, u32[]{:S(2)}, u32[]{:S(2)}) %collective-permute-start.6) | collective-permute-done | bytes 32800 | tf_op jit(solution)/shard_map/ppermute | solution.py:237
  36.3 0.0 collective-permute-start.7
  36.3 1.2 %collective-permute-done.7.other_ref = f32[64,128]{1,0:T(8,128)S(1)} collective-permute-done((f32[64,128]{1,0:T(8,128)S(1)}, f32[64,128]{1,0:T(8,128)S(1)}, u32[]{:S(2)}, u32[]{:S(2)}) %collective-permute-start.7) | collective-permute-done | bytes 32800 | tf_op jit(solution)/shard_map/ppermute | solution.py:237
  37.5 0.1 mix.1
  37.6 3.3 %force.4 = f32[4,5248]{1,0:T(4,128)S(1)} custom-call(bf16[384,512]{1,0:T(8,128)(2,1)S(1)} %get-tuple-element.24.mix_ref, f32[4,128]{1,0:T(4,128)S(1)} %get-tuple-element.25.energy_ref, bf16[2,20,256,128]{3,2,1,0:T(8,128)(2,1)S(1)} %get-tuple-element.29.refs_0_, bf16[2,20,256,128]{3,2,1,0:T(8,128)(2,1)S(1)} %get-tuple-element.30.refs_1_, ...), custom_call_target="tpu_custom_call" | custom-call | tf_op jit(solution)/shard_map/force/pallas_call | solution.py:298
  40.9 1.9 %collective-permute-start.8 = (f32[4,5248]{1,0:T(4,128)S(1)}, f32[4,5248]{1,0:T(4,128)S(1)}, u32[]{:S(2)}, u32[]{:S(2)}) collective-permute-start(f32[4,5248]{1,0:T(4,128)S(1)} %force.4), channel_id=1, source_target_pairs={{0,16},{4,20},{8,24},{12,28},{16,0},{20,4},{24,8},{28,12},{1,17},{... | collective-permute-start | bytes 251912 | tf_op jit(solution)/shard_map/ppermute | solution.py:237
  42.8 0.0 copy-start.1
  42.8 1.7 %force.5 = f32[4,2688]{1,0:T(4,128)S(1)} custom-call(bf16[384,512]{1,0:T(8,128)(2,1)S(1)} %get-tuple-element.24.mix_ref, f32[4,128]{1,0:T(4,128)S(1)} %get-tuple-element.25.energy_ref, bf16[2,20,256,128]{3,2,1,0:T(8,128)(2,1)S(1)} %get-tuple-element.35.refs_0_, bf16[2,20,256,128]{3,2,1,0:T(8,128)(2,1)S(1)} %get-tuple-element.36.refs_1_, ...), custom_call_target="tpu_custom_call" | custom-call | tf_op jit(solution)/shard_map/force/pallas_call | solution.py:298
  44.6 1.1 %collective-permute-done.8 = f32[4,5248]{1,0:T(4,128)S(1)} collective-permute-done((f32[4,5248]{1,0:T(4,128)S(1)}, f32[4,5248]{1,0:T(4,128)S(1)}, u32[]{:S(2)}, u32[]{:S(2)}) %collective-permute-start.8) | collective-permute-done | bytes 84000 | tf_op jit(solution)/shard_map/ppermute | solution.py:237
  45.7 1.8 %collective-permute-start.9 = (f32[4,2688]{1,0:T(4,128)S(1)}, f32[4,2688]{1,0:T(4,128)S(1)}, u32[]{:S(2)}, u32[]{:S(2)}) collective-permute-start(f32[4,2688]{1,0:T(4,128)S(1)} %slice_add_fusion), channel_id=1, source_target_pairs={{0,8},{4,12},{8,0},{12,4},{16,24},{20,28},{24,16},{28,20},{1,9},{5... | collective-permute-start | bytes 129032 | tf_op jit(solution)/shard_map/ppermute | solution.py:237
  47.4 0.0 copy-done.1
  47.4 1.7 %force.3 = f32[4,2688]{1,0:T(4,128)S(1)} custom-call(bf16[384,512]{1,0:T(8,128)(2,1)S(1)} %get-tuple-element.24.mix_ref, f32[4,128]{1,0:T(4,128)S(1)} %get-tuple-element.25.energy_ref, bf16[2,20,256,128]{3,2,1,0:T(8,128)(2,1)S(1)} %get-tuple-element.26.refs_0_, bf16[2,20,256,128]{3,2,1,0:T(8,128)(2,1)S(1)} %get-tuple-element.27.refs_1_, ...), custom_call_target="tpu_custom_call" | custom-call | tf_op jit(solution)/shard_map/force/pallas_call | solution.py:298
  49.2 0.6 %collective-permute-done.9 = f32[4,2688]{1,0:T(4,128)S(1)} collective-permute-done((f32[4,2688]{1,0:T(4,128)S(1)}, f32[4,2688]{1,0:T(4,128)S(1)}, u32[]{:S(2)}, u32[]{:S(2)}) %collective-permute-start.9) | collective-permute-done | bytes 43040 | tf_op jit(solution)/shard_map/ppermute | solution.py:237
  49.8 0.6 %slice.32 = f32[4,2560]{1,0:T(4,128)} slice(f32[4,2688]{1,0:T(4,128)S(1)} %fusion), slice={[0:4], [0:2560]} | slice | bytes 81920 | tf_op jit(solution)/shard_map/slice | solution.py:325
  50.4 0.6 %slice_reduce_fusion = f32[]{:T(128)} fusion(f32[4,2688]{1,0:T(4,128)S(1)} %fusion), kind=kLoop, calls=%fused_computation.5 | loop fusion | flops 511 | bytes 2052 | tf_op jit(solution)/shard_map/reduce_sum | solution.py:325
  (9 shorter events, 0.1 us)
Async XLA Ops:
  0.6 11.6 %collective-permute-start.3 = (f32[4,2560]{1,0:T(4,128)}, f32[4,2560]{1,0:T(4,128)S(1)}, u32[]{:S(2)}, u32[]{:S(2)}) collective-permute-start(f32[4,2560]{1,0:T(4,128)} %refs_3_.1), channel_id=1, source_target_pairs={{0,8},{4,12},{8,0},{12,4},{16,24},{20,28},{24,16},{28,20},{1,9},{5... | collective-permute-start | bytes 122888 | tf_op jit(solution)/shard_map/ppermute | solution.py:237
  3.7 13.6 %collective-permute-start.2 = (f32[4,2560]{1,0:T(4,128)}, f32[4,2560]{1,0:T(4,128)S(1)}, u32[]{:S(2)}, u32[]{:S(2)}) collective-permute-start(f32[4,2560]{1,0:T(4,128)} %refs_3_.1), channel_id=1, source_target_pairs={{0,16},{4,20},{8,24},{12,28},{16,0},{20,4},{24,8},{28,12},{1,17},{... | collective-permute-start | bytes 122888 | tf_op jit(solution)/shard_map/ppermute | solution.py:237
  5.2 16.4 %collective-permute-start.1 = (f32[4,2560]{1,0:T(4,128)}, f32[4,2560]{1,0:T(4,128)S(1)}, u32[]{:S(2)}, u32[]{:S(2)}) collective-permute-start(f32[4,2560]{1,0:T(4,128)} %refs_3_.1), channel_id=1, source_target_pairs={{0,24},{4,28},{8,16},{12,20},{16,8},{20,12},{24,0},{28,4},{1,25},{... | collective-permute-start | bytes 122888 | tf_op jit(solution)/shard_map/ppermute | solution.py:237
  5.2 1.3 %collective-permute-start = (s32[128]{0:T(128)}, s32[128]{0:T(128)S(1)}, u32[]{:S(2)}, u32[]{:S(2)}) collective-permute-start(s32[128]{0:T(128)} %ids0_ref.7), channel_id=1, source_target_pairs={{0,4},{4,0},{8,12},{12,8},{16,20},{20,16},{24,28},{28,24},{1,5},{5... | collective-permute-start | bytes 1544 | tf_op jit(solution)/shard_map/ppermute | solution.py:237
  6.5 0.8 %copy-start = (f32[4,2560]{1,0:T(4,128)S(1)}, f32[4,2560]{1,0:T(4,128)}, u32[]{:S(2)}) copy-start(f32[4,2560]{1,0:T(4,128)} %refs_3_.1) | copy-start | bytes 122884
  7.3 0.7 %copy-start.2 = (s32[128]{0:T(128)S(1)}, s32[128]{0:T(128)}, u32[]{:S(2)}) copy-start(s32[128]{0:T(128)} %ids0_ref.7) | copy-start | bytes 1540
  12.3 0.7 %copy-start.3 = (s32[128]{0:T(128)S(1)}, s32[128]{0:T(128)}, u32[]{:S(2)}) copy-start(s32[128]{0:T(128)} %ids0_ref.7) | copy-start | bytes 1540
  26.2 1.3 %collective-permute-start.4 = (f32[64,128]{1,0:T(8,128)S(1)}, f32[64,128]{1,0:T(8,128)S(1)}, u32[]{:S(2)}, u32[]{:S(2)}) collective-permute-start(f32[64,128]{1,0:T(8,128)S(1)} %slice_bitcast_fusion), channel_id=1, source_target_pairs={{0,4},{4,0},{8,12},{12,8},{16,20},{20,16},{24,28},{28,24},{1,5},{5... | collective-permute-start | bytes 98312 | tf_op jit(solution)/shard_map/ppermute | solution.py:237
  27.5 3.9 %collective-permute-start.5 = (f32[64,128]{1,0:T(8,128)S(1)}, f32[64,128]{1,0:T(8,128)S(1)}, u32[]{:S(2)}, u32[]{:S(2)}) collective-permute-start(f32[64,128]{1,0:T(8,128)S(1)} %bitcast_add_fusion), channel_id=1, source_target_pairs={{0,1},{1,0},{2,3},{3,2},{4,5},{5,4},{6,7},{7,6},{8,9},{9,8},{10,11... | collective-permute-start | bytes 98312 | tf_op jit(solution)/shard_map/ppermute | solution.py:237
  31.4 4.9 %collective-permute-start.6 = (f32[64,128]{1,0:T(8,128)S(1)}, f32[64,128]{1,0:T(8,128)S(1)}, u32[]{:S(2)}, u32[]{:S(2)}) collective-permute-start(f32[64,128]{1,0:T(8,128)S(1)} %add.19), channel_id=1, source_target_pairs={{0,2},{1,3},{2,0},{3,1},{4,6},{5,7},{6,4},{7,5},{8,10},{9,11},{10,... | collective-permute-start | bytes 98312 | tf_op jit(solution)/shard_map/ppermute | solution.py:237
  36.3 1.2 %collective-permute-start.7 = (f32[64,128]{1,0:T(8,128)S(1)}, f32[64,128]{1,0:T(8,128)S(1)}, u32[]{:S(2)}, u32[]{:S(2)}) collective-permute-start(f32[64,128]{1,0:T(8,128)S(1)} %add.20.own_ref), channel_id=1, source_target_pairs={{0,4},{4,0},{8,12},{12,8},{16,20},{20,16},{24,28},{28,24},{1,5},{5... | collective-permute-start | bytes 98312 | tf_op jit(solution)/shard_map/ppermute | solution.py:237
  40.9 4.7 %collective-permute-start.8 = (f32[4,5248]{1,0:T(4,128)S(1)}, f32[4,5248]{1,0:T(4,128)S(1)}, u32[]{:S(2)}, u32[]{:S(2)}) collective-permute-start(f32[4,5248]{1,0:T(4,128)S(1)} %force.4), channel_id=1, source_target_pairs={{0,16},{4,20},{8,24},{12,28},{16,0},{20,4},{24,8},{28,12},{1,17},{... | collective-permute-start | bytes 251912 | tf_op jit(solution)/shard_map/ppermute | solution.py:237
  42.8 4.6 %copy-start.1 = (f32[4,2560]{1,0:T(4,128)S(1)}, f32[4,2560]{1,0:T(4,128)}, u32[]{:S(2)}) copy-start(f32[4,2560]{1,0:T(4,128)} %refs_3_.1) | copy-start | bytes 122884
  45.7 4.1 %collective-permute-start.9 = (f32[4,2688]{1,0:T(4,128)S(1)}, f32[4,2688]{1,0:T(4,128)S(1)}, u32[]{:S(2)}, u32[]{:S(2)}) collective-permute-start(f32[4,2688]{1,0:T(4,128)S(1)} %slice_add_fusion), channel_id=1, source_target_pairs={{0,8},{4,12},{8,0},{12,4},{16,24},{20,28},{24,16},{28,20},{1,9},{5... | collective-permute-start | bytes 129032 | tf_op jit(solution)/shard_map/ppermute | solution.py:237

commit v5 on v4

--- a/solution.py
+++ b/solution.py
@@ -66,32 +66,33 @@
     return sorted({*range(0, rows - 7, 8), rows - 8})
 
 
-def fill_yz_tables(ions_ref, coord_ref, tables):
+def yz_table_pieces(ions_ref, coord_ref, tables):
     rows = ions_ref.shape[1] // LANES
-    for s in range(rows):
-        at = slice(s * LANES, (s + 1) * LANES)
-        coord_ref[0, s : s + 1, :] = ions_ref[1:2, at]
-        coord_ref[1, s : s + 1, :] = ions_ref[2:3, at]
-    for axis in range(2):
-        for start in row_starts(rows):
-            base = cos_sin_turns(coord_ref[axis, start : start + 8, :])
-            value = (jnp.ones_like(base[0]), jnp.zeros_like(base[0]))
-            for m in range(HALF + 1):
-                up = 2 * (HALF + m) * rows + start
-                down = 2 * (HALF - m) * rows + start
-                if m < HALF:
-                    tables[axis][up : up + 8, :] = value[0]
-                    tables[axis][up + rows : up + rows + 8, :] = value[1]
-                if m:
-                    tables[axis][down : down + 8, :] = value[0]
-                    tables[axis][down + rows : down + rows + 8, :] = -value[1]
-                value = base if m == 0 else times(value, base)
-
-
-def fill_x_tables(ions_ref, basis_ref, left_ref):
+
+    def piece(axis, start):
+        for s in range(start, start + 8):
+            coord_ref[axis, s : s + 1, :] = ions_ref[1 + axis : 2 + axis, s * LANES : (s + 1) * LANES]
+        base = cos_sin_turns(coord_ref[axis, start : start + 8, :])
+        value = (jnp.ones_like(base[0]), jnp.zeros_like(base[0]))
+        for m in range(HALF + 1):
+            up = 2 * (HALF + m) * rows + start
+            down = 2 * (HALF - m) * rows + start
+            if m < HALF:
+                tables[axis][up : up + 8, :] = value[0]
+                tables[axis][up + rows : up + rows + 8, :] = value[1]
+            if m:
+                tables[axis][down : down + 8, :] = value[0]
+                tables[axis][down + rows : down + rows + 8, :] = -value[1]
+            value = base if m == 0 else times(value, base)
+
+    return [functools.partial(piece, axis, start) for start in row_starts(rows) for axis in range(2)]
+
+
+def x_table_pieces(ions_ref, basis_ref, left_ref):
     rows = ions_ref.shape[1] // LANES
     wave = lax.broadcasted_iota(jnp.int32, (8, LANES), 0).astype(jnp.float32)
-    for s in range(rows):
+
+    def piece(s):
         at = slice(s * LANES, (s + 1) * LANES)
         coord = ions_ref[0:1, at]
         value = cos_sin_turns(wave * coord)
@@ -107,14 +108,15 @@
             left_ref[half * KX : (half + 1) * KX, at] = high
             left_ref[(2 + half) * KX : (3 + half) * KX, at] = low
 
-
-def fill_columns(ids_ref, tables, phase_ref, columns):
+    return [functools.partial(piece, s) for s in range(rows)]
+
+
+def fill_columns(rows_ref, group, tables, phase_ref, columns):
     y_table, z_table = tables
     rows = phase_ref.shape[1] // LANES
     for c in columns:
-        col = ids_ref[c]
-        y_at = (col >> 6) * (2 * rows)
-        z_at = (col & (SPAN - 1)) * (2 * rows)
+        y_at = rows_ref[2 * group, c]
+        z_at = rows_ref[2 * group + 1, c]
         for start in row_starts(rows):
             y_part = [y_table[pl.ds(y_at + half * rows + start, 8), :] for half in range(2)]
             z_part = [z_table[pl.ds(z_at + half * rows + start, 8), :] for half in range(2)]
@@ -122,49 +124,89 @@
             phase_ref[0, at, :], phase_ref[1, at, :] = times(y_part, z_part)
 
 
-def add_factors(left_ref, phase_ref, high_ref, low_ref, group, before_ref, out_ref, next_columns):
+def add_factors(left_ref, phase_ref, high_ref, low_ref, group, work):
     rows = phase_ref.shape[1] // LANES
     tiles = rows // 2
-    share = -(-LANES // tiles)
     by_high = jnp.zeros((4 * KX, TILE), jnp.float32)
     by_low = jnp.zeros((2 * KX, TILE), jnp.float32)
-    for tile in range(tiles):
-        pair = (2 * tile, 2 * tile + 1)
-        for s in pair:
-            for half in range(2):
-                to = slice(half * LANES, (half + 1) * LANES)
-                high, low = split(phase_ref[half, pl.ds(s, LANES, stride=rows), :])
-                high_ref[group, s, to, :] = high
-                low_ref[group, s, to, :] = low
-        next_columns(range(tile * share, min((tile + 1) * share, LANES)))
-        high = jnp.concatenate([high_ref[group, s] for s in pair], 1)
-        low = jnp.concatenate([low_ref[group, s] for s in pair], 1)
-        left = left_ref[:, tile * TILE : (tile + 1) * TILE]
-        by_high += dot(left, high, NT)
-        by_low += dot(left[: 2 * KX], low, NT)
+    for tile in range(tiles + 1):
+        if tile:
+            pair = (2 * tile - 2, 2 * tile - 1)
+            high = jnp.concatenate([high_ref[group, s] for s in pair], 1)
+            low = jnp.concatenate([low_ref[group, s] for s in pair], 1)
+            left = left_ref[:, (tile - 1) * TILE : tile * TILE]
+            by_high += dot(left, high, NT)
+            by_low += dot(left[: 2 * KX], low, NT)
+        if tile < tiles:
+            for s in (2 * tile, 2 * tile + 1):
+                for half in range(2):
+                    to = slice(half * LANES, (half + 1) * LANES)
+                    high, low = split(phase_ref[half, pl.ds(s, LANES, stride=rows), :])
+                    high_ref[group, s, to, :] = high
+                    low_ref[group, s, to, :] = low
+            for pieces in work:
+                for piece in pieces[tile * len(pieces) // tiles : (tile + 1) * len(pieces) // tiles]:
+                    piece()
     product = by_high[: 2 * KX] + by_high[2 * KX :] + by_low
-    out_ref[group, :KX, :] = before_ref[group, :KX, :] + (product[:KX, :LANES] - product[KX:, LANES:])
-    out_ref[group, KX:, :] = before_ref[group, KX:, :] + (product[:KX, LANES:] + product[KX:, :LANES])
-
-
-def factor_kernel(
-    ions_ref, ids0_ref, ids1_ref, before_ref, out_ref, high_ref, low_ref, basis_ref,
-    coord_ref, left_ref, y_table, z_table, phase0_ref, phase1_ref,
-):
-    tables = (y_table, z_table)
-    fill_yz_tables(ions_ref, coord_ref, tables)
-    fill_x_tables(ions_ref, basis_ref, left_ref)
+    real = product[:KX, :LANES] - product[KX:, LANES:]
+    imag = product[:KX, LANES:] + product[KX:, :LANES]
+    return jnp.concatenate([real, imag], 0)
+
+
+def factor_kernel(ids0_ref, ids1_ref, *refs, blocks, has_before):
+    refs = list(refs)
+    before_ref = refs.pop(0) if has_before else None
+    ions = [refs.pop(0) for _ in range(blocks)]
+    out_ref = refs.pop(0)
+    outs = [[refs.pop(0) for _ in range(3)] for _ in range(blocks)]
+    coord_ref, found_ref, rows_ref, sem = (refs.pop(0) for _ in range(4))
+    sets = [[refs.pop(0) for _ in range(3)] for _ in range(min(blocks, 2))]
+    phases = refs
+    rows = ions[0].shape[1] // LANES
+    for group, ids_ref in enumerate((ids0_ref, ids1_ref)):
+        found_ref[2 * group : 2 * group + 1, :] = (ids_ref[...] >> 6) * (2 * rows)
+        found_ref[2 * group + 1 : 2 * group + 2, :] = (ids_ref[...] & (SPAN - 1)) * (2 * rows)
+    copy = pltpu.make_async_copy(found_ref, rows_ref, sem)
+    copy.start()
+
+    def tables_of(block):
+        left_ref, *tables = sets[block % 2]
+        return (
+            yz_table_pieces(ions[block], coord_ref, tables),
+            x_table_pieces(ions[block], outs[block][2], left_ref),
+        )
+
+    def columns_of(block, group):
+        tables = sets[block % 2][1:]
+        return [functools.partial(fill_columns, rows_ref, group, tables, phases[group], [c]) for c in range(LANES)]
+
+    for pieces in tables_of(0):
+        for piece in pieces:
+            piece()
+
+    copy.wait()
 
     def first_columns(step, carry):
-        fill_columns(ids0_ref, tables, phase0_ref, [step * 16 + i for i in range(16)])
+        fill_columns(rows_ref, 0, sets[0][1:], phases[0], [step * 16 + i for i in range(16)])
         return carry
 
     lax.fori_loop(0, LANES // 16, first_columns, 0)
-    add_factors(
-        left_ref, phase0_ref, high_ref, low_ref, 0, before_ref, out_ref,
-        lambda columns: fill_columns(ids1_ref, tables, phase1_ref, columns),
-    )
-    add_factors(left_ref, phase1_ref, high_ref, low_ref, 1, before_ref, out_ref, lambda columns: None)
+    for group in range(2):
+        out_ref[group] = before_ref[group] if has_before else jnp.zeros_like(out_ref[group])
+    for block in range(blocks):
+        high_ref, low_ref, _ = outs[block]
+        following = tables_of(block + 1) if block + 1 < blocks else ([], [])
+        for group in range(2):
+            if group == 0:
+                work = [following[0], columns_of(block, 1)]
+            elif block + 1 < blocks:
+                work = [following[1], columns_of(block + 1, 0)]
+            else:
+                work = []
+
+            @pl.when(rows_ref[0, block] >= 0)
+            def _():
+                out_ref[group] += add_factors(sets[block % 2][0], phases[group], high_ref, low_ref, group, work)
 
 
 def mix_kernel(ids0_ref, ids1_ref, own_ref, other_ref, mix_ref, energy_ref):
@@ -245,37 +287,45 @@
     rows = count // LANES
     total = count * groups * ranks
 
-    ids = (col_ids, flip(col_ids, "kcol", 1))
+    ids = [part.reshape(1, LANES) for part in (col_ids, flip(col_ids, "kcol", 1))]
     ion_blocks = [ions] + [flip(ions, "kcol", 2 * i) for i in range(1, blocks)]
 
-    smem = pl.BlockSpec(memory_space=pltpu.SMEM)
     vmem = pl.BlockSpec(memory_space=pltpu.VMEM)
     params = pltpu.CompilerParams(vmem_limit_bytes=24 * MIB)
     halves_shape = jax.ShapeDtypeStruct((2, rows, TILE, LANES), jnp.bfloat16)
-    factor_call = pl.pallas_call(
-        factor_kernel,
-        in_specs=[vmem, smem, smem, vmem],
-        out_specs=[vmem] * 4,
-        out_shape=[
-            jax.ShapeDtypeStruct((2, 2 * KX, LANES), jnp.float32),
-            halves_shape,
-            halves_shape,
-            jax.ShapeDtypeStruct((2 * KX, count), jnp.float32),
-        ],
-        scratch_shapes=[
-            pltpu.VMEM((2, rows, LANES), jnp.float32),
+
+    def factors_of(ion_blocks, before):
+        number = len(ion_blocks)
+        extra = [] if before is None else [before]
+        sets = [
             pltpu.VMEM((4 * KX, count), jnp.bfloat16),
             *[pltpu.VMEM((2 * (SPAN + 1) * rows, LANES), jnp.float32)] * 2,
-            *[pltpu.VMEM((2, LANES * rows, LANES), jnp.float32)] * 2,
-        ],
-        compiler_params=params,
-        name="factor",
-    )
-    partial_factor = jnp.zeros((2, 2 * KX, LANES), jnp.float32)
-    saved = []
-    for block in ion_blocks:
-        partial_factor, high, low, basis = factor_call(block, *ids, partial_factor)
-        saved.append((high, low, basis, block))
+        ]
+        out, *rest = pl.pallas_call(
+            functools.partial(factor_kernel, blocks=number, has_before=before is not None),
+            in_specs=[vmem] * (2 + number + len(extra)),
+            out_specs=[vmem] * (1 + 3 * number),
+            out_shape=[
+                jax.ShapeDtypeStruct((2, 2 * KX, LANES), jnp.float32),
+                *[halves_shape, halves_shape, jax.ShapeDtypeStruct((2 * KX, count), jnp.float32)] * number,
+            ],
+            scratch_shapes=[
+                pltpu.VMEM((2, rows, LANES), jnp.float32),
+                pltpu.VMEM((4, LANES), jnp.int32),
+                pltpu.SMEM((4, LANES), jnp.int32),
+                pltpu.SemaphoreType.DMA,
+                *sets * min(number, 2),
+                *[pltpu.VMEM((2, LANES * rows, LANES), jnp.float32)] * 2,
+            ],
+            compiler_params=params,
+            name="factor",
+        )(*ids, *extra, *ion_blocks)
+        return out, [(*rest[3 * i : 3 * i + 3], ion_blocks[i]) for i in range(number)]
+
+    partial_factor, saved = factors_of(ion_blocks[:1], None)
+    for first in range(1, blocks, 3):
+        partial_factor, more = factors_of(ion_blocks[first : first + 3], partial_factor)
+        saved += more
 
     own = partial_factor[0] + flip(partial_factor[1], "kcol", 1)
     step = 1
@@ -292,7 +342,7 @@
         ],
         compiler_params=params,
         name="mix",
-    )(*[part.reshape(1, LANES) for part in ids], own, flip(own, "kcol", 1))
+    )(*ids, own, flip(own, "kcol", 1))
 
     def forces_of(parts, energy):
         return pl.pallas_call(

time: 53 us -> 48.5 us (0.915)
  Pallas kernels: 24.4 us -> 20.5 us
  local copies, waits for them, and re-layouts: 2.72 us -> 2.07 us
    pallas_call x4 -> x2, Pallas kernels: 17.5 us -> 13.7 us  [factors_of(): pl.pallas_call(functools.partial(factor_kernel, blocks=number, has_before...]
    unnamed x8 -> x6, local copies, waits for them, and re-layouts: 2.08 us -> 1.44 us
  transfers between devices with their start and end apart: 10 -> 10, of which waited for: 7 -> 7; matrix products, arithmetic and copies ran while one was open for 0% -> 0% of each run, Pallas kernels for 31% -> 14%
where the time goes in v5:
time: 48.5 us; the launch traced here: 48.3 us
  Pallas kernels  20.5 us (42%)
  starting transfers between devices  13.7 us (28%)
  waiting for transfers between devices  8.88 us (18%)
  between operations  2.51 us (5%)
  local copies, waits for them, and re-layouts  2.07 us (4%)
  other arithmetic  0.65 us (1%)
    pallas_call x2, Pallas kernels, factors_of(): pl.pallas_call(functools.partial(factor_kernel, blocks=number, has_before...  13.7 us
    ppermute x10, starting transfers between devices, flip(): return lax.ppermute(value, axis, [(i, i ^ step) for i in range(size)])  13.7 us
    ppermute x10, waiting for transfers between devices, flip(): return lax.ppermute(value, axis, [(i, i ^ step) for i in range(size)])  8.88 us
    pallas_call x3, Pallas kernels, forces_of(): pl.pallas_call(functools.partial(force_kernel, force_scale=0.04 * math.pi...  6.71 us
    unnamed x6, local copies, waits for them, and re-layouts  1.44 us
  transfers between devices with their start and end apart: 10, of which 7 were waited for; matrix products, arithmetic and copies ran while one was open for 0% of the time, Pallas kernels for 14%

profile of v5, /device:TPU:0, one launch (start us, length us, event | category | flops | bytes accessed | tf_op | source)
XLA Modules:
  0.0 48.3 jit_solution(12188129091935779703)
XLA Ops:
  0.6 3.0 %collective-permute-start.1 = (f32[4,2560]{1,0:T(4,128)}, f32[4,2560]{1,0:T(4,128)S(1)}, u32[]{:S(2)}, u32[]{:S(2)}) collective-permute-start(f32[4,2560]{1,0:T(4,128)} %refs_3_.1), channel_id=1, source_target_pairs={{0,8},{4,12},{8,0},{12,4},{16,24},{20,28},{24,16},{28,20},{1,9},{5... | collective-permute-start | bytes 122888 | tf_op jit(solution)/shard_map/ppermute | solution.py:279
  3.7 1.5 %collective-permute-start.2 = (f32[4,2560]{1,0:T(4,128)}, f32[4,2560]{1,0:T(4,128)S(1)}, u32[]{:S(2)}, u32[]{:S(2)}) collective-permute-start(f32[4,2560]{1,0:T(4,128)} %refs_3_.1), channel_id=1, source_target_pairs={{0,16},{4,20},{8,24},{12,28},{16,0},{20,4},{24,8},{28,12},{1,17},{... | collective-permute-start | bytes 122888 | tf_op jit(solution)/shard_map/ppermute | solution.py:279
  5.2 0.0 collective-permute-start.3
  5.2 0.0 collective-permute-start
  5.2 1.3 %collective-permute-done = s32[128]{0:T(128)S(1)} collective-permute-done((s32[128]{0:T(128)}, s32[128]{0:T(128)S(1)}, u32[]{:S(2)}, u32[]{:S(2)}) %collective-permute-start) | collective-permute-done | bytes 544 | tf_op jit(solution)/shard_map/ppermute | solution.py:279
  6.5 0.0 copy-start
  6.5 0.8 %copy-done = f32[4,2560]{1,0:T(4,128)S(1)} copy-done((f32[4,2560]{1,0:T(4,128)S(1)}, f32[4,2560]{1,0:T(4,128)}, u32[]{:S(2)}) %copy-start) | copy-done | bytes 40984
  7.3 0.0 copy-start.2
  7.3 0.7 %copy-done.2 = s32[128]{0:T(128)S(1)} copy-done((s32[128]{0:T(128)S(1)}, s32[128]{0:T(128)}, u32[]{:S(2)}) %copy-start.2) | copy-done | bytes 536
  7.9 3.6 %factor.2 = (f32[2,64,128]{2,1,0:T(8,128)S(1)}, bf16[2,20,256,128]{3,2,1,0:T(8,128)(2,1)S(1)}, bf16[2,20,256,128]{3,2,1,0:T(8,128)(2,1)S(1)}, f32[64,2560]{1,0:T(8,128)S(1)}) custom-call(s32[1,128]{1,0:T(1,128)S(1)} %bitcast.6, s32[1,128]{1,0:T(1,128)S(1)} %bitcast.9, f32[4,2560]{1,0:T(4,128)S(1)} %copy-done), custom_call_target="tpu_custom_call" | custom-call | tf_op jit(solution)/shard_map/factor/pallas_call | solution.py:304
  11.5 0.0 collective-permute-done.1.refs_1_.refs_3_
  11.5 0.0 collective-permute-done.2.refs_2_.refs_3_
  11.5 0.0 collective-permute-done.3.refs_3_.refs_7_
  11.5 10.1 %factor.3 = (f32[2,64,128]{2,1,0:T(8,128)S(1)}, bf16[2,20,256,128]{3,2,1,0:T(8,128)(2,1)S(1)}, bf16[2,20,256,128]{3,2,1,0:T(8,128)(2,1)S(1)}, f32[64,2560]{1,0:T...) custom-call(s32[1,128]{1,0:T(1,128)S(1)} %bitcast.7, ...), custom_call_target="tpu_custom_call" | custom-call | tf_op jit(solution)/shard_map/factor/pallas_call | solution.py:304
  21.7 0.3 collective-permute-start.4
  22.0 1.0 %collective-permute-done.4 = f32[64,128]{1,0:T(8,128)S(1)} collective-permute-done((f32[64,128]{1,0:T(8,128)S(1)}, f32[64,128]{1,0:T(8,128)S(1)}, u32[]{:S(2)}, u32[]{:S(2)}) %collective-permute-start.4) | collective-permute-done | bytes 32800 | tf_op jit(solution)/shard_map/ppermute | solution.py:279
  23.0 2.0 %collective-permute-start.5 = (f32[64,128]{1,0:T(8,128)S(1)}, f32[64,128]{1,0:T(8,128)S(1)}, u32[]{:S(2)}, u32[]{:S(2)}) collective-permute-start(f32[64,128]{1,0:T(8,128)S(1)} %bitcast_add_fusion), channel_id=1, source_target_pairs={{0,1},{1,0},{2,3},{3,2},{4,5},{5,4},{6,7},{7,6},{8,9},{9,8},{10,11... | collective-permute-start | bytes 98312 | tf_op jit(solution)/shard_map/ppermute | solution.py:279
  25.0 1.9 %collective-permute-done.5 = f32[64,128]{1,0:T(8,128)S(1)} collective-permute-done((f32[64,128]{1,0:T(8,128)S(1)}, f32[64,128]{1,0:T(8,128)S(1)}, u32[]{:S(2)}, u32[]{:S(2)}) %collective-permute-start.5) | collective-permute-done | bytes 32800 | tf_op jit(solution)/shard_map/ppermute | solution.py:279
  26.9 3.0 %collective-permute-start.6 = (f32[64,128]{1,0:T(8,128)S(1)}, f32[64,128]{1,0:T(8,128)S(1)}, u32[]{:S(2)}, u32[]{:S(2)}) collective-permute-start(f32[64,128]{1,0:T(8,128)S(1)} %add.19), channel_id=1, source_target_pairs={{0,2},{1,3},{2,0},{3,1},{4,6},{5,7},{6,4},{7,5},{8,10},{9,11},{10,... | collective-permute-start | bytes 98312 | tf_op jit(solution)/shard_map/ppermute | solution.py:279
  29.9 1.9 %collective-permute-done.6 = f32[64,128]{1,0:T(8,128)S(1)} collective-permute-done((f32[64,128]{1,0:T(8,128)S(1)}, f32[64,128]{1,0:T(8,128)S(1)}, u32[]{:S(2)}, u32[]{:S(2)}) %collective-permute-start.6) | collective-permute-done | bytes 32800 | tf_op jit(solution)/shard_map/ppermute | solution.py:279
  31.8 0.0 collective-permute-start.7
  31.8 1.2 %collective-permute-done.7.other_ref = f32[64,128]{1,0:T(8,128)S(1)} collective-permute-done((f32[64,128]{1,0:T(8,128)S(1)}, f32[64,128]{1,0:T(8,128)S(1)}, u32[]{:S(2)}, u32[]{:S(2)}) %collective-permute-start.7) | collective-permute-done | bytes 32800 | tf_op jit(solution)/shard_map/ppermute | solution.py:279
  33.0 0.1 mix.1
  33.1 3.3 %force.4 = f32[4,5248]{1,0:T(4,128)S(1)} custom-call(bf16[384,512]{1,0:T(8,128)(2,1)S(1)} %get-tuple-element.20.mix_ref, f32[4,128]{1,0:T(4,128)S(1)} %get-tuple-element.21.energy_ref, bf16[2,20,256,128]{3,2,1,0:T(8,128)(2,1)S(1)} %get-tuple-element.25.refs_0_, bf16[2,20,256,128]{3,2,1,0:T(8,128)(2,1)S(1)} %get-tuple-element.26.refs_1_, ...), custom_call_target="tpu_custom_call" | custom-call | tf_op jit(solution)/shard_map/force/pallas_call | solution.py:348
  36.4 1.9 %collective-permute-start.8 = (f32[4,5248]{1,0:T(4,128)S(1)}, f32[4,5248]{1,0:T(4,128)S(1)}, u32[]{:S(2)}, u32[]{:S(2)}) collective-permute-start(f32[4,5248]{1,0:T(4,128)S(1)} %force.4), channel_id=1, source_target_pairs={{0,16},{4,20},{8,24},{12,28},{16,0},{20,4},{24,8},{28,12},{1,17},{... | collective-permute-start | bytes 251912 | tf_op jit(solution)/shard_map/ppermute | solution.py:279
  38.3 0.0 copy-start.1
  38.3 1.7 %force.5 = f32[4,2688]{1,0:T(4,128)S(1)} custom-call(bf16[384,512]{1,0:T(8,128)(2,1)S(1)} %get-tuple-element.20.mix_ref, f32[4,128]{1,0:T(4,128)S(1)} %get-tuple-element.21.energy_ref, bf16[2,20,256,128]{3,2,1,0:T(8,128)(2,1)S(1)} %get-tuple-element.31.refs_0_, bf16[2,20,256,128]{3,2,1,0:T(8,128)(2,1)S(1)} %get-tuple-element.32.refs_1_, ...), custom_call_target="tpu_custom_call" | custom-call | tf_op jit(solution)/shard_map/force/pallas_call | solution.py:348
  40.1 1.1 %collective-permute-done.8 = f32[4,5248]{1,0:T(4,128)S(1)} collective-permute-done((f32[4,5248]{1,0:T(4,128)S(1)}, f32[4,5248]{1,0:T(4,128)S(1)}, u32[]{:S(2)}, u32[]{:S(2)}) %collective-permute-start.8) | collective-permute-done | bytes 84000 | tf_op jit(solution)/shard_map/ppermute | solution.py:279
  41.2 1.8 %collective-permute-start.9 = (f32[4,2688]{1,0:T(4,128)S(1)}, f32[4,2688]{1,0:T(4,128)S(1)}, u32[]{:S(2)}, u32[]{:S(2)}) collective-permute-start(f32[4,2688]{1,0:T(4,128)S(1)} %slice_add_fusion), channel_id=1, source_target_pairs={{0,8},{4,12},{8,0},{12,4},{16,24},{20,28},{24,16},{28,20},{1,9},{5... | collective-permute-start | bytes 129032 | tf_op jit(solution)/shard_map/ppermute | solution.py:279
  43.0 0.0 copy-done.1
  43.0 1.7 %force.3 = f32[4,2688]{1,0:T(4,128)S(1)} custom-call(bf16[384,512]{1,0:T(8,128)(2,1)S(1)} %get-tuple-element.20.mix_ref, f32[4,128]{1,0:T(4,128)S(1)} %get-tuple-element.21.energy_ref, bf16[2,20,256,128]{3,2,1,0:T(8,128)(2,1)S(1)} %get-tuple-element.22.refs_0_, bf16[2,20,256,128]{3,2,1,0:T(8,128)(2,1)S(1)} %get-tuple-element.23.refs_1_, ...), custom_call_target="tpu_custom_call" | custom-call | tf_op jit(solution)/shard_map/force/pallas_call | solution.py:348
  44.8 0.5 %collective-permute-done.9 = f32[4,2688]{1,0:T(4,128)S(1)} collective-permute-done((f32[4,2688]{1,0:T(4,128)S(1)}, f32[4,2688]{1,0:T(4,128)S(1)}, u32[]{:S(2)}, u32[]{:S(2)}) %collective-permute-start.9) | collective-permute-done | bytes 43040 | tf_op jit(solution)/shard_map/ppermute | solution.py:279
  45.3 0.6 %slice.32 = f32[4,2560]{1,0:T(4,128)} slice(f32[4,2688]{1,0:T(4,128)S(1)} %fusion), slice={[0:4], [0:2560]} | slice | bytes 81920 | tf_op jit(solution)/shard_map/slice | solution.py:375
  45.9 0.6 %slice_reduce_fusion = f32[]{:T(128)} fusion(f32[4,2688]{1,0:T(4,128)S(1)} %fusion), kind=kLoop, calls=%fused_computation.5 | loop fusion | flops 511 | bytes 2052 | tf_op jit(solution)/shard_map/reduce_sum | solution.py:375
  (8 shorter events, 0.1 us)
Async XLA Ops:
  0.6 10.9 %collective-permute-start.1 = (f32[4,2560]{1,0:T(4,128)}, f32[4,2560]{1,0:T(4,128)S(1)}, u32[]{:S(2)}, u32[]{:S(2)}) collective-permute-start(f32[4,2560]{1,0:T(4,128)} %refs_3_.1), channel_id=1, source_target_pairs={{0,8},{4,12},{8,0},{12,4},{16,24},{20,28},{24,16},{28,20},{1,9},{5... | collective-permute-start | bytes 122888 | tf_op jit(solution)/shard_map/ppermute | solution.py:279
  3.7 7.9 %collective-permute-start.2 = (f32[4,2560]{1,0:T(4,128)}, f32[4,2560]{1,0:T(4,128)S(1)}, u32[]{:S(2)}, u32[]{:S(2)}) collective-permute-start(f32[4,2560]{1,0:T(4,128)} %refs_3_.1), channel_id=1, source_target_pairs={{0,16},{4,20},{8,24},{12,28},{16,0},{20,4},{24,8},{28,12},{1,17},{... | collective-permute-start | bytes 122888 | tf_op jit(solution)/shard_map/ppermute | solution.py:279
  5.2 6.3 %collective-permute-start.3 = (f32[4,2560]{1,0:T(4,128)}, f32[4,2560]{1,0:T(4,128)S(1)}, u32[]{:S(2)}, u32[]{:S(2)}) collective-permute-start(f32[4,2560]{1,0:T(4,128)} %refs_3_.1), channel_id=1, source_target_pairs={{0,24},{4,28},{8,16},{12,20},{16,8},{20,12},{24,0},{28,4},{1,25},{... | collective-permute-start | bytes 122888 | tf_op jit(solution)/shard_map/ppermute | solution.py:279
  5.2 1.3 %collective-permute-start = (s32[128]{0:T(128)}, s32[128]{0:T(128)S(1)}, u32[]{:S(2)}, u32[]{:S(2)}) collective-permute-start(s32[128]{0:T(128)} %param.3), channel_id=1, source_target_pairs={{0,4},{4,0},{8,12},{12,8},{16,20},{20,16},{24,28},{28,24},{1,5},{5... | collective-permute-start | bytes 1544 | tf_op jit(solution)/shard_map/ppermute | solution.py:279
  6.5 0.8 %copy-start = (f32[4,2560]{1,0:T(4,128)S(1)}, f32[4,2560]{1,0:T(4,128)}, u32[]{:S(2)}) copy-start(f32[4,2560]{1,0:T(4,128)} %refs_3_.1) | copy-start | bytes 122884
  7.3 0.7 %copy-start.2 = (s32[128]{0:T(128)S(1)}, s32[128]{0:T(128)}, u32[]{:S(2)}) copy-start(s32[128]{0:T(128)} %param.3) | copy-start | bytes 1540
  21.7 1.3 %collective-permute-start.4 = (f32[64,128]{1,0:T(8,128)S(1)}, f32[64,128]{1,0:T(8,128)S(1)}, u32[]{:S(2)}, u32[]{:S(2)}) collective-permute-start(f32[64,128]{1,0:T(8,128)S(1)} %slice_bitcast_fusion), channel_id=1, source_target_pairs={{0,4},{4,0},{8,12},{12,8},{16,20},{20,16},{24,28},{28,24},{1,5},{5... | collective-permute-start | bytes 98312 | tf_op jit(solution)/shard_map/ppermute | solution.py:279
  23.0 3.9 %collective-permute-start.5 = (f32[64,128]{1,0:T(8,128)S(1)}, f32[64,128]{1,0:T(8,128)S(1)}, u32[]{:S(2)}, u32[]{:S(2)}) collective-permute-start(f32[64,128]{1,0:T(8,128)S(1)} %bitcast_add_fusion), channel_id=1, source_target_pairs={{0,1},{1,0},{2,3},{3,2},{4,5},{5,4},{6,7},{7,6},{8,9},{9,8},{10,11... | collective-permute-start | bytes 98312 | tf_op jit(solution)/shard_map/ppermute | solution.py:279
  26.9 4.9 %collective-permute-start.6 = (f32[64,128]{1,0:T(8,128)S(1)}, f32[64,128]{1,0:T(8,128)S(1)}, u32[]{:S(2)}, u32[]{:S(2)}) collective-permute-start(f32[64,128]{1,0:T(8,128)S(1)} %add.19), channel_id=1, source_target_pairs={{0,2},{1,3},{2,0},{3,1},{4,6},{5,7},{6,4},{7,5},{8,10},{9,11},{10,... | collective-permute-start | bytes 98312 | tf_op jit(solution)/shard_map/ppermute | solution.py:279
  31.8 1.2 %collective-permute-start.7 = (f32[64,128]{1,0:T(8,128)S(1)}, f32[64,128]{1,0:T(8,128)S(1)}, u32[]{:S(2)}, u32[]{:S(2)}) collective-permute-start(f32[64,128]{1,0:T(8,128)S(1)} %add.20.own_ref), channel_id=1, source_target_pairs={{0,4},{4,0},{8,12},{12,8},{16,20},{20,16},{24,28},{28,24},{1,5},{5... | collective-permute-start | bytes 98312 | tf_op jit(solution)/shard_map/ppermute | solution.py:279
  36.4 4.7 %collective-permute-start.8 = (f32[4,5248]{1,0:T(4,128)S(1)}, f32[4,5248]{1,0:T(4,128)S(1)}, u32[]{:S(2)}, u32[]{:S(2)}) collective-permute-start(f32[4,5248]{1,0:T(4,128)S(1)} %force.4), channel_id=1, source_target_pairs={{0,16},{4,20},{8,24},{12,28},{16,0},{20,4},{24,8},{28,12},{1,17},{... | collective-permute-start | bytes 251912 | tf_op jit(solution)/shard_map/ppermute | solution.py:279
  38.3 4.7 %copy-start.1 = (f32[4,2560]{1,0:T(4,128)S(1)}, f32[4,2560]{1,0:T(4,128)}, u32[]{:S(2)}) copy-start(f32[4,2560]{1,0:T(4,128)} %refs_3_.1) | copy-start | bytes 122884
  41.2 4.1 %collective-permute-start.9 = (f32[4,2688]{1,0:T(4,128)S(1)}, f32[4,2688]{1,0:T(4,128)S(1)}, u32[]{:S(2)}, u32[]{:S(2)}) collective-permute-start(f32[4,2688]{1,0:T(4,128)S(1)} %slice_add_fusion), channel_id=1, source_target_pairs={{0,8},{4,12},{8,0},{12,4},{16,24},{20,28},{24,16},{28,20},{1,9},{5... | collective-permute-start | bytes 129032 | tf_op jit(solution)/shard_map/ppermute | solution.py:279

commit v6 on v5

--- a/solution.py
+++ b/solution.py
@@ -122,6 +122,19 @@
             z_part = [z_table[pl.ds(z_at + half * rows + start, 8), :] for half in range(2)]
             at = pl.ds(c * rows + start, 8)
             phase_ref[0, at, :], phase_ref[1, at, :] = times(y_part, z_part)
+
+
+def fetch_kernel(ions_hbm, ids_hbm, ions_ref, ids_ref, y_table, z_table, coord_ref, sems):
+    copies = [
+        pltpu.make_async_copy(ions_hbm, ions_ref, sems.at[0]),
+        pltpu.make_async_copy(ids_hbm, ids_ref, sems.at[1]),
+    ]
+    for copy in copies:
+        copy.start()
+    for copy in copies:
+        copy.wait()
+    for piece in yz_table_pieces(ions_ref, coord_ref, (y_table, z_table)):
+        piece()
 
 
 def add_factors(left_ref, phase_ref, high_ref, low_ref, group, work):
@@ -156,11 +169,12 @@
 def factor_kernel(ids0_ref, ids1_ref, *refs, blocks, has_before):
     refs = list(refs)
     before_ref = refs.pop(0) if has_before else None
+    given = [] if has_before else [refs.pop(0) for _ in range(2)]
     ions = [refs.pop(0) for _ in range(blocks)]
     out_ref = refs.pop(0)
     outs = [[refs.pop(0) for _ in range(3)] for _ in range(blocks)]
     coord_ref, found_ref, rows_ref, sem = (refs.pop(0) for _ in range(4))
-    sets = [[refs.pop(0) for _ in range(3)] for _ in range(min(blocks, 2))]
+    sets = [[refs.pop(0)] + given] if given else [[refs.pop(0) for _ in range(3)] for _ in range(min(blocks, 2))]
     phases = refs
     rows = ions[0].shape[1] // LANES
     for group, ids_ref in enumerate((ids0_ref, ids1_ref)):
@@ -180,7 +194,7 @@
         tables = sets[block % 2][1:]
         return [functools.partial(fill_columns, rows_ref, group, tables, phases[group], [c]) for c in range(LANES)]
 
-    for pieces in tables_of(0):
+    for pieces in tables_of(0)[len(given) // 2 :]:
         for piece in pieces:
             piece()
 
@@ -274,6 +288,18 @@
     out_ref[:, out_ref.shape[1] - LANES :] = energy_ref[...]
 
 
+def last_kernel(value_ref, *refs, energy_scale):
+    *received, out_ref, energy_ref = refs
+    count = out_ref.shape[1]
+    value = value_ref[:, :count]
+    energy = value_ref[:, count:]
+    for ref in received:
+        value = value + ref[:, :count]
+        energy = energy + ref[:, ref.shape[1] - LANES :]
+    out_ref[...] = value
+    energy_ref[0, 0] = jnp.float32(energy_scale) * jnp.sum(energy)
+
+
 def flip(value, axis, step):
     size = lax.axis_size(axis)
     return lax.ppermute(value, axis, [(i, i ^ step) for i in range(size)])
@@ -287,20 +313,42 @@
     rows = count // LANES
     total = count * groups * ranks
 
-    ids = [part.reshape(1, LANES) for part in (col_ids, flip(col_ids, "kcol", 1))]
-    ion_blocks = [ions] + [flip(ions, "kcol", 2 * i) for i in range(1, blocks)]
+    def mask(i):
+        return 2 * i | (i.bit_count() & 1)
 
     vmem = pl.BlockSpec(memory_space=pltpu.VMEM)
+    hbm = pl.BlockSpec(memory_space=pltpu.HBM)
     params = pltpu.CompilerParams(vmem_limit_bytes=24 * MIB)
+    own_ids = col_ids.reshape(1, LANES)
+    other_ids = flip(own_ids, "kcol", 1)
+    far_ions = [flip(ions, "kcol", mask(i)) for i in range(1, blocks)]
+    near_ions, near_ids, *own_tables = pl.pallas_call(
+        fetch_kernel,
+        in_specs=[hbm, hbm],
+        out_specs=[vmem] * 4,
+        out_shape=[
+            jax.ShapeDtypeStruct(ions.shape, jnp.float32),
+            jax.ShapeDtypeStruct((1, LANES), jnp.int32),
+            *[jax.ShapeDtypeStruct((2 * (SPAN + 1) * rows, LANES), jnp.float32)] * 2,
+        ],
+        scratch_shapes=[pltpu.VMEM((2, rows, LANES), jnp.float32), pltpu.SemaphoreType.DMA((2,))],
+        compiler_params=params,
+        name="fetch",
+    )(ions, own_ids)
+    ids = (near_ids, other_ids)
+    ion_blocks = [near_ions, *far_ions]
     halves_shape = jax.ShapeDtypeStruct((2, rows, TILE, LANES), jnp.bfloat16)
 
-    def factors_of(ion_blocks, before):
+    table_shape = (2 * (SPAN + 1) * rows, LANES)
+
+    def factors_of(ion_blocks, before=None, tables=()):
         number = len(ion_blocks)
-        extra = [] if before is None else [before]
-        sets = [
-            pltpu.VMEM((4 * KX, count), jnp.bfloat16),
-            *[pltpu.VMEM((2 * (SPAN + 1) * rows, LANES), jnp.float32)] * 2,
-        ]
+        extra = list(tables) if before is None else [before]
+        left_shape = pltpu.VMEM((4 * KX, count), jnp.bfloat16)
+        if tables:
+            sets = [left_shape]
+        else:
+            sets = [left_shape, *[pltpu.VMEM(table_shape, jnp.float32)] * 2] * min(number, 2)
         out, *rest = pl.pallas_call(
             functools.partial(factor_kernel, blocks=number, has_before=before is not None),
             in_specs=[vmem] * (2 + number + len(extra)),
@@ -314,7 +362,7 @@
                 pltpu.VMEM((4, LANES), jnp.int32),
                 pltpu.SMEM((4, LANES), jnp.int32),
                 pltpu.SemaphoreType.DMA,
-                *sets * min(number, 2),
+                *sets,
                 *[pltpu.VMEM((2, LANES * rows, LANES), jnp.float32)] * 2,
             ],
             compiler_params=params,
@@ -322,7 +370,7 @@
         )(*ids, *extra, *ion_blocks)
         return out, [(*rest[3 * i : 3 * i + 3], ion_blocks[i]) for i in range(number)]
 
-    partial_factor, saved = factors_of(ion_blocks[:1], None)
+    partial_factor, saved = factors_of(ion_blocks[:1], tables=own_tables)
     for first in range(1, blocks, 3):
         partial_factor, more = factors_of(ion_blocks[first : first + 3], partial_factor)
         saved += more
@@ -369,10 +417,17 @@
 
     size = blocks // 2
     while size:
-        received.append(flip(with_received(size, 2 * size), "kcol", 2 * size))
+        received.append(flip(with_received(size, 2 * size), "kcol", mask(size)))
         size //= 2
-    result = with_received(0, 1)
-    return result[:, :count], jnp.float32(0.01 / total) * jnp.sum(result[:, count:])
+    forces, energy_out = pl.pallas_call(
+        functools.partial(last_kernel, energy_scale=0.01 / total),
+        in_specs=[vmem] * (1 + len(received)),
+        out_specs=[vmem, pl.BlockSpec(memory_space=pltpu.SMEM)],
+        out_shape=[jax.ShapeDtypeStruct(ions.shape, jnp.float32), jax.ShapeDtypeStruct((1, 1), jnp.float32)],
+        compiler_params=params,
+        name="last",
+    )(forces_of(saved[:1], energy), *received)
+    return forces, energy_out.reshape(())
 
 
 def solution(mesh):

time: 48.5 us -> 44.3 us (0.913)
  waiting for transfers between devices: 8.88 us -> 6.94 us
  between operations: 2.51 us -> 0.89 us
  Pallas kernels: 20.5 us -> 21.5 us
  local copies, waits for them, and re-layouts: 2.07 us -> 1.44 us
  other arithmetic: 0.65 us -> 0.03 us
    ppermute x10, waiting for transfers between devices: 8.88 us -> 6.94 us  [flip(): return lax.ppermute(value, axis, [(i, i ^ step) for i in range(size)])]
    pallas_call x0 -> x2, Pallas kernels: none -> 0.93 us  [the longest x1 0.64 us: per_device(): pl.pallas_call(functools.partial(last_kernel, energy_scale=0.01 / total),...]
    slice x3 -> x0, local copies, waits for them, and re-layouts: 0.63 us -> none  [the longest x1 0.62 us: per_device(): result[:, :count]]
    reduce_sum x1 -> x0, other arithmetic: 0.6 us -> none  [per_device(): jnp.sum(result[:, count:])]
    unnamed x6 -> x4, local copies, waits for them, and re-layouts: 1.44 us -> 1.43 us
  transfers between devices with their start and end apart: 10 -> 10, of which waited for: 7 -> 6; matrix products, arithmetic and copies ran while one was open for 0% -> 0% of each run, Pallas kernels for 14% -> 16%
where the time goes in v6:
time: 44.3 us; the launch traced here: 44.1 us
  Pallas kernels  21.5 us (49%)
  starting transfers between devices  13.3 us (30%)
  waiting for transfers between devices  6.94 us (16%)
  local copies, waits for them, and re-layouts  1.44 us (3%)
  between operations  0.89 us (2%)
    pallas_call x2, Pallas kernels, factors_of(): pl.pallas_call(functools.partial(factor_kernel, blocks=number, has_before...  13.8 us
    ppermute x10, starting transfers between devices, flip(): return lax.ppermute(value, axis, [(i, i ^ step) for i in range(size)])  13.3 us
    ppermute x10, waiting for transfers between devices, flip(): return lax.ppermute(value, axis, [(i, i ^ step) for i in range(size)])  6.94 us
    pallas_call x3, Pallas kernels, forces_of(): pl.pallas_call(functools.partial(force_kernel, force_scale=0.04 * math.pi...  6.72 us
    unnamed x4, local copies, waits for them, and re-layouts  1.43 us
  transfers between devices with their start and end apart: 10, of which 6 were waited for; matrix products, arithmetic and copies ran while one was open for 0% of the time, Pallas kernels for 16%

profile of v6, /device:TPU:0, one launch (start us, length us, event | category | flops | bytes accessed | tf_op | source)
XLA Modules:
  0.0 44.1 jit_solution(18193248301227460225)
XLA Ops:
  0.6 2.5 %collective-permute-start.1 = (f32[4,2560]{1,0:T(4,128)}, f32[4,2560]{1,0:T(4,128)S(1)}, u32[]{:S(2)}, u32[]{:S(2)}) collective-permute-start(f32[4,2560]{1,0:T(4,128)} %ions_hbm.1), channel_id=1, source_target_pairs={{0,12},{4,8},{8,4},{12,0},{16,28},{20,24},{24,20},{28,16},{1,13},{... | collective-permute-start | bytes 122888 | tf_op jit(solution)/shard_map/ppermute | solution.py:305
  3.1 1.8 %collective-permute-start.2 = (f32[4,2560]{1,0:T(4,128)}, f32[4,2560]{1,0:T(4,128)S(1)}, u32[]{:S(2)}, u32[]{:S(2)}) collective-permute-start(f32[4,2560]{1,0:T(4,128)} %ions_hbm.1), channel_id=1, source_target_pairs={{0,20},{4,16},{8,28},{12,24},{16,4},{20,0},{24,12},{28,8},{1,21},{... | collective-permute-start | bytes 122888 | tf_op jit(solution)/shard_map/ppermute | solution.py:305
  4.9 0.0 collective-permute-start.3
  4.9 0.1 collective-permute-start
  5.0 0.0 copy-start
  5.0 0.8 %copy-done = f32[4,2560]{1,0:T(4,128)S(1)} copy-done((f32[4,2560]{1,0:T(4,128)S(1)}, f32[4,2560]{1,0:T(4,128)}, u32[]{:S(2)}) %copy-start) | copy-done | bytes 40984
  5.8 0.0 copy-start.1
  5.8 0.7 %copy-done.1 = s32[128]{0:T(128)S(1)} copy-done((s32[128]{0:T(128)S(1)}, s32[128]{0:T(128)}, u32[]{:S(2)}) %copy-start.1) | copy-done | bytes 536
  6.5 0.3 fetch.1
  6.8 0.0 collective-permute-done.ids1_ref
  6.8 3.5 %factor.2 = (f32[2,64,128]{2,1,0:T(8,128)S(1)}, bf16[2,20,256,128]{3,2,1,0:T(8,128)(2,1)S(1)}, bf16[2,20,256,128]{3,2,1,0:T(8,128)(2,1)S(1)}, f32[64,2560]{1,0:T(8,128)S(1)}) custom-call(s32[1,128]{1,0:T(1,128)S(1)} %get-tuple-element.24.ids0_ref, s32[1,128]{1,0:T(1,128)S(1)} %collective-permute-done.ids1_ref, f32[2600,128]{1,0:T(8,128)S(1)} %get-tuple-element.25.refs_0_, ...), custom_call_target="tpu_custom_call" | custom-call | tf_op jit(solution)/shard_map/factor/pallas_call | solution.py:352
  10.3 0.0 collective-permute-done.1.refs_1_.refs_3_
  10.3 0.0 collective-permute-done.2.refs_2_.refs_3_
  10.4 0.0 collective-permute-done.3.refs_3_.refs_7_
  10.4 10.2 %factor.3 = (f32[2,64,128]{2,1,0:T(8,128)S(1)}, bf16[2,20,256,128]{3,2,1,0:T(8,128)(2,1)S(1)}, bf16[2,20,256,128]{3,2,1,0:T(8,128)(2,1)S(1)}, f32[64,2560]{1,0:T...) custom-call(s32[1,128]{1,0:T(1,128)S(1)} %get-tuple-element.24.ids0_, ...), custom_call_target="tpu_custom_call" | custom-call | tf_op jit(solution)/shard_map/factor/pallas_call | solution.py:352
  20.6 0.4 collective-permute-start.4
  21.0 0.9 %collective-permute-done.4 = f32[64,128]{1,0:T(8,128)S(1)} collective-permute-done((f32[64,128]{1,0:T(8,128)S(1)}, f32[64,128]{1,0:T(8,128)S(1)}, u32[]{:S(2)}, u32[]{:S(2)}) %collective-permute-start.4) | collective-permute-done | bytes 32800 | tf_op jit(solution)/shard_map/ppermute | solution.py:305
  21.9 2.0 %collective-permute-start.5 = (f32[64,128]{1,0:T(8,128)S(1)}, f32[64,128]{1,0:T(8,128)S(1)}, u32[]{:S(2)}, u32[]{:S(2)}) collective-permute-start(f32[64,128]{1,0:T(8,128)S(1)} %bitcast_add_fusion), channel_id=1, source_target_pairs={{0,1},{1,0},{2,3},{3,2},{4,5},{5,4},{6,7},{7,6},{8,9},{9,8},{10,11... | collective-permute-start | bytes 98312 | tf_op jit(solution)/shard_map/ppermute | solution.py:305
  23.9 1.9 %collective-permute-done.5 = f32[64,128]{1,0:T(8,128)S(1)} collective-permute-done((f32[64,128]{1,0:T(8,128)S(1)}, f32[64,128]{1,0:T(8,128)S(1)}, u32[]{:S(2)}, u32[]{:S(2)}) %collective-permute-start.5) | collective-permute-done | bytes 32800 | tf_op jit(solution)/shard_map/ppermute | solution.py:305
  25.8 3.0 %collective-permute-start.6 = (f32[64,128]{1,0:T(8,128)S(1)}, f32[64,128]{1,0:T(8,128)S(1)}, u32[]{:S(2)}, u32[]{:S(2)}) collective-permute-start(f32[64,128]{1,0:T(8,128)S(1)} %add.13), channel_id=1, source_target_pairs={{0,2},{1,3},{2,0},{3,1},{4,6},{5,7},{6,4},{7,5},{8,10},{9,11},{10,... | collective-permute-start | bytes 98312 | tf_op jit(solution)/shard_map/ppermute | solution.py:305
  28.9 1.9 %collective-permute-done.6 = f32[64,128]{1,0:T(8,128)S(1)} collective-permute-done((f32[64,128]{1,0:T(8,128)S(1)}, f32[64,128]{1,0:T(8,128)S(1)}, u32[]{:S(2)}, u32[]{:S(2)}) %collective-permute-start.6) | collective-permute-done | bytes 32800 | tf_op jit(solution)/shard_map/ppermute | solution.py:305
  30.7 0.0 collective-permute-start.7
  30.8 1.2 %collective-permute-done.7.other_ref = f32[64,128]{1,0:T(8,128)S(1)} collective-permute-done((f32[64,128]{1,0:T(8,128)S(1)}, f32[64,128]{1,0:T(8,128)S(1)}, u32[]{:S(2)}, u32[]{:S(2)}) %collective-permute-start.7) | collective-permute-done | bytes 32800 | tf_op jit(solution)/shard_map/ppermute | solution.py:305
  32.0 0.1 mix.1
  32.1 3.3 %force.4 = f32[4,5248]{1,0:T(4,128)S(1)} custom-call(bf16[384,512]{1,0:T(8,128)(2,1)S(1)} %get-tuple-element.30.mix_ref, f32[4,128]{1,0:T(4,128)S(1)} %get-tuple-element.31.energy_ref, bf16[2,20,256,128]{3,2,1,0:T(8,128)(2,1)S(1)} %get-tuple-element.35.refs_0_, bf16[2,20,256,128]{3,2,1,0:T(8,128)(2,1)S(1)} %get-tuple-element.36.refs_1_, ...), custom_call_target="tpu_custom_call" | custom-call | tf_op jit(solution)/shard_map/force/pallas_call | solution.py:396
  35.3 1.7 %collective-permute-start.8 = (f32[4,5248]{1,0:T(4,128)S(1)}, f32[4,5248]{1,0:T(4,128)S(1)}, u32[]{:S(2)}, u32[]{:S(2)}) collective-permute-start(f32[4,5248]{1,0:T(4,128)S(1)} %force.4), channel_id=1, source_target_pairs={{0,20},{4,16},{8,28},{12,24},{16,4},{20,0},{24,12},{28,8},{1,21},{... | collective-permute-start | bytes 251912 | tf_op jit(solution)/shard_map/ppermute | solution.py:305
  37.1 1.7 %force.5 = f32[4,2688]{1,0:T(4,128)S(1)} custom-call(bf16[384,512]{1,0:T(8,128)(2,1)S(1)} %get-tuple-element.30.mix_ref, f32[4,128]{1,0:T(4,128)S(1)} %get-tuple-element.31.energy_ref, bf16[2,20,256,128]{3,2,1,0:T(8,128)(2,1)S(1)} %get-tuple-element.41.refs_0_, bf16[2,20,256,128]{3,2,1,0:T(8,128)(2,1)S(1)} %get-tuple-element.42.refs_1_, ...), custom_call_target="tpu_custom_call" | custom-call | tf_op jit(solution)/shard_map/force/pallas_call | solution.py:396
  38.8 1.0 %collective-permute-done.8.refs_0_ = f32[4,5248]{1,0:T(4,128)S(1)} collective-permute-done((f32[4,5248]{1,0:T(4,128)S(1)}, f32[4,5248]{1,0:T(4,128)S(1)}, u32[]{:S(2)}, u32[]{:S(2)}) %collective-permute-start.8) | collective-permute-done | bytes 84000 | tf_op jit(solution)/shard_map/ppermute | solution.py:305
  39.8 1.7 %collective-permute-start.9 = (f32[4,2688]{1,0:T(4,128)S(1)}, f32[4,2688]{1,0:T(4,128)S(1)}, u32[]{:S(2)}, u32[]{:S(2)}) collective-permute-start(f32[4,2688]{1,0:T(4,128)S(1)} %slice_add_fusion), channel_id=1, source_target_pairs={{0,12},{4,8},{8,4},{12,0},{16,28},{20,24},{24,20},{28,16},{1,13},{... | collective-permute-start | bytes 129032 | tf_op jit(solution)/shard_map/ppermute | solution.py:305
  41.5 1.7 %force.3.value_ref = f32[4,2688]{1,0:T(4,128)S(1)} custom-call(bf16[384,512]{1,0:T(8,128)(2,1)S(1)} %get-tuple-element.30.mix_ref, f32[4,128]{1,0:T(4,128)S(1)} %get-tuple-element.31.energy_ref, bf16[2,20,256,128]{3,2,1,0:T(8,128)(2,1)S(1)} %get-tuple-element.32.refs_0_, bf16[2,20,256,128]{3,2,1,0:T(8,128)(2,1)S(1)} %get-tuple-element.33.refs_1_, ...), custom_call_target="tpu_custom_call" | custom-call | tf_op jit(solution)/shard_map/force/pallas_call | solution.py:396
  43.2 0.1 collective-permute-done.9.refs_1_
  43.3 0.6 %last.1 = (f32[4,2560]{1,0:T(4,128)}, f32[1,1]{1,0:T(1,128)}) custom-call(f32[4,2688]{1,0:T(4,128)S(1)} %force.3.value_ref, f32[4,5248]{1,0:T(4,128)S(1)} %collective-permute-done.8.refs_0_, f32[4,2688]{1,0:T(4,128)S(1)} %collective-permute-done.9.refs_1_), custom_call_target="tpu_custom_call" | custom-call | tf_op jit(solution)/shard_map/last/pallas_call | solution.py:422
  (5 shorter events, 0.0 us)
Async XLA Ops:
  0.6 9.7 %collective-permute-start.1 = (f32[4,2560]{1,0:T(4,128)}, f32[4,2560]{1,0:T(4,128)S(1)}, u32[]{:S(2)}, u32[]{:S(2)}) collective-permute-start(f32[4,2560]{1,0:T(4,128)} %ions_hbm.1), channel_id=1, source_target_pairs={{0,12},{4,8},{8,4},{12,0},{16,28},{20,24},{24,20},{28,16},{1,13},{... | collective-permute-start | bytes 122888 | tf_op jit(solution)/shard_map/ppermute | solution.py:305
  3.1 7.2 %collective-permute-start.2 = (f32[4,2560]{1,0:T(4,128)}, f32[4,2560]{1,0:T(4,128)S(1)}, u32[]{:S(2)}, u32[]{:S(2)}) collective-permute-start(f32[4,2560]{1,0:T(4,128)} %ions_hbm.1), channel_id=1, source_target_pairs={{0,20},{4,16},{8,28},{12,24},{16,4},{20,0},{24,12},{28,8},{1,21},{... | collective-permute-start | bytes 122888 | tf_op jit(solution)/shard_map/ppermute | solution.py:305
  4.9 5.5 %collective-permute-start.3 = (f32[4,2560]{1,0:T(4,128)}, f32[4,2560]{1,0:T(4,128)S(1)}, u32[]{:S(2)}, u32[]{:S(2)}) collective-permute-start(f32[4,2560]{1,0:T(4,128)} %ions_hbm.1), channel_id=1, source_target_pairs={{0,24},{4,28},{8,16},{12,20},{16,8},{20,12},{24,0},{28,4},{1,25},{... | collective-permute-start | bytes 122888 | tf_op jit(solution)/shard_map/ppermute | solution.py:305
  4.9 1.9 %collective-permute-start = (s32[1,128]{1,0:T(1,128)}, s32[1,128]{1,0:T(1,128)S(1)}, u32[]{:S(2)}, u32[]{:S(2)}) collective-permute-start(s32[1,128]{1,0:T(1,128)} %bitcast.6), channel_id=1, source_target_pairs={{0,4},{4,0},{8,12},{12,8},{16,20},{20,16},{24,28},{28,24},{1,5},{5... | collective-permute-start | bytes 1544 | tf_op jit(solution)/shard_map/ppermute | solution.py:305
  5.0 0.8 %copy-start = (f32[4,2560]{1,0:T(4,128)S(1)}, f32[4,2560]{1,0:T(4,128)}, u32[]{:S(2)}) copy-start(f32[4,2560]{1,0:T(4,128)} %ions_hbm.1) | copy-start | bytes 122884
  5.8 0.7 %copy-start.1 = (s32[128]{0:T(128)S(1)}, s32[128]{0:T(128)}, u32[]{:S(2)}) copy-start(s32[128]{0:T(128)} %param.3) | copy-start | bytes 1540
  20.6 1.3 %collective-permute-start.4 = (f32[64,128]{1,0:T(8,128)S(1)}, f32[64,128]{1,0:T(8,128)S(1)}, u32[]{:S(2)}, u32[]{:S(2)}) collective-permute-start(f32[64,128]{1,0:T(8,128)S(1)} %slice_bitcast_fusion), channel_id=1, source_target_pairs={{0,4},{4,0},{8,12},{12,8},{16,20},{20,16},{24,28},{28,24},{1,5},{5... | collective-permute-start | bytes 98312 | tf_op jit(solution)/shard_map/ppermute | solution.py:305
  21.9 3.9 %collective-permute-start.5 = (f32[64,128]{1,0:T(8,128)S(1)}, f32[64,128]{1,0:T(8,128)S(1)}, u32[]{:S(2)}, u32[]{:S(2)}) collective-permute-start(f32[64,128]{1,0:T(8,128)S(1)} %bitcast_add_fusion), channel_id=1, source_target_pairs={{0,1},{1,0},{2,3},{3,2},{4,5},{5,4},{6,7},{7,6},{8,9},{9,8},{10,11... | collective-permute-start | bytes 98312 | tf_op jit(solution)/shard_map/ppermute | solution.py:305
  25.8 4.9 %collective-permute-start.6 = (f32[64,128]{1,0:T(8,128)S(1)}, f32[64,128]{1,0:T(8,128)S(1)}, u32[]{:S(2)}, u32[]{:S(2)}) collective-permute-start(f32[64,128]{1,0:T(8,128)S(1)} %add.13), channel_id=1, source_target_pairs={{0,2},{1,3},{2,0},{3,1},{4,6},{5,7},{6,4},{7,5},{8,10},{9,11},{10,... | collective-permute-start | bytes 98312 | tf_op jit(solution)/shard_map/ppermute | solution.py:305
  30.7 1.2 %collective-permute-start.7 = (f32[64,128]{1,0:T(8,128)S(1)}, f32[64,128]{1,0:T(8,128)S(1)}, u32[]{:S(2)}, u32[]{:S(2)}) collective-permute-start(f32[64,128]{1,0:T(8,128)S(1)} %add.14.own_ref), channel_id=1, source_target_pairs={{0,4},{4,0},{8,12},{12,8},{16,20},{20,16},{24,28},{28,24},{1,5},{5... | collective-permute-start | bytes 98312 | tf_op jit(solution)/shard_map/ppermute | solution.py:305
  35.3 4.4 %collective-permute-start.8 = (f32[4,5248]{1,0:T(4,128)S(1)}, f32[4,5248]{1,0:T(4,128)S(1)}, u32[]{:S(2)}, u32[]{:S(2)}) collective-permute-start(f32[4,5248]{1,0:T(4,128)S(1)} %force.4), channel_id=1, source_target_pairs={{0,20},{4,16},{8,28},{12,24},{16,4},{20,0},{24,12},{28,8},{1,21},{... | collective-permute-start | bytes 251912 | tf_op jit(solution)/shard_map/ppermute | solution.py:305
  39.8 3.5 %collective-permute-start.9 = (f32[4,2688]{1,0:T(4,128)S(1)}, f32[4,2688]{1,0:T(4,128)S(1)}, u32[]{:S(2)}, u32[]{:S(2)}) collective-permute-start(f32[4,2688]{1,0:T(4,128)S(1)} %slice_add_fusion), channel_id=1, source_target_pairs={{0,12},{4,8},{8,4},{12,0},{16,28},{20,24},{24,20},{28,16},{1,13},{... | collective-permute-start | bytes 129032 | tf_op jit(solution)/shard_map/ppermute | solution.py:305

commit v7 on v6

--- a/solution.py
+++ b/solution.py
@@ -137,29 +137,33 @@
         piece()
 
 
+def order_ids(own_ref, other_ref):
+    odd = jnp.broadcast_to(lax.axis_index("ion") & 1, own_ref.shape) == 1
+    own, other = own_ref[...], other_ref[...]
+    return jnp.where(odd, other, own), jnp.where(odd, own, other)
+
+
 def add_factors(left_ref, phase_ref, high_ref, low_ref, group, work):
     rows = phase_ref.shape[1] // LANES
     tiles = rows // 2
     by_high = jnp.zeros((4 * KX, TILE), jnp.float32)
     by_low = jnp.zeros((2 * KX, TILE), jnp.float32)
-    for tile in range(tiles + 1):
-        if tile:
-            pair = (2 * tile - 2, 2 * tile - 1)
-            high = jnp.concatenate([high_ref[group, s] for s in pair], 1)
-            low = jnp.concatenate([low_ref[group, s] for s in pair], 1)
-            left = left_ref[:, (tile - 1) * TILE : tile * TILE]
-            by_high += dot(left, high, NT)
-            by_low += dot(left[: 2 * KX], low, NT)
-        if tile < tiles:
-            for s in (2 * tile, 2 * tile + 1):
-                for half in range(2):
-                    to = slice(half * LANES, (half + 1) * LANES)
-                    high, low = split(phase_ref[half, pl.ds(s, LANES, stride=rows), :])
-                    high_ref[group, s, to, :] = high
-                    low_ref[group, s, to, :] = low
-            for pieces in work:
-                for piece in pieces[tile * len(pieces) // tiles : (tile + 1) * len(pieces) // tiles]:
-                    piece()
+    for tile in range(tiles):
+        pair = (2 * tile, 2 * tile + 1)
+        for s in pair:
+            for half in range(2):
+                to = slice(half * LANES, (half + 1) * LANES)
+                high, low = split(phase_ref[half, pl.ds(s, LANES, stride=rows), :])
+                high_ref[group, s, to, :] = high
+                low_ref[group, s, to, :] = low
+        for pieces in work:
+            for piece in pieces[tile * len(pieces) // tiles : (tile + 1) * len(pieces) // tiles]:
+                piece()
+        high = jnp.concatenate([high_ref[group, s] for s in pair], 1)
+        low = jnp.concatenate([low_ref[group, s] for s in pair], 1)
+        left = left_ref[:, tile * TILE : (tile + 1) * TILE]
+        by_high += dot(left, high, NT)
+        by_low += dot(left[: 2 * KX], low, NT)
     product = by_high[: 2 * KX] + by_high[2 * KX :] + by_low
     real = product[:KX, :LANES] - product[KX:, LANES:]
     imag = product[:KX, LANES:] + product[KX:, :LANES]
@@ -177,9 +181,9 @@
     sets = [[refs.pop(0)] + given] if given else [[refs.pop(0) for _ in range(3)] for _ in range(min(blocks, 2))]
     phases = refs
     rows = ions[0].shape[1] // LANES
-    for group, ids_ref in enumerate((ids0_ref, ids1_ref)):
-        found_ref[2 * group : 2 * group + 1, :] = (ids_ref[...] >> 6) * (2 * rows)
-        found_ref[2 * group + 1 : 2 * group + 2, :] = (ids_ref[...] & (SPAN - 1)) * (2 * rows)
+    for group, ids in enumerate(order_ids(ids0_ref, ids1_ref)):
+        found_ref[2 * group : 2 * group + 1, :] = (ids >> 6) * (2 * rows)
+        found_ref[2 * group + 1 : 2 * group + 2, :] = (ids & (SPAN - 1)) * (2 * rows)
     copy = pltpu.make_async_copy(found_ref, rows_ref, sem)
     copy.start()
 
@@ -227,9 +231,9 @@
     wave_x = lax.broadcasted_iota(jnp.int32, (KX, LANES), 0)
     halving = jnp.where(wave_x == 0, jnp.float32(0.5), jnp.float32(1.0))
     energies = []
-    for group, (ids_ref, factor_ref) in enumerate(((ids0_ref, own_ref), (ids1_ref, other_ref))):
-        wave_y = (ids_ref[...] >> 6) - HALF
-        wave_z = (ids_ref[...] & (SPAN - 1)) - HALF
+    for group, (ids, factor_ref) in enumerate(zip(order_ids(ids0_ref, ids1_ref), (own_ref, other_ref))):
+        wave_y = (ids >> 6) - HALF
+        wave_z = (ids & (SPAN - 1)) - HALF
         squared = wave_x * wave_x + jnp.broadcast_to(wave_y * wave_y + wave_z * wave_z, (KX, LANES))
         inside = (squared <= 1024) & (squared > 0)
         squared_f = squared.astype(jnp.float32)
@@ -303,6 +307,16 @@
 def flip(value, axis, step):
     size = lax.axis_size(axis)
     return lax.ppermute(value, axis, [(i, i ^ step) for i in range(size)])
+
+
+def permute(value, target):
+    groups, ranks = lax.axis_size("kcol"), lax.axis_size("ion")
+    pairs = []
+    for k in range(groups):
+        for z in range(ranks):
+            to_k, to_z = target(k, z)
+            pairs.append((k * ranks + z, to_k * ranks + to_z))
+    return lax.ppermute(value, ("kcol", "ion"), pairs)
 
 
 def per_device(ions, col_ids):
@@ -378,7 +392,7 @@
     own = partial_factor[0] + flip(partial_factor[1], "kcol", 1)
     step = 1
     while step < ranks:
-        own = own + flip(own, "ion", step)
+        own = own + permute(own, lambda k, z, step=step: (k ^ (step & 1), z ^ step))
         step *= 2
     mix, energy = pl.pallas_call(
         mix_kernel,

time: 44.3 us -> 44 us (level)
  starting transfers between devices: 13.3 us -> 12.7 us
    ppermute x10 -> x8, starting transfers between devices: 13.3 us -> 7.92 us  [flip(): return lax.ppermute(value, axis, [(i, i ^ step) for i in range(size)])]
    ppermute x0 -> x2, starting transfers between devices: none -> 4.77 us  [permute(): return lax.ppermute(value, ('kcol', 'ion'), pairs)]
    ppermute x0 -> x2, waiting for transfers between devices: none -> 3.68 us  [permute(): return lax.ppermute(value, ('kcol', 'ion'), pairs)]
    ppermute x10 -> x8, waiting for transfers between devices: 6.94 us -> 3.67 us  [flip(): return lax.ppermute(value, axis, [(i, i ^ step) for i in range(size)])]
  transfers between devices with their start and end apart: 10 -> 10, of which waited for: 6 -> 6; matrix products, arithmetic and copies ran while one was open for 0% -> 0% of each run, Pallas kernels for 16% -> 17%
where the time goes in v7:
time: 44 us; the launch traced here: 43.9 us
  Pallas kernels  21.5 us (49%)
  starting transfers between devices  12.7 us (29%)
  waiting for transfers between devices  7.34 us (17%)
  local copies, waits for them, and re-layouts  1.44 us (3%)
  between operations  0.89 us (2%)
    pallas_call x2, Pallas kernels, factors_of(): pl.pallas_call(functools.partial(factor_kernel, blocks=number, has_before...  13.7 us
    ppermute x8, starting transfers between devices, flip(): return lax.ppermute(value, axis, [(i, i ^ step) for i in range(size)])  7.92 us
    pallas_call x3, Pallas kernels, forces_of(): pl.pallas_call(functools.partial(force_kernel, force_scale=0.04 * math.pi...  6.72 us
    ppermute x2, starting transfers between devices, permute(): return lax.ppermute(value, ('kcol', 'ion'), pairs)  4.77 us
    ppermute x2, waiting for transfers between devices, permute(): return lax.ppermute(value, ('kcol', 'ion'), pairs)  3.68 us
    ppermute x8, waiting for transfers between devices, flip(): return lax.ppermute(value, axis, [(i, i ^ step) for i in range(size)])  3.67 us
    unnamed x4, local copies, waits for them, and re-layouts  1.43 us
  transfers between devices with their start and end apart: 10, of which 6 were waited for; matrix products, arithmetic and copies ran while one was open for 0% of the time, Pallas kernels for 17%

profile of v7, /device:TPU:0, one launch (start us, length us, event | category | flops | bytes accessed | tf_op | source)
XLA Modules:
  0.0 43.9 jit_solution(11765061244004406108)
XLA Ops:
  0.6 2.5 %collective-permute-start.1 = (f32[4,2560]{1,0:T(4,128)}, f32[4,2560]{1,0:T(4,128)S(1)}, u32[]{:S(2)}, u32[]{:S(2)}) collective-permute-start(f32[4,2560]{1,0:T(4,128)} %ions_hbm.1), channel_id=1, source_target_pairs={{0,12},{4,8},{8,4},{12,0},{16,28},{20,24},{24,20},{28,16},{1,13},{... | collective-permute-start | bytes 122888 | tf_op jit(solution)/shard_map/ppermute | solution.py:309
  3.1 1.8 %collective-permute-start.2 = (f32[4,2560]{1,0:T(4,128)}, f32[4,2560]{1,0:T(4,128)S(1)}, u32[]{:S(2)}, u32[]{:S(2)}) collective-permute-start(f32[4,2560]{1,0:T(4,128)} %ions_hbm.1), channel_id=1, source_target_pairs={{0,20},{4,16},{8,28},{12,24},{16,4},{20,0},{24,12},{28,8},{1,21},{... | collective-permute-start | bytes 122888 | tf_op jit(solution)/shard_map/ppermute | solution.py:309
  4.9 0.0 collective-permute-start.3
  4.9 0.1 collective-permute-start
  5.0 0.0 copy-start
  5.0 0.8 %copy-done = f32[4,2560]{1,0:T(4,128)S(1)} copy-done((f32[4,2560]{1,0:T(4,128)S(1)}, f32[4,2560]{1,0:T(4,128)}, u32[]{:S(2)}) %copy-start) | copy-done | bytes 40984
  5.8 0.0 copy-start.1
  5.8 0.7 %copy-done.1 = s32[128]{0:T(128)S(1)} copy-done((s32[128]{0:T(128)S(1)}, s32[128]{0:T(128)}, u32[]{:S(2)}) %copy-start.1) | copy-done | bytes 536
  6.5 0.3 fetch.1
  6.8 0.0 collective-permute-done.ids1_ref
  6.8 3.6 %factor.2 = (f32[2,64,128]{2,1,0:T(8,128)S(1)}, bf16[2,20,256,128]{3,2,1,0:T(8,128)(2,1)S(1)}, bf16[2,20,256,128]{3,2,1,0:T(8,128)(2,1)S(1)}, f32[64,2560]{1,0:T(8,128)S(1)}) custom-call(s32[1,128]{1,0:T(1,128)S(1)} %get-tuple-element.24.ids0_ref, s32[1,128]{1,0:T(1,128)S(1)} %collective-permute-done.ids1_ref, f32[2600,128]{1,0:T(8,128)S(1)} %get-tuple-element.25.refs_0_, ...), custom_call_target="tpu_custom_call" | custom-call | tf_op jit(solution)/shard_map/factor/pallas_call | solution.py:366
  10.3 0.0 collective-permute-done.1.refs_1_.refs_3_
  10.4 0.0 collective-permute-done.2.refs_2_.refs_3_
  10.4 0.0 collective-permute-done.3.refs_3_.refs_7_
  10.4 10.2 %factor.3 = (f32[2,64,128]{2,1,0:T(8,128)S(1)}, bf16[2,20,256,128]{3,2,1,0:T(8,128)(2,1)S(1)}, bf16[2,20,256,128]{3,2,1,0:T(8,128)(2,1)S(1)}, f32[64,2560]{1,0:T...) custom-call(s32[1,128]{1,0:T(1,128)S(1)} %get-tuple-element.24.ids0_, ...), custom_call_target="tpu_custom_call" | custom-call | tf_op jit(solution)/shard_map/factor/pallas_call | solution.py:366
  20.6 0.4 collective-permute-start.4
  21.0 0.9 %collective-permute-done.4 = f32[64,128]{1,0:T(8,128)S(1)} collective-permute-done((f32[64,128]{1,0:T(8,128)S(1)}, f32[64,128]{1,0:T(8,128)S(1)}, u32[]{:S(2)}, u32[]{:S(2)}) %collective-permute-start.4) | collective-permute-done | bytes 32800 | tf_op jit(solution)/shard_map/ppermute | solution.py:309
  21.8 2.0 %collective-permute-start.5 = (f32[64,128]{1,0:T(8,128)S(1)}, f32[64,128]{1,0:T(8,128)S(1)}, u32[]{:S(2)}, u32[]{:S(2)}) collective-permute-start(f32[64,128]{1,0:T(8,128)S(1)} %bitcast_add_fusion), channel_id=1, source_target_pairs={{0,5},{1,4},{2,7},{3,6},{4,1},{5,0},{6,3},{7,2},{8,13},{9,12},{10,... | collective-permute-start | bytes 98312 | tf_op jit(solution)/shard_map/ppermute | solution.py:319
  23.9 1.6 %collective-permute-done.5 = f32[64,128]{1,0:T(8,128)S(1)} collective-permute-done((f32[64,128]{1,0:T(8,128)S(1)}, f32[64,128]{1,0:T(8,128)S(1)}, u32[]{:S(2)}, u32[]{:S(2)}) %collective-permute-start.5) | collective-permute-done | bytes 32800 | tf_op jit(solution)/shard_map/ppermute | solution.py:319
  25.5 2.7 %collective-permute-start.6 = (f32[64,128]{1,0:T(8,128)S(1)}, f32[64,128]{1,0:T(8,128)S(1)}, u32[]{:S(2)}, u32[]{:S(2)}) collective-permute-start(f32[64,128]{1,0:T(8,128)S(1)} %add.13), channel_id=1, source_target_pairs={{0,2},{1,3},{2,0},{3,1},{4,6},{5,7},{6,4},{7,5},{8,10},{9,11},{10,... | collective-permute-start | bytes 98312 | tf_op jit(solution)/shard_map/ppermute | solution.py:319
  28.2 2.1 %collective-permute-done.6 = f32[64,128]{1,0:T(8,128)S(1)} collective-permute-done((f32[64,128]{1,0:T(8,128)S(1)}, f32[64,128]{1,0:T(8,128)S(1)}, u32[]{:S(2)}, u32[]{:S(2)}) %collective-permute-start.6) | collective-permute-done | bytes 32800 | tf_op jit(solution)/shard_map/ppermute | solution.py:319
  30.3 0.0 collective-permute-start.7
  30.3 1.2 %collective-permute-done.7.other_ref = f32[64,128]{1,0:T(8,128)S(1)} collective-permute-done((f32[64,128]{1,0:T(8,128)S(1)}, f32[64,128]{1,0:T(8,128)S(1)}, u32[]{:S(2)}, u32[]{:S(2)}) %collective-permute-start.7) | collective-permute-done | bytes 32800 | tf_op jit(solution)/shard_map/ppermute | solution.py:309
  31.5 0.1 mix.1
  31.6 3.3 %force.4 = f32[4,5248]{1,0:T(4,128)S(1)} custom-call(bf16[384,512]{1,0:T(8,128)(2,1)S(1)} %get-tuple-element.30.mix_ref, f32[4,128]{1,0:T(4,128)S(1)} %get-tuple-element.31.energy_ref, bf16[2,20,256,128]{3,2,1,0:T(8,128)(2,1)S(1)} %get-tuple-element.35.refs_0_, bf16[2,20,256,128]{3,2,1,0:T(8,128)(2,1)S(1)} %get-tuple-element.36.refs_1_, ...), custom_call_target="tpu_custom_call" | custom-call | tf_op jit(solution)/shard_map/force/pallas_call | solution.py:410
  34.9 1.6 %collective-permute-start.8 = (f32[4,5248]{1,0:T(4,128)S(1)}, f32[4,5248]{1,0:T(4,128)S(1)}, u32[]{:S(2)}, u32[]{:S(2)}) collective-permute-start(f32[4,5248]{1,0:T(4,128)S(1)} %force.4), channel_id=1, source_target_pairs={{0,20},{4,16},{8,28},{12,24},{16,4},{20,0},{24,12},{28,8},{1,21},{... | collective-permute-start | bytes 251912 | tf_op jit(solution)/shard_map/ppermute | solution.py:309
  36.5 1.7 %force.5 = f32[4,2688]{1,0:T(4,128)S(1)} custom-call(bf16[384,512]{1,0:T(8,128)(2,1)S(1)} %get-tuple-element.30.mix_ref, f32[4,128]{1,0:T(4,128)S(1)} %get-tuple-element.31.energy_ref, bf16[2,20,256,128]{3,2,1,0:T(8,128)(2,1)S(1)} %get-tuple-element.41.refs_0_, bf16[2,20,256,128]{3,2,1,0:T(8,128)(2,1)S(1)} %get-tuple-element.42.refs_1_, ...), custom_call_target="tpu_custom_call" | custom-call | tf_op jit(solution)/shard_map/force/pallas_call | solution.py:410
  38.2 1.2 %collective-permute-done.8.refs_0_ = f32[4,5248]{1,0:T(4,128)S(1)} collective-permute-done((f32[4,5248]{1,0:T(4,128)S(1)}, f32[4,5248]{1,0:T(4,128)S(1)}, u32[]{:S(2)}, u32[]{:S(2)}) %collective-permute-start.8) | collective-permute-done | bytes 84000 | tf_op jit(solution)/shard_map/ppermute | solution.py:309
  39.4 1.5 %collective-permute-start.9 = (f32[4,2688]{1,0:T(4,128)S(1)}, f32[4,2688]{1,0:T(4,128)S(1)}, u32[]{:S(2)}, u32[]{:S(2)}) collective-permute-start(f32[4,2688]{1,0:T(4,128)S(1)} %slice_add_fusion), channel_id=1, source_target_pairs={{0,12},{4,8},{8,4},{12,0},{16,28},{20,24},{24,20},{28,16},{1,13},{... | collective-permute-start | bytes 129032 | tf_op jit(solution)/shard_map/ppermute | solution.py:309
  41.0 1.7 %force.3.value_ref = f32[4,2688]{1,0:T(4,128)S(1)} custom-call(bf16[384,512]{1,0:T(8,128)(2,1)S(1)} %get-tuple-element.30.mix_ref, f32[4,128]{1,0:T(4,128)S(1)} %get-tuple-element.31.energy_ref, bf16[2,20,256,128]{3,2,1,0:T(8,128)(2,1)S(1)} %get-tuple-element.32.refs_0_, bf16[2,20,256,128]{3,2,1,0:T(8,128)(2,1)S(1)} %get-tuple-element.33.refs_1_, ...), custom_call_target="tpu_custom_call" | custom-call | tf_op jit(solution)/shard_map/force/pallas_call | solution.py:410
  42.7 0.4 collective-permute-done.9.refs_1_
  43.1 0.6 %last.1 = (f32[4,2560]{1,0:T(4,128)}, f32[1,1]{1,0:T(1,128)}) custom-call(f32[4,2688]{1,0:T(4,128)S(1)} %force.3.value_ref, f32[4,5248]{1,0:T(4,128)S(1)} %collective-permute-done.8.refs_0_, f32[4,2688]{1,0:T(4,128)S(1)} %collective-permute-done.9.refs_1_), custom_call_target="tpu_custom_call" | custom-call | tf_op jit(solution)/shard_map/last/pallas_call | solution.py:436
  (5 shorter events, 0.0 us)
Async XLA Ops:
  0.6 9.7 %collective-permute-start.1 = (f32[4,2560]{1,0:T(4,128)}, f32[4,2560]{1,0:T(4,128)S(1)}, u32[]{:S(2)}, u32[]{:S(2)}) collective-permute-start(f32[4,2560]{1,0:T(4,128)} %ions_hbm.1), channel_id=1, source_target_pairs={{0,12},{4,8},{8,4},{12,0},{16,28},{20,24},{24,20},{28,16},{1,13},{... | collective-permute-start | bytes 122888 | tf_op jit(solution)/shard_map/ppermute | solution.py:309
  3.1 7.3 %collective-permute-start.2 = (f32[4,2560]{1,0:T(4,128)}, f32[4,2560]{1,0:T(4,128)S(1)}, u32[]{:S(2)}, u32[]{:S(2)}) collective-permute-start(f32[4,2560]{1,0:T(4,128)} %ions_hbm.1), channel_id=1, source_target_pairs={{0,20},{4,16},{8,28},{12,24},{16,4},{20,0},{24,12},{28,8},{1,21},{... | collective-permute-start | bytes 122888 | tf_op jit(solution)/shard_map/ppermute | solution.py:309
  4.9 5.5 %collective-permute-start.3 = (f32[4,2560]{1,0:T(4,128)}, f32[4,2560]{1,0:T(4,128)S(1)}, u32[]{:S(2)}, u32[]{:S(2)}) collective-permute-start(f32[4,2560]{1,0:T(4,128)} %ions_hbm.1), channel_id=1, source_target_pairs={{0,24},{4,28},{8,16},{12,20},{16,8},{20,12},{24,0},{28,4},{1,25},{... | collective-permute-start | bytes 122888 | tf_op jit(solution)/shard_map/ppermute | solution.py:309
  4.9 1.9 %collective-permute-start = (s32[1,128]{1,0:T(1,128)}, s32[1,128]{1,0:T(1,128)S(1)}, u32[]{:S(2)}, u32[]{:S(2)}) collective-permute-start(s32[1,128]{1,0:T(1,128)} %bitcast.6), channel_id=1, source_target_pairs={{0,4},{4,0},{8,12},{12,8},{16,20},{20,16},{24,28},{28,24},{1,5},{5... | collective-permute-start | bytes 1544 | tf_op jit(solution)/shard_map/ppermute | solution.py:309
  5.0 0.8 %copy-start = (f32[4,2560]{1,0:T(4,128)S(1)}, f32[4,2560]{1,0:T(4,128)}, u32[]{:S(2)}) copy-start(f32[4,2560]{1,0:T(4,128)} %ions_hbm.1) | copy-start | bytes 122884
  5.8 0.7 %copy-start.1 = (s32[128]{0:T(128)S(1)}, s32[128]{0:T(128)}, u32[]{:S(2)}) copy-start(s32[128]{0:T(128)} %param.3) | copy-start | bytes 1540
  20.6 1.3 %collective-permute-start.4 = (f32[64,128]{1,0:T(8,128)S(1)}, f32[64,128]{1,0:T(8,128)S(1)}, u32[]{:S(2)}, u32[]{:S(2)}) collective-permute-start(f32[64,128]{1,0:T(8,128)S(1)} %slice_bitcast_fusion), channel_id=1, source_target_pairs={{0,4},{4,0},{8,12},{12,8},{16,20},{20,16},{24,28},{28,24},{1,5},{5... | collective-permute-start | bytes 98312 | tf_op jit(solution)/shard_map/ppermute | solution.py:309
  21.8 3.6 %collective-permute-start.5 = (f32[64,128]{1,0:T(8,128)S(1)}, f32[64,128]{1,0:T(8,128)S(1)}, u32[]{:S(2)}, u32[]{:S(2)}) collective-permute-start(f32[64,128]{1,0:T(8,128)S(1)} %bitcast_add_fusion), channel_id=1, source_target_pairs={{0,5},{1,4},{2,7},{3,6},{4,1},{5,0},{6,3},{7,2},{8,13},{9,12},{10,... | collective-permute-start | bytes 98312 | tf_op jit(solution)/shard_map/ppermute | solution.py:319
  25.5 4.8 %collective-permute-start.6 = (f32[64,128]{1,0:T(8,128)S(1)}, f32[64,128]{1,0:T(8,128)S(1)}, u32[]{:S(2)}, u32[]{:S(2)}) collective-permute-start(f32[64,128]{1,0:T(8,128)S(1)} %add.13), channel_id=1, source_target_pairs={{0,2},{1,3},{2,0},{3,1},{4,6},{5,7},{6,4},{7,5},{8,10},{9,11},{10,... | collective-permute-start | bytes 98312 | tf_op jit(solution)/shard_map/ppermute | solution.py:319
  30.3 1.2 %collective-permute-start.7 = (f32[64,128]{1,0:T(8,128)S(1)}, f32[64,128]{1,0:T(8,128)S(1)}, u32[]{:S(2)}, u32[]{:S(2)}) collective-permute-start(f32[64,128]{1,0:T(8,128)S(1)} %add.14.own_ref), channel_id=1, source_target_pairs={{0,4},{4,0},{8,12},{12,8},{16,20},{20,16},{24,28},{28,24},{1,5},{5... | collective-permute-start | bytes 98312 | tf_op jit(solution)/shard_map/ppermute | solution.py:309
  34.9 4.5 %collective-permute-start.8 = (f32[4,5248]{1,0:T(4,128)S(1)}, f32[4,5248]{1,0:T(4,128)S(1)}, u32[]{:S(2)}, u32[]{:S(2)}) collective-permute-start(f32[4,5248]{1,0:T(4,128)S(1)} %force.4), channel_id=1, source_target_pairs={{0,20},{4,16},{8,28},{12,24},{16,4},{20,0},{24,12},{28,8},{1,21},{... | collective-permute-start | bytes 251912 | tf_op jit(solution)/shard_map/ppermute | solution.py:309
  39.4 3.6 %collective-permute-start.9 = (f32[4,2688]{1,0:T(4,128)S(1)}, f32[4,2688]{1,0:T(4,128)S(1)}, u32[]{:S(2)}, u32[]{:S(2)}) collective-permute-start(f32[4,2688]{1,0:T(4,128)S(1)} %slice_add_fusion), channel_id=1, source_target_pairs={{0,12},{4,8},{8,4},{12,0},{16,28},{20,24},{24,20},{28,16},{1,13},{... | collective-permute-start | bytes 129032 | tf_op jit(solution)/shard_map/ppermute | solution.py:309
